TPU v7x, 32 devices: a whole 2x2x4 slice. The times are simulated.
32 devices in a mesh: context: 8 (over z, core), expert: 4 (over y, x).
Axes of the slice: x: 2, y: 2, z: 4, core: 2. Of those that a mesh axis runs over, the one named last changes fastest.
Arguments:
- residual: bfloat16 [2048, 6144], P(('context', 'expert')), may hold values from -6 to 6
- attn_queries: bfloat16 [2048, 8192], P('context', 'expert'), may hold values from -6 to 6
- attn_keys: bfloat16 [2048, 8192], P('context', 'expert'), may hold values from -0.5 to 0.5
- attn_values: bfloat16 [2048, 8192], P('context', 'expert'), may hold values from -6 to 6
- decay_rate: float32 [64, 2048], P('expert', 'context'), may hold values from 0 to 1, as said below
- start_state: float32 [64, 128, 128], P('expert'), may hold values from -12 to 12
- out_proj: bfloat16 [8192, 6144], P('expert', 'context'), may hold values from -0.0625 to 0.0625
- moe_gain: float32 [6144], replicated, may hold values from 0.5 to 1.5
- gate_proj: bfloat16 [4, 6144, 4608], P('expert', None, 'context'), may hold values from -0.078125 to 0.078125
- up_proj: bfloat16 [4, 6144, 4608], P('expert', None, 'context'), may hold values from -0.078125 to 0.078125
- down_proj: bfloat16 [4, 4608, 6144], P('expert', None, 'context'), may hold values from -0.09375 to 0.09375
- expert_ids: int32 [2048, 2], P(('context', 'expert')), may hold values from 0 to 3, all different within a row; in each aligned block of 64 rows (0 to 63, 64 to 127, ...) at most 48 rows name the same one
- expert_gates: float32 [2048, 2], P(('context', 'expert')), may hold values from 0.25 to 1
Outputs:
- layer_out: bfloat16 [2048, 6144], P(('context', 'expert'))
Inputs may be any that keep to these rules, and one draw needn't show every extreme that they name: `decay_rate`: non-negative rates. `expert_ids`: each row names two different experts; among the 64 rows of one aligned block no expert is named by more than 48 rows.
All inputs are finite; a program needn't handle non-finite values.
Results may differ from a plain program's by a relative error of at most 0.015.
Values may be sent and summed in bfloat16 or wider, within the bound.
No kernel may reach another device: no remote copies, remote signals or barrier semaphores. Data moves between devices by JAX's collectives and lax.ppermute only.
A program may use at most 192 MiB of HBM per device.

v0:
```python
import jax
import jax.numpy as jnp
from jax import lax
from jax.experimental import pallas as pl
from jax.experimental.pallas import tpu as pltpu
from jax.sharding import Mesh
from jax.sharding import PartitionSpec as P

BF = jnp.bfloat16
F32 = jnp.float32
GROUPS = (2, 1)


def after(x, *first):
    return lax.optimization_barrier((x, first))[0]


def swap_core(x):
    return lax.ppermute(x, "core", [(0, 1), (1, 0)])


def shift_z(x, by, wrap=False):
    n = lax.axis_size("z")
    if wrap:
        perm = [(i, (i + by) % n) for i in range(n)]
    else:
        perm = [(i, i + by) for i in range(n) if 0 <= i + by < n]
    return lax.ppermute(x, "z", perm)


def to_expert(x, k):
    n = lax.axis_size("expert")
    return lax.ppermute(x, "expert", [(i, i ^ k) for i in range(n)])


def by_core(core, own, other):
    first = core == 0
    return jnp.where(first, own, other), jnp.where(first, other, own)


def line_gather(x):
    n = lax.axis_size("z")
    right, left = [x], [x]
    for step in range(n - 1):
        onward = [(i, i + 1) for i in range(step, n - 1)]
        rightward, leftward = lax.optimization_barrier((right[-1], left[-1]))
        right.append(lax.ppermute(rightward, "z", onward))
        left.append(lax.ppermute(leftward, "z", [(n - 1 - i, n - 1 - j) for i, j in onward]))
    return right[:0:-1] + left


def copy_shard(z, n, s, pieces, rows, target, sem, skipped=0):
    for i in range(s, s + n):

        @pl.when(n - 1 + s - z == i)
        def _(piece=pieces[i - skipped]):
            source = piece if rows is None else piece.at[rows]
            pltpu.make_async_copy(source, target, sem).start()


ANY = pl.BlockSpec(memory_space=pltpu.HBM)
VMEM = pl.BlockSpec(memory_space=pltpu.VMEM)
SMEM = pl.BlockSpec(memory_space=pltpu.SMEM)


def params(megabytes):
    return pltpu.CompilerParams(vmem_limit_bytes=megabytes << 20)


def where_am_i():
    return jnp.stack([lax.axis_index(a) for a in ("z", "core", "expert")]).astype(jnp.int32)


def project_kernel(block, n, n_exp, rows, me, *refs):
    count = max(block) + n - min(block)
    pieces, (weights, *outs) = refs[:count], refs[count:]
    outs, (x, w, x_sem, w_sem) = outs[:n_exp], outs[n_exp:]
    z, expert = me[0], me[2]
    cols = weights.shape[2]
    copies = []
    for i in range(2):
        to = w.at[:, pl.ds(i * cols, cols)]
        copies.append(pltpu.make_async_copy(weights.at[i], to, w_sem.at[i]))
        copies[-1].start()
    for k in range(n_exp):
        taken = pl.ds(pl.multiple_of((expert ^ k) * rows, 16), rows)
        for i, s in enumerate(block):
            to = x.at[pl.ds((k * len(block) + i) * rows, rows)]
            copy_shard(z, n, s, pieces, taken, to, x_sem.at[k * len(block) + i], min(block))
    for c in copies:
        c.wait()
    for i in range(n_exp * len(block)):
        to = x.at[pl.ds(i * rows, rows)]
        pltpu.make_async_copy(pieces[0].at[pl.ds(0, rows)], to, x_sem.at[i]).wait()
    size = rows * len(block)
    for k in range(n_exp):
        outs[k][...] = jnp.dot(
            x[pl.ds(k * size, size), :], w[...], preferred_element_type=F32
        ).astype(BF)


def project_call(block, n, n_exp, rows, pieces, weights):
    size = rows * len(block)
    depth, cols = weights.shape[1:]
    pieces = pieces[min(block) : max(block) + n]
    flops = 4 * n_exp * size * depth * cols
    return pl.pallas_call(
        lambda *refs: project_kernel(block, n, n_exp, rows, *refs),
        name="project",
        out_shape=[jax.ShapeDtypeStruct((size, 2 * cols), BF)] * n_exp,
        in_specs=[SMEM] + [ANY] * (len(pieces) + 1),
        out_specs=[VMEM] * n_exp,
        scratch_shapes=[
            pltpu.VMEM((n_exp * size, depth), BF),
            pltpu.VMEM((depth, 2 * cols), BF),
            pltpu.SemaphoreType.DMA((n_exp * len(block),)),
            pltpu.SemaphoreType.DMA((2,)),
        ],
        compiler_params=params(32),
        cost_estimate=pl.CostEstimate(flops=flops, transcendentals=0, bytes_accessed=12 << 20),
    )(where_am_i(), *pieces, weights)


def route_kernel(n, groups, me, *refs):
    pieces, (gain, *refs) = refs[: 2 * n - 1], refs[2 * n - 1 :]
    picks, outs, (x, sem) = refs[:groups], refs[groups:-2], refs[-2:]
    part = pieces[0].shape[1]
    for s in range(n):
        copy_shard(me[0], n, s, pieces, None, x.at[:, pl.ds(s * part, part)], sem.at[s])
    for s in range(n):
        pltpu.make_async_copy(pieces[0], x.at[:, pl.ds(s * part, part)], sem.at[s]).wait()
    full = x[...].astype(F32)
    scale = lax.rsqrt(jnp.mean(full * full, axis=-1, keepdims=True) + 1e-06)
    moe_in = (full * scale * gain[...]).astype(BF)
    n_exp = len(outs) // groups
    for i in range(groups):
        for k in range(n_exp):
            outs[i * n_exp + k][...] = jnp.dot(
                picks[i][k], moe_in, preferred_element_type=F32
            ).astype(BF)


def route_call(n, pieces, gain, picks):
    n_exp, _, size = picks[0].shape
    width = n * pieces[0].shape[1]
    sizes = [p.shape[1] for p in picks for _ in range(n_exp)]
    outs = pl.pallas_call(
        lambda *refs: route_kernel(n, len(picks), *refs),
        name="route",
        out_shape=[jax.ShapeDtypeStruct((taken, width), BF) for taken in sizes],
        in_specs=[SMEM] + [ANY] * (2 * n - 1) + [VMEM] * (1 + len(picks)),
        out_specs=[VMEM] * len(sizes),
        scratch_shapes=[pltpu.VMEM((size, width), BF), pltpu.SemaphoreType.DMA((n,))],
        compiler_params=params(32),
        cost_estimate=pl.CostEstimate(
            flops=2 * sum(sizes) * size * width, transcendentals=0, bytes_accessed=12 << 20
        ),
    )(where_am_i(), *pieces, gain, *picks)
    return [outs[i : i + n_exp] for i in range(0, len(outs), n_exp)]


def gate_up_kernel(count, tiles, *refs):
    pieces, weights, (out, x, w, acc, x_sem, w_sem) = (
        refs[:count],
        refs[count : count + 2],
        refs[count + 2 :],
    )
    units, deep = weights[0].shape[1:]
    tile = deep // tiles
    each = pieces[0].shape[0]

    def copies(t):
        made = []
        for i in range(4):
            made.append(
                pltpu.make_async_copy(
                    weights[i // 2].at[i % 2, :, pl.ds(t * tile, tile)],
                    w.at[t % 2, pl.ds(i * units, units)],
                    w_sem.at[t % 2, i],
                )
            )
        return made

    moves = [
        pltpu.make_async_copy(p, x.at[pl.ds(i * each, each)], x_sem.at[i])
        for i, p in enumerate(pieces)
    ]
    for c in copies(0) + moves + copies(1):
        c.start()
    for c in moves:
        c.wait()
    for t in range(tiles):
        for c in copies(t):
            c.wait()
        product = lax.dot_general(
            x[:, pl.ds(t * tile, tile)],
            w[t % 2],
            (((1,), (1,)), ((), ())),
            preferred_element_type=F32,
        )
        acc[...] = product if t == 0 else acc[...] + product
        if t + 2 < tiles:
            for c in copies(t + 2):
                c.start()
    gate, up = acc[:, : 2 * units], acc[:, 2 * units :]
    out[...] = (gate / (1.0 + jnp.exp(-gate)) * up).astype(BF)


def gate_up_call(pieces, weights):
    units, deep = weights[0].shape[1:]
    if pieces[0].shape[0] % 16:
        pieces = [jnp.concatenate(pieces, axis=0)]
    size = len(pieces) * pieces[0].shape[0]
    tiles = 4
    return pl.pallas_call(
        lambda *refs: gate_up_kernel(len(pieces), tiles, *refs),
        name="gate_up",
        out_shape=jax.ShapeDtypeStruct((size, 2 * units), BF),
        in_specs=[ANY] * (len(pieces) + 2),
        out_specs=VMEM,
        scratch_shapes=[
            pltpu.VMEM((size, deep), BF),
            pltpu.VMEM((2, 4 * units, deep // tiles), BF),
            pltpu.VMEM((size, 4 * units), F32),
            pltpu.SemaphoreType.DMA((len(pieces),)),
            pltpu.SemaphoreType.DMA((2, 4)),
        ],
        compiler_params=params(48),
        cost_estimate=pl.CostEstimate(
            flops=8 * size * deep * units,
            transcendentals=2 * size * units,
            bytes_accessed=8 * units * deep + 2 * size * deep,
        ),
    )(*pieces, *weights)


def down_kernel(n, count, me, *refs):
    pieces, (weights, *outs) = refs[: 2 * n - 1], refs[2 * n - 1 :]
    outs, (x, w, acc, x_sem, w_sem) = outs[:count], outs[count:]
    cols = weights.shape[2]
    deep = weights.shape[1] // n

    def copies(s):
        return [
            pltpu.make_async_copy(
                weights.at[i, pl.ds(s * deep, deep)],
                w.at[s, :, pl.ds(i * cols, cols)],
                w_sem.at[s, i],
            )
            for i in range(2)
        ]

    for s in range(n):
        copy_shard(me[0], n, s, pieces, None, x.at[s], x_sem.at[s])
        for c in copies(s):
            c.start()
    for s in range(n):
        pltpu.make_async_copy(pieces[0], x.at[s], x_sem.at[s]).wait()
        for c in copies(s):
            c.wait()
        product = jnp.dot(x[s], w[s], preferred_element_type=F32)
        acc[...] = product if s == 0 else acc[...] + product
    each = acc.shape[0] // count
    for i in range(count):
        outs[i][...] = acc[pl.ds(i * each, each), :].astype(BF)


def down_call(n, n_exp, pieces, weights):
    size, deep = pieces[0].shape
    cols = weights.shape[2]
    count = n_exp if size // n_exp % 16 == 0 else 1
    outs = pl.pallas_call(
        lambda *refs: down_kernel(n, count, *refs),
        name="down",
        out_shape=[jax.ShapeDtypeStruct((size // count, 2 * cols), BF)] * count,
        in_specs=[SMEM] + [ANY] * (2 * n),
        out_specs=[VMEM] * count,
        scratch_shapes=[
            pltpu.VMEM((n, size, deep), BF),
            pltpu.VMEM((n, deep, 2 * cols), BF),
            pltpu.VMEM((size, 2 * cols), F32),
            pltpu.SemaphoreType.DMA((n,)),
            pltpu.SemaphoreType.DMA((n, 2)),
        ],
        compiler_params=params(40),
        cost_estimate=pl.CostEstimate(
            flops=4 * n * size * deep * cols, transcendentals=0, bytes_accessed=20 << 20
        ),
    )(where_am_i(), *pieces, weights)
    return outs if count == n_exp else list(outs[0].reshape(n_exp, -1, 2 * cols))


def absolute(pieces, axis):
    n = len(pieces)
    z = lax.axis_index("z")
    stacked = jnp.stack(pieces)
    return jnp.concatenate(
        [
            lax.dynamic_index_in_dim(stacked, lax.rem(z - s + n, n), 0, keepdims=False)
            for s in range(n)
        ],
        axis=axis,
    )


def attention(queries, keys, values, decay_rate, start_state, first):
    core, z, n_z = lax.axis_index("core"), lax.axis_index("z"), lax.axis_size("z")
    heads, head_dim = start_state.shape[:2]
    length = queries.shape[0]
    queries = queries.reshape(length, heads, head_dim)
    keys = keys.reshape(length, heads, head_dim)
    values = values.reshape(length, heads, head_dim)
    positions = jnp.arange(length)
    upto = positions[:, None] <= positions[None, :]
    cum = jnp.dot(decay_rate, upto.astype(F32), precision=lax.Precision.HIGHEST)
    total = cum[:, -1]
    scaled_keys = keys.astype(F32) * jnp.exp(cum - total[:, None]).T[:, :, None]
    local = jnp.einsum(
        "shd,she->hde", scaled_keys, values.astype(F32), precision=lax.Precision.HIGHEST
    )
    other_total, other_local = swap_core(total), swap_core(local.astype(BF)).astype(F32)
    total0, total1 = by_core(core, total, other_total)
    half = heads // 2

    def mine(x):
        return lax.dynamic_slice_in_dim(x, core * half, half, 0)

    own_half, other_half = mine(local), mine(other_local)
    local0, local1 = by_core(core, own_half, other_half)
    chip_total = total0 + total1
    chip_state = (jnp.exp(-mine(total1))[:, None, None] * local0 + local1).astype(BF)
    chip_state = after(chip_state, first)
    earlier_states = [shift_z(chip_state, k) for k in range(1, n_z)]
    earlier_totals = [shift_z(chip_total, k) for k in range(1, n_z)]

    causal = upto.T[None, :, :]
    diff = cum[:, None, :] - cum[:, :, None]
    decay = jnp.where(causal, jnp.exp(jnp.where(causal, diff, 0.0)), 0.0)
    scores = jnp.einsum("thd,shd->hts", queries, keys, preferred_element_type=F32)
    weights = (scores * decay).astype(BF)
    intra = jnp.einsum("hts,shd->thd", weights, values, preferred_element_type=F32)

    earlier_states = after(earlier_states, intra)
    passed = jnp.zeros_like(total)
    incoming = jnp.zeros((half, head_dim, head_dim), F32)
    for state, decayed in zip(earlier_states, earlier_totals):
        incoming = incoming + jnp.exp(-mine(passed))[:, None, None] * state.astype(F32)
        passed = passed + decayed
    incoming = incoming + jnp.exp(-mine(passed))[:, None, None] * mine(start_state)
    incoming = incoming.astype(BF)
    in0, in1 = by_core(core, incoming, swap_core(incoming))
    incoming = jnp.concatenate([in0, in1], axis=0).astype(F32)
    incoming = jnp.where(
        core == 0, incoming, jnp.exp(-total0)[:, None, None] * incoming + other_local
    )
    inter = jnp.einsum(
        "thd,hde->the", queries.astype(F32), incoming, precision=lax.Precision.HIGHEST
    )
    attended = intra + inter * jnp.exp(-cum).T[:, :, None]
    scale = lax.rsqrt(jnp.mean(attended * attended, axis=-1, keepdims=True) + 1e-06)
    return (attended * scale).astype(BF).reshape(length, heads * head_dim)


def shards(
    residual,
    attn_queries,
    attn_keys,
    attn_values,
    decay_rate,
    start_state,
    out_proj,
    moe_gain,
    gate_proj,
    up_proj,
    down_proj,
    expert_ids,
    expert_gates,
):
    n_z, n_exp = lax.axis_size("z"), lax.axis_size("expert")
    z, core, expert = lax.axis_index("z"), lax.axis_index("core"), lax.axis_index("expert")
    rows, width = residual.shape
    part = width // n_z
    capacity = 3 * rows // n_exp

    w_out, w_gate, w_up, w_down = [
        lax.all_gather(w, "core") for w in (out_proj, gate_proj[0].T, up_proj[0].T, down_proj[0])
    ]

    named = jnp.concatenate([expert_ids.astype(F32), expert_gates], axis=1)
    named = absolute([named[None]] + [shift_z(named[None], k, True) for k in range(1, n_z)], 0)
    ids, gates = named[:, :, :2].astype(jnp.int32), named[:, :, 2:]

    def columns_of(k):
        return lax.dynamic_slice_in_dim(residual, lax.rem(z + k, n_z) * part, part, axis=1)

    kept = [columns_of(0)] + [shift_z(columns_of(k), k, True) for k in range(1, n_z)]
    kept = absolute(kept, 0).reshape(n_z, rows, part)

    partner = expert ^ jnp.arange(n_exp)
    names = ids[:, :, :, None] == partner
    member = jnp.any(names, axis=2)
    before = jnp.arange(rows)[None, :] < jnp.arange(rows)[:, None]
    slot = jnp.einsum(
        "tu,suk->stk", before.astype(BF), member.astype(BF), preferred_element_type=F32
    ).astype(jnp.int32)
    places = jnp.arange(capacity)
    placed = member[:, :, :, None] & (slot[:, :, :, None] == places)
    chosen = names[:, :, :, :, None] & (slot[:, :, None, :, None] == places)
    chosen = chosen.astype(BF).reshape(n_z, rows, 2, n_exp * capacity)

    head_out = attention(
        attn_queries, attn_keys, attn_values, decay_rate, start_state, (named, kept)
    )
    acts = line_gather(head_out)
    gain = moe_gain.reshape(1, width)

    def of_block(x, block):
        return jnp.stack([x[s] for s in block])

    def project(block, first):
        pieces = project_call(block, n_z, n_exp, rows, acts, w_out)
        arrived = [pieces[0]] + [
            to_expert(after(pieces[k], first), k) for k in range(1, n_exp)
        ]
        total = jnp.concatenate([kept[s] for s in block], axis=0).astype(F32)
        for x in arrived:
            total = total + x.astype(F32)
        return total.astype(BF), arrived

    def route(block, groups, pieces):
        picks = []
        for group in groups:
            here = jnp.array([[s == t for t in block] for s in group])[None, :, None, :, None]
            one = of_block(placed, group).transpose(2, 0, 3, 1)[:, :, :, None, :] & here
            one = one.astype(BF)
            picks.append(one.reshape(n_exp, len(group) * capacity, len(block) * rows))
        return route_call(n_z, pieces, gain, picks)

    def combine(block, stream, hidden):
        expert_out = down_call(n_z, n_exp, hidden, w_down)
        returned = [to_expert(expert_out[k], k) if k else expert_out[k] for k in range(n_exp)]
        returned = [x.reshape(len(block), capacity, part) for x in returned]
        returned = jnp.concatenate(returned, axis=1)
        out = stream.reshape(len(block), rows, part).astype(F32)
        for j in range(2):
            picked = jnp.einsum(
                "str,srd->std",
                of_block(chosen, block)[:, :, j],
                returned,
                preferred_element_type=F32,
            )
            out = out + picked * of_block(gates, block)[:, :, j, None]
        return out.astype(BF)

    middle_first = sorted(range(n_z), key=lambda s: abs(2 * s - n_z + 1))
    size = n_z // len(GROUPS)
    near = slice(n_z - 2, n_z + 1)
    groups, streams, waiting = [], [], []
    summed = sent = full = routed = hidden = ()
    for i, count in enumerate(GROUPS):
        block = middle_first[i * size : (i + 1) * size]
        stream, summed = project(block, summed)
        full = line_gather(after(stream, full, sent))
        fine = [block[j : j + size // count] for j in range(0, size, size // count)]
        sent = route(block, fine, full)
        for group, rows_for in zip(fine, sent):
            routed = [rows_for[0]] + [
                to_expert(after(rows_for[k], routed), k) for k in range(1, n_exp)
            ]
            started = hidden[near]
            made = gate_up_call([after(x, started) for x in routed], (w_gate, w_up))
            hidden = line_gather(after(made, hidden[1:-1]))
            at = [block.index(s) * rows for s in group]
            groups.append(group)
            streams.append(jnp.stack([stream[r : r + rows] for r in at]))
            waiting.append(hidden)
    out = [None] * n_z
    for i, group in enumerate(groups):
        later = waiting[i + 1][near] if i + 1 < len(groups) else ()
        pieces = [after(x, later) for x in waiting[i]]
        for s, piece in zip(group, combine(group, streams[i], pieces)):
            out[s] = piece
    out = jnp.stack(out)

    def rows_of(k):
        return lax.dynamic_index_in_dim(out, lax.rem(z + k, n_z), 0, keepdims=False)

    return absolute([rows_of(0)] + [shift_z(rows_of(k), k, True) for k in range(1, n_z)], 1)


def solution(mesh):
    n_ctx, n_exp = mesh.shape["context"], mesh.shape["expert"]
    fine = Mesh(mesh.devices.reshape(n_ctx // 2, 2, n_exp), ("z", "core", "expert"))
    ctx = ("z", "core")
    owner = ("z", "core", "expert")
    placed = (
        P(owner, None),
        P(ctx, "expert"),
        P(ctx, "expert"),
        P(ctx, "expert"),
        P("expert", ctx),
        P("expert", None, None),
        P("expert", ctx),
        P(),
        P("expert", None, ctx),
        P("expert", None, ctx),
        P("expert", None, ctx),
        P(owner, None),
        P(owner, None),
    )
    return jax.shard_map(
        shards, mesh=fine, in_specs=placed, out_specs=P(owner, None), check_vma=False
    )
```

profile of v0, /device:TPU:0, one launch (start us, length us, event | category | flops | bytes accessed | tf_op | source)
XLA Modules:
  0.0 456.4 jit_solution(7496436168877497330)
XLA Ops:
  8.8 5.1 %collective-permute-start.7 = (f32[1,64,4]{1,2,0:T(4,128)S(1)}, f32[1,64,4]{1,2,0:T(4,128)S(1)}, u32[]{:S(2)}, u32[]{:S(2)}) collective-permute-start(f32[1,64,4]{1,2,0:T(4,128)S(1)} %get-tuple-element.270), channel_id=1, source_target_pairs={{0,24},{8,0},{16,8},{24,16},{1,25},{9,1},{17,9},{25,17},{2,26},{10... | collective-permute-start | bytes 3080 | tf_op jit(solution)/shard_map/ppermute | solution.py:28
  17.1 3.4 fusion.64
  20.6 4.6 %convolution_bitcast_fusion = f32[256,16,128]{0,2,1:T(8,128)} fusion(bf16[256,16,128]{0,2,1:T(8,128)(2,1)S(1)} %bitcast.196, f32[16,256]{1,0:T(8,128)S(1)} %bitcast.211, pred[256,256]{1,0:T(8,128)(4,1)S(1)} %iota_compare_fusion.2, bf16[256,2048]{1,0:T(8,128)(2,1)} %param.19, bf16[256,2048]{1,0:T(8,128)(2,1)S(1)} %copy-done), kind=kOutput, calls=%fused_computation.23 | convolution fusion | flops 542113792 | bytes 5324800 | tf_op jit(solution)/shard_map/hts,shd->thd/dot_general | solution.py:341
  25.2 4.7 %collective-permute-start.13 = (f32[16]{0:T(128)S(1)}, f32[16]{0:T(128)S(1)}, u32[]{:S(2)}, u32[]{:S(2)}) collective-permute-start(f32[16]{0:T(128)S(1)} %get-tuple-element.221), channel_id=1, source_target_pairs={{0,24},{1,25},{2,26},{3,27},{4,28},{5,29},{6,30},{7,31}} | collective-permute-start | bytes 200 | tf_op jit(solution)/shard_map/ppermute | solution.py:28
  31.2 2.5 collective-permute-start.12
  36.5 1.9 collective-permute-start.9
  40.0 3.2 collective-permute-done.8
  43.1 5.7 %collective-permute-done.9 = bf16[8,128,128]{2,1,0:T(8,128)(2,1)S(1)} collective-permute-done((bf16[8,128,128]{2,1,0:T(8,128)(2,1)S(1)}, bf16[8,128,128]{2,1,0:T(8,128)(2,1)S(1)}, u32[]{:S(2)}, u32[]{:S(2)}) %collective-permute-start.9) | collective-permute-done | bytes 262176 | tf_op jit(solution)/shard_map/ppermute | solution.py:28
  48.8 4.9 %collective-permute-done.10 = bf16[8,128,128]{2,1,0:T(8,128)(2,1)S(1)} collective-permute-done((bf16[8,128,128]{2,1,0:T(8,128)(2,1)S(1)}, bf16[8,128,128]{2,1,0:T(8,128)(2,1)S(1)}, u32[]{:S(2)}, u32[]{:S(2)}) %collective-permute-start.10) | collective-permute-done | bytes 262176 | tf_op jit(solution)/shard_map/ppermute | solution.py:28
  54.1 1.9 collective-permute-done.14
  56.1 2.5 multiply_reduce_fusion
  59.6 7.7 %collective-permute-start.15 = (bf16[256,2048]{1,0:T(8,128)(2,1)S(1)}, bf16[256,2048]{1,0:T(8,128)(2,1)S(1)}, u32[]{:S(2)}, u32[]{:S(2)}) collective-permute-start(bf16[256,2048]{1,0:T(8,128)(2,1)S(1)} %copy.55.refs_4_.refs_3_), channel_id=1, source_target_pairs={{0,8},{8,16},{16,24},{1,9},{9,17},{17,25},{2,10},{10,18},{18,26},{... | collective-permute-start | bytes 3145736 | tf_op jit(solution)/shard_map/ppermute | solution.py:47
  68.7 21.3 %collective-permute-done.15.refs_3_.refs_2_ = bf16[256,2048]{1,0:T(8,128)(2,1)S(1)} collective-permute-done((bf16[256,2048]{1,0:T(8,128)(2,1)S(1)}, bf16[256,2048]{1,0:T(8,128)(2,1)S(1)}, u32[]{:S(2)}, u32[]{:S(2)}) %collective-permute-start.15) | collective-permute-done | bytes 1048608 | tf_op jit(solution)/shard_map/ppermute | solution.py:47
  90.0 4.3 collective-permute-done.16.refs_5_.refs_4_
  94.2 1.7 collective-permute-start.17
  98.0 2.2 collective-permute-start.2
  100.2 6.0 %collective-permute-start.1 = (bf16[64,1536]{1,0:T(8,128)(2,1)}, bf16[64,1536]{1,0:T(8,128)(2,1)}, u32[]{:S(2)}, u32[]{:S(2)}) collective-permute-start(bf16[64,1536]{1,0:T(8,128)(2,1)} %get-tuple-element.238), channel_id=1, source_target_pairs={{0,16},{8,24},{16,0},{24,8},{1,17},{9,25},{17,1},{25,9},{2,18},{10... | collective-permute-start | bytes 589832 | tf_op jit(solution)/shard_map/ppermute | solution.py:28
  106.2 2.0 collective-permute-start
  109.5 22.0 %collective-permute-done.18.refs_6_.refs_5_ = bf16[256,2048]{1,0:T(8,128)(2,1)} collective-permute-done((bf16[256,2048]{1,0:T(8,128)(2,1)}, bf16[256,2048]{1,0:T(8,128)(2,1)}, u32[]{:S(2)}, u32[]{:S(2)}) %collective-permute-start.18) | collective-permute-done | bytes 1048608 | tf_op jit(solution)/shard_map/ppermute | solution.py:48
  131.5 1.6 collective-permute-start.19
  134.5 2.8 copy-done.2
  137.3 6.5 %project.3 = (bf16[128,1536]{1,0:T(8,128)(2,1)S(1)}, bf16[128,1536]{1,0:T(8,128)(2,1)S(1)}, bf16[128,1536]{1,0:T(8,128)(2,1)S(1)}, bf16[128,1536]{1,0:T(8,128)(2,1)S(1)}) custom-call(s32[3]{0:T(128)S(1)} %pad_add_fusion.refs_0_, bf16[256,2048]{1,0:T(8,128)(2,1)} %collective-permute-done.17.refs_2_.refs_1_, ...), custom_call_target="tpu_custom_call" | custom-call | flops 3221225472 | bytes 12582912 | tf_op jit(solution)/shard_map/project/pallas_call | solution.py:107
  149.3 5.9 %collective-permute-done.21 = bf16[128,1536]{1,0:T(8,128)(2,1)S(1)} collective-permute-done((bf16[128,1536]{1,0:T(8,128)(2,1)S(1)}, bf16[128,1536]{1,0:T(8,128)(2,1)S(1)}, u32[]{:S(2)}, u32[]{:S(2)}) %collective-permute-start.21) | collective-permute-done | bytes 393248 | tf_op jit(solution)/shard_map/ppermute | solution.py:33
  155.1 5.4 %collective-permute-done.22 = bf16[128,1536]{1,0:T(8,128)(2,1)S(1)} collective-permute-done((bf16[128,1536]{1,0:T(8,128)(2,1)S(1)}, bf16[128,1536]{1,0:T(8,128)(2,1)S(1)}, u32[]{:S(2)}, u32[]{:S(2)}) %collective-permute-start.22) | collective-permute-done | bytes 393248 | tf_op jit(solution)/shard_map/ppermute | solution.py:33
  160.8 8.3 %collective-permute-start.27 = (bf16[128,1536]{1,0:T(8,128)(2,1)S(1)}, bf16[128,1536]{1,0:T(8,128)(2,1)S(1)}, u32[]{:S(2)}, u32[]{:S(2)}) collective-permute-start(bf16[128,1536]{1,0:T(8,128)(2,1)S(1)} %add_convert_fusion.refs_4_), channel_id=1, source_target_pairs={{0,8},{8,16},{16,24},{1,9},{9,17},{17,25},{2,10},{10,18},{18,26},{... | collective-permute-start | bytes 1179656 | tf_op jit(solution)/shard_map/ppermute | solution.py:47
  171.2 6.6 %project.2 = (bf16[128,1536]{1,0:T(8,128)(2,1)S(1)}, bf16[128,1536]{1,0:T(8,128)(2,1)}, bf16[128,1536]{1,0:T(8,128)(2,1)}, bf16[128,1536]{1,0:T(8,128)(2,1)}) custom-call(s32[3]{0:T(128)S(1)} %pad_add_fusion.refs_0_, bf16[256,2048]{1,0:T(8,128)(2,1)} %collective-permute-done.19.refs_1_, bf16[256,2048]{1,0:T(8,128)(2,1)} %collective-permute-done.17.refs_2_.refs_1_, ...), custom_call_target="tpu_custom_call" | custom-call | flops 3221225472 | bytes 12582912 | tf_op jit(solution)/shard_map/project/pallas_call | solution.py:107
  184.6 12.7 %collective-permute-done.30.refs_6_ = bf16[128,1536]{1,0:T(8,128)(2,1)S(1)} collective-permute-done((bf16[128,1536]{1,0:T(8,128)(2,1)}, bf16[128,1536]{1,0:T(8,128)(2,1)S(1)}, u32[]{:S(2)}, u32[]{:S(2)}) %collective-permute-start.30) | collective-permute-done | bytes 393248 | tf_op jit(solution)/shard_map/ppermute | solution.py:48
  200.7 7.0 %collective-permute-done.32.refs_7_ = bf16[128,1536]{1,0:T(8,128)(2,1)S(1)} collective-permute-done((bf16[128,1536]{1,0:T(8,128)(2,1)S(1)}, bf16[128,1536]{1,0:T(8,128)(2,1)S(1)}, u32[]{:S(2)}, u32[]{:S(2)}) %collective-permute-start.32) | collective-permute-done | bytes 393248 | tf_op jit(solution)/shard_map/ppermute | solution.py:48
  207.7 3.9 route.2
  214.1 2.2 collective-permute-start.33
  218.7 1.7 collective-permute-start.40
  221.8 8.3 %collective-permute-done.34.refs_5_ = bf16[128,1536]{1,0:T(8,128)(2,1)} collective-permute-done((bf16[128,1536]{1,0:T(8,128)(2,1)S(1)}, bf16[128,1536]{1,0:T(8,128)(2,1)}, u32[]{:S(2)}, u32[]{:S(2)}) %collective-permute-start.34) | collective-permute-done | bytes 393248 | tf_op jit(solution)/shard_map/ppermute | solution.py:48
  235.2 9.7 %collective-permute-done.41.refs_3_ = bf16[48,6144]{1,0:T(8,128)(2,1)} collective-permute-done((bf16[48,6144]{1,0:T(8,128)(2,1)}, bf16[48,6144]{1,0:T(8,128)(2,1)}, u32[]{:S(2)}, u32[]{:S(2)}) %collective-permute-start.41) | collective-permute-done | bytes 589856 | tf_op jit(solution)/shard_map/ppermute | solution.py:33
  245.0 2.2 collective-permute-start.45
  252.6 15.7 %gate_up.3.refs_4_ = bf16[192,1152]{1,0:T(8,128)(2,1)S(1)} custom-call(bf16[48,6144]{1,0:T(8,128)(2,1)S(1)} %get-tuple-element.138.refs_0_, bf16[48,6144]{1,0:T(8,128)(2,1)S(1)} %copy-done.5, bf16[48,6144]{1,0:T(8,128)(2,1)S(1)} %copy-done.7, bf16[48,6144]{1,0:T(8,128)(2,1)} %collective-permute-done.41.refs_3_, bf16[2,576,6144]{2,1,0:T(8,128)(2,1)} %bitcast.187, ...), custom_call_target="tpu_custom_call" | custom-call | flops 5435817984 | bytes 30670848 | tf_op jit(solution)/shard_map/gate_up/pallas_call | solution.py:215
  268.4 5.3 %collective-permute-start.42 = (bf16[192,1152]{1,0:T(8,128)(2,1)S(1)}, bf16[192,1152]{1,0:T(8,128)(2,1)S(1)}, u32[]{:S(2)}, u32[]{:S(2)}) collective-permute-start(bf16[192,1152]{1,0:T(8,128)(2,1)S(1)} %gate_up.3.refs_4_), channel_id=1, source_target_pairs={{0,8},{8,16},{16,24},{1,9},{9,17},{17,25},{2,10},{10,18},{18,26},{... | collective-permute-start | bytes 1327112 | tf_op jit(solution)/shard_map/ppermute | solution.py:47
  275.0 3.7 route.3
  279.1 1.9 collective-permute-start.52
  286.6 15.9 %gate_up.4.refs_4_ = bf16[192,1152]{1,0:T(8,128)(2,1)S(1)} custom-call(bf16[48,6144]{1,0:T(8,128)(2,1)S(1)} %get-tuple-element.156.refs_0_, bf16[48,6144]{1,0:T(8,128)(2,1)S(1)} %collective-permute-done.44.refs_1_, bf16[48,6144]{1,0:T(8,128)(2,1)} %collective-permute-done.45.refs_2_, bf16[48,6144]{1,0:T(8,128)(2,1)} %collective-permute-done.46.refs_3_, ...), custom_call_target="tpu_custom_call" | custom-call | flops 5435817984 | bytes 30670848 | tf_op jit(solution)/shard_map/gate_up/pallas_call | solution.py:215
  302.5 4.9 %collective-permute-start.49 = (bf16[192,1152]{1,0:T(8,128)(2,1)S(1)}, bf16[192,1152]{1,0:T(8,128)(2,1)S(1)}, u32[]{:S(2)}, u32[]{:S(2)}) collective-permute-start(bf16[192,1152]{1,0:T(8,128)(2,1)S(1)} %gate_up.4.refs_4_), channel_id=1, source_target_pairs={{0,8},{8,16},{16,24},{1,9},{9,17},{17,25},{2,10},{10,18},{18,26},{... | collective-permute-start | bytes 1327112 | tf_op jit(solution)/shard_map/ppermute | solution.py:47
  308.6 4.5 collective-permute-done.49.refs_3_
  313.1 5.2 %collective-permute-done.50.refs_5_ = bf16[192,1152]{1,0:T(8,128)(2,1)S(1)} collective-permute-done((bf16[192,1152]{1,0:T(8,128)(2,1)S(1)}, bf16[192,1152]{1,0:T(8,128)(2,1)S(1)}, u32[]{:S(2)}, u32[]{:S(2)}) %collective-permute-start.50) | collective-permute-done | bytes 442400 | tf_op jit(solution)/shard_map/ppermute | solution.py:48
  319.7 1.7 collective-permute-start.55
  321.4 16.5 %gate_up.5.refs_4_ = bf16[384,1152]{1,0:T(8,128)(2,1)S(1)} custom-call(bf16[96,6144]{1,0:T(8,128)(2,1)S(1)} %get-tuple-element.168.refs_0_, bf16[96,6144]{1,0:T(8,128)(2,1)S(1)} %collective-permute-done.51.refs_1_, bf16[96,6144]{1,0:T(8,128)(2,1)S(1)} %collective-permute-done.52.refs_2_, bf16[96,6144]{1,0:T(8,128)(2,1)S(1)} %collective-permute-done.53.refs_3_, ...), custom_call_target="tpu_custom_call" | custom-call | flops 10871635968 | bytes 33030144 | tf_op jit(solution)/shard_map/gate_up/pallas_call | solution.py:215
  338.0 5.9 %collective-permute-start.56 = (bf16[384,1152]{1,0:T(8,128)(2,1)S(1)}, bf16[384,1152]{1,0:T(8,128)(2,1)S(1)}, u32[]{:S(2)}, u32[]{:S(2)}) collective-permute-start(bf16[384,1152]{1,0:T(8,128)(2,1)S(1)} %gate_up.5.refs_4_), channel_id=1, source_target_pairs={{0,8},{8,16},{16,24},{1,9},{9,17},{17,25},{2,10},{10,18},{18,26},{... | collective-permute-start | bytes 2654216 | tf_op jit(solution)/shard_map/ppermute | solution.py:47
  348.9 5.5 %collective-permute-done.56.refs_3_ = bf16[384,1152]{1,0:T(8,128)(2,1)S(1)} collective-permute-done((bf16[384,1152]{1,0:T(8,128)(2,1)S(1)}, bf16[384,1152]{1,0:T(8,128)(2,1)S(1)}, u32[]{:S(2)}, u32[]{:S(2)}) %collective-permute-start.56) | collective-permute-done | bytes 884768 | tf_op jit(solution)/shard_map/ppermute | solution.py:47
  354.4 12.5 %collective-permute-done.57.refs_5_ = bf16[384,1152]{1,0:T(8,128)(2,1)} collective-permute-done((bf16[384,1152]{1,0:T(8,128)(2,1)S(1)}, bf16[384,1152]{1,0:T(8,128)(2,1)}, u32[]{:S(2)}, u32[]{:S(2)}) %collective-permute-start.57) | collective-permute-done | bytes 884768 | tf_op jit(solution)/shard_map/ppermute | solution.py:48
  366.9 1.6 collective-permute-start.58
  377.1 8.0 %down.4 = (bf16[48,1536]{1,0:T(8,128)(2,1)S(1)}, bf16[48,1536]{1,0:T(8,128)(2,1)S(1)}, bf16[48,1536]{1,0:T(8,128)(2,1)}, bf16[48,1536]{1,0:T(8,128)(2,1)}) custom-call(s32[3]{0:T(128)S(1)} %pad_add_fusion.refs_0_, bf16[192,1152]{1,0:T(8,128)(2,1)S(1)} %copy-done.17, bf16[192,1152]{1,0:T(8,128)(2,1)} %collective-permute-done.47.refs_2_, ...), custom_call_target="tpu_custom_call" | custom-call | flops 2717908992 | bytes 20971520 | tf_op jit(solution)/shard_map/down/pallas_call | solution.py:272
  386.4 1.7 collective-permute-start.69
  389.1 1.6 copy.48
  390.7 1.8 collective-permute-start.67
  399.8 4.3 collective-permute-done.71.refs_7_
  404.1 7.2 %down.5 = (bf16[48,1536]{1,0:T(8,128)(2,1)S(1)}, bf16[48,1536]{1,0:T(8,128)(2,1)S(1)}, bf16[48,1536]{1,0:T(8,128)(2,1)S(1)}, bf16[48,1536]{1,0:T(8,128)(2,1)S(1)}) custom-call(s32[3]{0:T(128)S(1)} %pad_add_fusion.refs_0_, bf16[192,1152]{1,0:T(8,128)(2,1)S(1)} %collective-permute-done.70.refs_1_, bf16[192,1152]{1,0:T(8,128)(2,1)} %collective-permute-done.54.refs_2_, ...), custom_call_target="tpu_custom_call" | custom-call | flops 2717908992 | bytes 20971520 | tf_op jit(solution)/shard_map/down/pallas_call | solution.py:272
  411.3 1.7 collective-permute-start.74
  413.1 1.7 collective-permute-start.72
  414.8 9.3 %down.3 = (bf16[96,1536]{1,0:T(8,128)(2,1)S(1)}, bf16[96,1536]{1,0:T(8,128)(2,1)S(1)}, bf16[96,1536]{1,0:T(8,128)(2,1)S(1)}, bf16[96,1536]{1,0:T(8,128)(2,1)S(1)}) custom-call(s32[3]{0:T(128)S(1)} %pad_add_fusion.refs_0_, bf16[384,1152]{1,0:T(8,128)(2,1)S(1)} %collective-permute-done.60.refs_1_, bf16[384,1152]{1,0:T(8,128)(2,1)} %collective-permute-done.58.refs_2_, ...), custom_call_target="tpu_custom_call" | custom-call | flops 5435817984 | bytes 20971520 | tf_op jit(solution)/shard_map/down/pallas_call | solution.py:272
  424.2 1.7 collective-permute-start.64
  426.0 1.7 collective-permute-start.62
  428.3 3.7 collective-permute-done.64
  432.0 3.1 collective-permute-done.63
  435.9 1.9 collective-permute-start.77
  438.4 3.2 collective-permute-done.77
  441.7 6.6 %collective-permute-done.76 = bf16[64,1536]{1,0:T(8,128)(2,1)S(1)} collective-permute-done((bf16[64,1536]{1,0:T(8,128)(2,1)S(1)}, bf16[64,1536]{1,0:T(8,128)(2,1)S(1)}, u32[]{:S(2)}, u32[]{:S(2)}) %collective-permute-start.76) | collective-permute-done | bytes 196640 | tf_op jit(solution)/shard_map/ppermute | solution.py:28
  (276 shorter events, 89.3 us)
Async XLA Ops:
  6.5 127.9 %all-gather.10.cloned.1.call-start = ((), (), s32[]{:S(2)}) async-start(), calls=%async_computation.1 | async-start | bytes 9437184 | tf_op jit(solution)/shard_map/all_gather | solution.py:386
  7.3 243.2 %all-gather.12.cloned.1.call-start = ((), (), s32[]{:S(2)}) async-start(), calls=%async_computation.2 | async-start | bytes 21233664 | tf_op jit(solution)/shard_map/all_gather | solution.py:386
  8.0 242.5 %all-gather.14.cloned.1.call-start = ((), (), s32[]{:S(2)}) async-start(), calls=%async_computation.3 | async-start | bytes 21233664 | tf_op jit(solution)/shard_map/all_gather | solution.py:386
  8.7 364.3 %all-gather.8.cloned.1.call-start = ((), (), s32[]{:S(2)}) async-start(), calls=%async_computation | async-start | bytes 21233664 | tf_op jit(solution)/shard_map/all_gather | solution.py:386
  8.8 21.1 %collective-permute-start.7 = (f32[1,64,4]{1,2,0:T(4,128)S(1)}, f32[1,64,4]{1,2,0:T(4,128)S(1)}, u32[]{:S(2)}, u32[]{:S(2)}) collective-permute-start(f32[1,64,4]{1,2,0:T(4,128)S(1)} %get-tuple-element.270), channel_id=1, source_target_pairs={{0,24},{8,0},{16,8},{24,16},{1,25},{9,1},{17,9},{25,17},{2,26},{10... | collective-permute-start | bytes 3080 | tf_op jit(solution)/shard_map/ppermute | solution.py:28
  13.9 17.3 %collective-permute-start.6 = (f32[1,64,4]{1,2,0:T(4,128)S(1)}, f32[1,64,4]{1,2,0:T(4,128)S(1)}, u32[]{:S(2)}, u32[]{:S(2)}) collective-permute-start(f32[1,64,4]{1,2,0:T(4,128)S(1)} %get-tuple-element.270), channel_id=1, source_target_pairs={{0,16},{8,24},{16,0},{24,8},{1,17},{9,25},{17,1},{25,9},{2,18},{10... | collective-permute-start | bytes 3080 | tf_op jit(solution)/shard_map/ppermute | solution.py:28
  13.9 19.8 %collective-permute-start.5 = (f32[1,64,4]{1,2,0:T(4,128)S(1)}, f32[1,64,4]{1,2,0:T(4,128)S(1)}, u32[]{:S(2)}, u32[]{:S(2)}) collective-permute-start(f32[1,64,4]{1,2,0:T(4,128)S(1)} %get-tuple-element.270), channel_id=1, source_target_pairs={{0,8},{8,16},{16,24},{24,0},{1,9},{9,17},{17,25},{25,1},{2,10},{10... | collective-permute-start | bytes 3080 | tf_op jit(solution)/shard_map/ppermute | solution.py:28
  20.5 13.2 %collective-permute-start.4 = (bf16[16,128,128]{2,1,0:T(8,128)(2,1)}, bf16[16,128,128]{2,1,0:T(8,128)(2,1)}, u32[]{:S(2)}, u32[]{:S(2)}) collective-permute-start(bf16[16,128,128]{2,1,0:T(8,128)(2,1)} %get-tuple-element.272), channel_id=1, source_target_pairs={{0,4},{4,0},{1,5},{5,1},{2,6},{6,2},{3,7},{7,3},{8,12},{12,8},{9,1... | collective-permute-start | bytes 1572872 | tf_op jit(solution)/shard_map/ppermute | solution.py:19
  25.2 13.3 %collective-permute-start.13 = (f32[16]{0:T(128)S(1)}, f32[16]{0:T(128)S(1)}, u32[]{:S(2)}, u32[]{:S(2)}) collective-permute-start(f32[16]{0:T(128)S(1)} %get-tuple-element.221), channel_id=1, source_target_pairs={{0,24},{1,25},{2,26},{3,27},{4,28},{5,29},{6,30},{7,31}} | collective-permute-start | bytes 200 | tf_op jit(solution)/shard_map/ppermute | solution.py:28
  36.5 12.3 %collective-permute-start.9 = (bf16[8,128,128]{2,1,0:T(8,128)(2,1)S(1)}, bf16[8,128,128]{2,1,0:T(8,128)(2,1)S(1)}, u32[]{:S(2)}, u32[]{:S(2)}) collective-permute-start(bf16[8,128,128]{2,1,0:T(8,128)(2,1)S(1)} %add_convert_fusion.3), channel_id=1, source_target_pairs={{0,16},{8,24},{1,17},{9,25},{2,18},{10,26},{3,19},{11,27},{4,20},{... | collective-permute-start | bytes 786440 | tf_op jit(solution)/shard_map/ppermute | solution.py:28
  38.5 15.3 %collective-permute-start.10 = (bf16[8,128,128]{2,1,0:T(8,128)(2,1)S(1)}, bf16[8,128,128]{2,1,0:T(8,128)(2,1)S(1)}, u32[]{:S(2)}, u32[]{:S(2)}) collective-permute-start(bf16[8,128,128]{2,1,0:T(8,128)(2,1)S(1)} %add_convert_fusion.3), channel_id=1, source_target_pairs={{0,24},{1,25},{2,26},{3,27},{4,28},{5,29},{6,30},{7,31}} | collective-permute-start | bytes 786440 | tf_op jit(solution)/shard_map/ppermute | solution.py:28
  59.6 30.4 %collective-permute-start.15 = (bf16[256,2048]{1,0:T(8,128)(2,1)S(1)}, bf16[256,2048]{1,0:T(8,128)(2,1)S(1)}, u32[]{:S(2)}, u32[]{:S(2)}) collective-permute-start(bf16[256,2048]{1,0:T(8,128)(2,1)S(1)} %copy.55.refs_4_.refs_3_), channel_id=1, source_target_pairs={{0,8},{8,16},{16,24},{1,9},{9,17},{17,25},{2,10},{10,18},{18,26},{... | collective-permute-start | bytes 3145736 | tf_op jit(solution)/shard_map/ppermute | solution.py:47
  67.3 26.9 %collective-permute-start.16 = (bf16[256,2048]{1,0:T(8,128)(2,1)S(1)}, bf16[256,2048]{1,0:T(8,128)(2,1)}, u32[]{:S(2)}, u32[]{:S(2)}) collective-permute-start(bf16[256,2048]{1,0:T(8,128)(2,1)S(1)} %copy.55.refs_4_.refs_3_), channel_id=1, source_target_pairs={{24,16},{16,8},{8,0},{25,17},{17,9},{9,1},{26,18},{18,10},{10,2},{... | collective-permute-start | bytes 3145736 | tf_op jit(solution)/shard_map/ppermute | solution.py:48
  94.2 15.2 %collective-permute-start.17 = (bf16[256,2048]{1,0:T(8,128)(2,1)S(1)}, bf16[256,2048]{1,0:T(8,128)(2,1)}, u32[]{:S(2)}, u32[]{:S(2)}) collective-permute-start(bf16[256,2048]{1,0:T(8,128)(2,1)S(1)} %collective-permute-done.15.refs_3_.refs_2_), channel_id=1, source_target_pairs={{8,16},{16,24},{9,17},{17,25},{10,18},{18,26},{11,19},{19,27},{12,... | collective-permute-start | bytes 3145736 | tf_op jit(solution)/shard_map/ppermute | solution.py:47
  95.9 35.6 %collective-permute-start.18 = (bf16[256,2048]{1,0:T(8,128)(2,1)}, bf16[256,2048]{1,0:T(8,128)(2,1)}, u32[]{:S(2)}, u32[]{:S(2)}) collective-permute-start(bf16[256,2048]{1,0:T(8,128)(2,1)} %collective-permute-done.16.refs_5_.refs_4_), channel_id=1, source_target_pairs={{16,8},{8,0},{17,9},{9,1},{18,10},{10,2},{19,11},{11,3},{20,12},{1... | collective-permute-start | bytes 3145736 | tf_op jit(solution)/shard_map/ppermute | solution.py:48
  98.0 45.8 %collective-permute-start.2 = (bf16[64,1536]{1,0:T(8,128)(2,1)}, bf16[64,1536]{1,0:T(8,128)(2,1)S(1)}, u32[]{:S(2)}, u32[]{:S(2)}) collective-permute-start(bf16[64,1536]{1,0:T(8,128)(2,1)} %get-tuple-element.237), channel_id=1, source_target_pairs={{0,24},{8,0},{16,8},{24,16},{1,25},{9,1},{17,9},{25,17},{2,26},{10... | collective-permute-start | bytes 589832 | tf_op jit(solution)/shard_map/ppermute | solution.py:28
  100.2 45.1 %collective-permute-start.1 = (bf16[64,1536]{1,0:T(8,128)(2,1)}, bf16[64,1536]{1,0:T(8,128)(2,1)}, u32[]{:S(2)}, u32[]{:S(2)}) collective-permute-start(bf16[64,1536]{1,0:T(8,128)(2,1)} %get-tuple-element.238), channel_id=1, source_target_pairs={{0,16},{8,24},{16,0},{24,8},{1,17},{9,25},{17,1},{25,9},{2,18},{10... | collective-permute-start | bytes 589832 | tf_op jit(solution)/shard_map/ppermute | solution.py:28
  106.2 40.7 %collective-permute-start = (bf16[64,1536]{1,0:T(8,128)(2,1)}, bf16[64,1536]{1,0:T(8,128)(2,1)}, u32[]{:S(2)}, u32[]{:S(2)}) collective-permute-start(bf16[64,1536]{1,0:T(8,128)(2,1)} %get-tuple-element.236), channel_id=1, source_target_pairs={{0,8},{8,16},{16,24},{24,0},{1,9},{9,17},{17,25},{25,1},{2,10},{10... | collective-permute-start | bytes 589832 | tf_op jit(solution)/shard_map/ppermute | solution.py:28
  131.5 39.6 %collective-permute-start.19 = (bf16[256,2048]{1,0:T(8,128)(2,1)}, bf16[256,2048]{1,0:T(8,128)(2,1)}, u32[]{:S(2)}, u32[]{:S(2)}) collective-permute-start(bf16[256,2048]{1,0:T(8,128)(2,1)} %collective-permute-done.17.refs_2_.refs_1_), channel_id=1, source_target_pairs={{16,24},{17,25},{18,26},{19,27},{20,28},{21,29},{22,30},{23,31}} | collective-permute-start | bytes 3145736 | tf_op jit(solution)/shard_map/ppermute | solution.py:47
  133.2 38.0 %collective-permute-start.20 = (bf16[256,2048]{1,0:T(8,128)(2,1)}, bf16[256,2048]{1,0:T(8,128)(2,1)}, u32[]{:S(2)}, u32[]{:S(2)}) collective-permute-start(bf16[256,2048]{1,0:T(8,128)(2,1)} %collective-permute-done.18.refs_6_.refs_5_), channel_id=1, source_target_pairs={{8,0},{9,1},{10,2},{11,3},{12,4},{13,5},{14,6},{15,7}} | collective-permute-start | bytes 3145736 | tf_op jit(solution)/shard_map/ppermute | solution.py:48
  143.8 11.3 %collective-permute-start.21 = (bf16[128,1536]{1,0:T(8,128)(2,1)S(1)}, bf16[128,1536]{1,0:T(8,128)(2,1)S(1)}, u32[]{:S(2)}, u32[]{:S(2)}) collective-permute-start(bf16[128,1536]{1,0:T(8,128)(2,1)S(1)} %get-tuple-element.124), channel_id=1, source_target_pairs={{0,1},{1,0},{2,3},{3,2},{4,5},{5,4},{6,7},{7,6},{8,9},{9,8},{10,11... | collective-permute-start | bytes 1179656 | tf_op jit(solution)/shard_map/ppermute | solution.py:33
  145.4 15.2 %collective-permute-start.22 = (bf16[128,1536]{1,0:T(8,128)(2,1)S(1)}, bf16[128,1536]{1,0:T(8,128)(2,1)S(1)}, u32[]{:S(2)}, u32[]{:S(2)}) collective-permute-start(bf16[128,1536]{1,0:T(8,128)(2,1)S(1)} %get-tuple-element.125), channel_id=1, source_target_pairs={{0,2},{1,3},{2,0},{3,1},{4,6},{5,7},{6,4},{7,5},{8,10},{9,11},{10,... | collective-permute-start | bytes 1179656 | tf_op jit(solution)/shard_map/ppermute | solution.py:33
  146.9 13.6 %collective-permute-start.23 = (bf16[128,1536]{1,0:T(8,128)(2,1)S(1)}, bf16[128,1536]{1,0:T(8,128)(2,1)S(1)}, u32[]{:S(2)}, u32[]{:S(2)}) collective-permute-start(bf16[128,1536]{1,0:T(8,128)(2,1)S(1)} %get-tuple-element.126), channel_id=1, source_target_pairs={{0,3},{1,2},{2,1},{3,0},{4,7},{5,6},{6,5},{7,4},{8,11},{9,10},{10,... | collective-permute-start | bytes 1179656 | tf_op jit(solution)/shard_map/ppermute | solution.py:33
  160.8 21.2 %collective-permute-start.27 = (bf16[128,1536]{1,0:T(8,128)(2,1)S(1)}, bf16[128,1536]{1,0:T(8,128)(2,1)S(1)}, u32[]{:S(2)}, u32[]{:S(2)}) collective-permute-start(bf16[128,1536]{1,0:T(8,128)(2,1)S(1)} %add_convert_fusion.refs_4_), channel_id=1, source_target_pairs={{0,8},{8,16},{16,24},{1,9},{9,17},{17,25},{2,10},{10,18},{18,26},{... | collective-permute-start | bytes 1179656 | tf_op jit(solution)/shard_map/ppermute | solution.py:47
  169.1 12.9 %collective-permute-start.28 = (bf16[128,1536]{1,0:T(8,128)(2,1)S(1)}, bf16[128,1536]{1,0:T(8,128)(2,1)}, u32[]{:S(2)}, u32[]{:S(2)}) collective-permute-start(bf16[128,1536]{1,0:T(8,128)(2,1)S(1)} %add_convert_fusion.refs_4_), channel_id=1, source_target_pairs={{24,16},{16,8},{8,0},{25,17},{17,9},{9,1},{26,18},{18,10},{10,2},{... | collective-permute-start | bytes 1179656 | tf_op jit(solution)/shard_map/ppermute | solution.py:48
  178.5 20.9 %collective-permute-start.26 = (bf16[128,1536]{1,0:T(8,128)(2,1)}, bf16[128,1536]{1,0:T(8,128)(2,1)S(1)}, u32[]{:S(2)}, u32[]{:S(2)}) collective-permute-start(bf16[128,1536]{1,0:T(8,128)(2,1)} %get-tuple-element.131), channel_id=1, source_target_pairs={{0,3},{1,2},{2,1},{3,0},{4,7},{5,6},{6,5},{7,4},{8,11},{9,10},{10,... | collective-permute-start | bytes 1179656 | tf_op jit(solution)/shard_map/ppermute | solution.py:33
  180.0 19.4 %collective-permute-start.25 = (bf16[128,1536]{1,0:T(8,128)(2,1)}, bf16[128,1536]{1,0:T(8,128)(2,1)S(1)}, u32[]{:S(2)}, u32[]{:S(2)}) collective-permute-start(bf16[128,1536]{1,0:T(8,128)(2,1)} %get-tuple-element.129), channel_id=1, source_target_pairs={{0,2},{1,3},{2,0},{3,1},{4,6},{5,7},{6,4},{7,5},{8,10},{9,11},{10,... | collective-permute-start | bytes 1179656 | tf_op jit(solution)/shard_map/ppermute | solution.py:33
  181.2 18.2 %collective-permute-start.24 = (bf16[128,1536]{1,0:T(8,128)(2,1)}, bf16[128,1536]{1,0:T(8,128)(2,1)S(1)}, u32[]{:S(2)}, u32[]{:S(2)}) collective-permute-start(bf16[128,1536]{1,0:T(8,128)(2,1)} %get-tuple-element.127), channel_id=1, source_target_pairs={{0,1},{1,0},{2,3},{3,2},{4,5},{5,4},{6,7},{7,6},{8,9},{9,8},{10,11... | collective-permute-start | bytes 1179656 | tf_op jit(solution)/shard_map/ppermute | solution.py:33
  182.7 14.7 %collective-permute-start.30 = (bf16[128,1536]{1,0:T(8,128)(2,1)}, bf16[128,1536]{1,0:T(8,128)(2,1)S(1)}, u32[]{:S(2)}, u32[]{:S(2)}) collective-permute-start(bf16[128,1536]{1,0:T(8,128)(2,1)} %collective-permute-done.28.refs_5_), channel_id=1, source_target_pairs={{16,8},{8,0},{17,9},{9,1},{18,10},{10,2},{19,11},{11,3},{20,12},{1... | collective-permute-start | bytes 1179656 | tf_op jit(solution)/shard_map/ppermute | solution.py:48
  216.3 13.7 %collective-permute-start.34 = (bf16[128,1536]{1,0:T(8,128)(2,1)S(1)}, bf16[128,1536]{1,0:T(8,128)(2,1)}, u32[]{:S(2)}, u32[]{:S(2)}) collective-permute-start(bf16[128,1536]{1,0:T(8,128)(2,1)S(1)} %add_convert_fusion.1.refs_4_), channel_id=1, source_target_pairs={{24,16},{16,8},{8,0},{25,17},{17,9},{9,1},{26,18},{18,10},{10,2},{... | collective-permute-start | bytes 1179656 | tf_op jit(solution)/shard_map/ppermute | solution.py:48
  217.6 15.9 %collective-permute-start.39 = (bf16[48,6144]{1,0:T(8,128)(2,1)}, bf16[48,6144]{1,0:T(8,128)(2,1)S(1)}, u32[]{:S(2)}, u32[]{:S(2)}) collective-permute-start(bf16[48,6144]{1,0:T(8,128)(2,1)} %get-tuple-element.139), channel_id=1, source_target_pairs={{0,1},{1,0},{2,3},{3,2},{4,5},{5,4},{6,7},{7,6},{8,9},{9,8},{10,11... | collective-permute-start | bytes 1769480 | tf_op jit(solution)/shard_map/ppermute | solution.py:33
  218.7 15.7 %collective-permute-start.40 = (bf16[48,6144]{1,0:T(8,128)(2,1)}, bf16[48,6144]{1,0:T(8,128)(2,1)S(1)}, u32[]{:S(2)}, u32[]{:S(2)}) collective-permute-start(bf16[48,6144]{1,0:T(8,128)(2,1)} %get-tuple-element.140), channel_id=1, source_target_pairs={{0,2},{1,3},{2,0},{3,1},{4,6},{5,7},{6,4},{7,5},{8,10},{9,11},{10,... | collective-permute-start | bytes 1769480 | tf_op jit(solution)/shard_map/ppermute | solution.py:33
  220.4 24.6 %collective-permute-start.41 = (bf16[48,6144]{1,0:T(8,128)(2,1)}, bf16[48,6144]{1,0:T(8,128)(2,1)}, u32[]{:S(2)}, u32[]{:S(2)}) collective-permute-start(bf16[48,6144]{1,0:T(8,128)(2,1)} %get-tuple-element.141), channel_id=1, source_target_pairs={{0,3},{1,2},{2,1},{3,0},{4,7},{5,6},{6,5},{7,4},{8,11},{9,10},{10,... | collective-permute-start | bytes 1769480 | tf_op jit(solution)/shard_map/ppermute | solution.py:33
  230.0 18.4 %collective-permute-start.35 = (bf16[128,1536]{1,0:T(8,128)(2,1)}, bf16[128,1536]{1,0:T(8,128)(2,1)}, u32[]{:S(2)}, u32[]{:S(2)}) collective-permute-start(bf16[128,1536]{1,0:T(8,128)(2,1)} %collective-permute-done.33.refs_3_), channel_id=1, source_target_pairs={{8,16},{16,24},{9,17},{17,25},{10,18},{18,26},{11,19},{19,27},{12,... | collective-permute-start | bytes 1179656 | tf_op jit(solution)/shard_map/ppermute | solution.py:47
  231.4 17.0 %collective-permute-start.36 = (bf16[128,1536]{1,0:T(8,128)(2,1)}, bf16[128,1536]{1,0:T(8,128)(2,1)}, u32[]{:S(2)}, u32[]{:S(2)}) collective-permute-start(bf16[128,1536]{1,0:T(8,128)(2,1)} %collective-permute-done.34.refs_5_), channel_id=1, source_target_pairs={{16,8},{8,0},{17,9},{9,1},{18,10},{10,2},{19,11},{11,3},{20,12},{1... | collective-permute-start | bytes 1179656 | tf_op jit(solution)/shard_map/ppermute | solution.py:48
  245.0 33.7 %collective-permute-start.44 = (bf16[48,6144]{1,0:T(8,128)(2,1)}, bf16[48,6144]{1,0:T(8,128)(2,1)S(1)}, u32[]{:S(2)}, u32[]{:S(2)}) collective-permute-start(bf16[48,6144]{1,0:T(8,128)(2,1)} %copy-done.24), channel_id=1, source_target_pairs={{0,1},{1,0},{2,3},{3,2},{4,5},{5,4},{6,7},{7,6},{8,9},{9,8},{10,11... | collective-permute-start | bytes 1769480 | tf_op jit(solution)/shard_map/ppermute | solution.py:33
  245.0 33.7 %collective-permute-start.45 = (bf16[48,6144]{1,0:T(8,128)(2,1)}, bf16[48,6144]{1,0:T(8,128)(2,1)}, u32[]{:S(2)}, u32[]{:S(2)}) collective-permute-start(bf16[48,6144]{1,0:T(8,128)(2,1)} %copy-done.23), channel_id=1, source_target_pairs={{0,2},{1,3},{2,0},{3,1},{4,6},{5,7},{6,4},{7,5},{8,10},{9,11},{10,... | collective-permute-start | bytes 1769480 | tf_op jit(solution)/shard_map/ppermute | solution.py:33
  247.2 31.5 %collective-permute-start.46 = (bf16[48,6144]{1,0:T(8,128)(2,1)}, bf16[48,6144]{1,0:T(8,128)(2,1)}, u32[]{:S(2)}, u32[]{:S(2)}) collective-permute-start(bf16[48,6144]{1,0:T(8,128)(2,1)} %copy-done.22), channel_id=1, source_target_pairs={{0,3},{1,2},{2,1},{3,0},{4,7},{5,6},{6,5},{7,4},{8,11},{9,10},{10,... | collective-permute-start | bytes 1769480 | tf_op jit(solution)/shard_map/ppermute | solution.py:33
  248.4 19.9 %collective-permute-start.37 = (bf16[128,1536]{1,0:T(8,128)(2,1)}, bf16[128,1536]{1,0:T(8,128)(2,1)S(1)}, u32[]{:S(2)}, u32[]{:S(2)}) collective-permute-start(bf16[128,1536]{1,0:T(8,128)(2,1)} %collective-permute-done.35.refs_2_), channel_id=1, source_target_pairs={{16,24},{17,25},{18,26},{19,27},{20,28},{21,29},{22,30},{23,31}} | collective-permute-start | bytes 1179656 | tf_op jit(solution)/shard_map/ppermute | solution.py:47
  249.1 24.5 %collective-permute-start.38 = (bf16[128,1536]{1,0:T(8,128)(2,1)}, bf16[128,1536]{1,0:T(8,128)(2,1)}, u32[]{:S(2)}, u32[]{:S(2)}) collective-permute-start(bf16[128,1536]{1,0:T(8,128)(2,1)} %collective-permute-done.36.refs_6_), channel_id=1, source_target_pairs={{8,0},{9,1},{10,2},{11,3},{12,4},{13,5},{14,6},{15,7}} | collective-permute-start | bytes 1179656 | tf_op jit(solution)/shard_map/ppermute | solution.py:48
  268.4 13.9 %collective-permute-start.42 = (bf16[192,1152]{1,0:T(8,128)(2,1)S(1)}, bf16[192,1152]{1,0:T(8,128)(2,1)S(1)}, u32[]{:S(2)}, u32[]{:S(2)}) collective-permute-start(bf16[192,1152]{1,0:T(8,128)(2,1)S(1)} %gate_up.3.refs_4_), channel_id=1, source_target_pairs={{0,8},{8,16},{16,24},{1,9},{9,17},{17,25},{2,10},{10,18},{18,26},{... | collective-permute-start | bytes 1327112 | tf_op jit(solution)/shard_map/ppermute | solution.py:47
  278.7 39.6 %collective-permute-start.51 = (bf16[96,6144]{1,0:T(8,128)(2,1)S(1)}, bf16[96,6144]{1,0:T(8,128)(2,1)S(1)}, u32[]{:S(2)}, u32[]{:S(2)}) collective-permute-start(bf16[96,6144]{1,0:T(8,128)(2,1)S(1)} %get-tuple-element.170), channel_id=1, source_target_pairs={{0,1},{1,0},{2,3},{3,2},{4,5},{5,4},{6,7},{7,6},{8,9},{9,8},{10,11... | collective-permute-start | bytes 3538952 | tf_op jit(solution)/shard_map/ppermute | solution.py:33
  279.1 39.2 %collective-permute-start.52 = (bf16[96,6144]{1,0:T(8,128)(2,1)S(1)}, bf16[96,6144]{1,0:T(8,128)(2,1)S(1)}, u32[]{:S(2)}, u32[]{:S(2)}) collective-permute-start(bf16[96,6144]{1,0:T(8,128)(2,1)S(1)} %get-tuple-element.173), channel_id=1, source_target_pairs={{0,2},{1,3},{2,0},{3,1},{4,6},{5,7},{6,4},{7,5},{8,10},{9,11},{10,... | collective-permute-start | bytes 3538952 | tf_op jit(solution)/shard_map/ppermute | solution.py:33
  281.0 37.3 %collective-permute-start.53 = (bf16[96,6144]{1,0:T(8,128)(2,1)S(1)}, bf16[96,6144]{1,0:T(8,128)(2,1)S(1)}, u32[]{:S(2)}, u32[]{:S(2)}) collective-permute-start(bf16[96,6144]{1,0:T(8,128)(2,1)S(1)} %get-tuple-element.176), channel_id=1, source_target_pairs={{0,3},{1,2},{2,1},{3,0},{4,7},{5,6},{6,5},{7,4},{8,11},{9,10},{10,... | collective-permute-start | bytes 3538952 | tf_op jit(solution)/shard_map/ppermute | solution.py:33
  283.8 18.6 %collective-permute-start.47 = (bf16[192,1152]{1,0:T(8,128)(2,1)S(1)}, bf16[192,1152]{1,0:T(8,128)(2,1)}, u32[]{:S(2)}, u32[]{:S(2)}) collective-permute-start(bf16[192,1152]{1,0:T(8,128)(2,1)S(1)} %collective-permute-done.42.refs_3_), channel_id=1, source_target_pairs={{8,16},{16,24},{9,17},{17,25},{10,18},{18,26},{11,19},{19,27},{12,... | collective-permute-start | bytes 1327112 | tf_op jit(solution)/shard_map/ppermute | solution.py:47
  285.3 17.2 %collective-permute-start.48 = (bf16[192,1152]{1,0:T(8,128)(2,1)S(1)}, bf16[192,1152]{1,0:T(8,128)(2,1)}, u32[]{:S(2)}, u32[]{:S(2)}) collective-permute-start(bf16[192,1152]{1,0:T(8,128)(2,1)S(1)} %collective-permute-done.43.refs_5_), channel_id=1, source_target_pairs={{16,8},{8,0},{17,9},{9,1},{18,10},{10,2},{19,11},{11,3},{20,12},{1... | collective-permute-start | bytes 1327112 | tf_op jit(solution)/shard_map/ppermute | solution.py:48
  302.5 10.6 %collective-permute-start.49 = (bf16[192,1152]{1,0:T(8,128)(2,1)S(1)}, bf16[192,1152]{1,0:T(8,128)(2,1)S(1)}, u32[]{:S(2)}, u32[]{:S(2)}) collective-permute-start(bf16[192,1152]{1,0:T(8,128)(2,1)S(1)} %gate_up.4.refs_4_), channel_id=1, source_target_pairs={{0,8},{8,16},{16,24},{1,9},{9,17},{17,25},{2,10},{10,18},{18,26},{... | collective-permute-start | bytes 1327112 | tf_op jit(solution)/shard_map/ppermute | solution.py:47
  307.3 10.9 %collective-permute-start.50 = (bf16[192,1152]{1,0:T(8,128)(2,1)S(1)}, bf16[192,1152]{1,0:T(8,128)(2,1)S(1)}, u32[]{:S(2)}, u32[]{:S(2)}) collective-permute-start(bf16[192,1152]{1,0:T(8,128)(2,1)S(1)} %gate_up.4.refs_4_), channel_id=1, source_target_pairs={{24,16},{16,8},{8,0},{25,17},{17,9},{9,1},{26,18},{18,10},{10,2},{... | collective-permute-start | bytes 1327112 | tf_op jit(solution)/shard_map/ppermute | solution.py:48
  318.3 19.7 %collective-permute-start.54 = (bf16[192,1152]{1,0:T(8,128)(2,1)S(1)}, bf16[192,1152]{1,0:T(8,128)(2,1)}, u32[]{:S(2)}, u32[]{:S(2)}) collective-permute-start(bf16[192,1152]{1,0:T(8,128)(2,1)S(1)} %collective-permute-done.49.refs_3_), channel_id=1, source_target_pairs={{8,16},{16,24},{9,17},{17,25},{10,18},{18,26},{11,19},{19,27},{12,... | collective-permute-start | bytes 1327112 | tf_op jit(solution)/shard_map/ppermute | solution.py:47
  319.7 18.3 %collective-permute-start.55 = (bf16[192,1152]{1,0:T(8,128)(2,1)S(1)}, bf16[192,1152]{1,0:T(8,128)(2,1)}, u32[]{:S(2)}, u32[]{:S(2)}) collective-permute-start(bf16[192,1152]{1,0:T(8,128)(2,1)S(1)} %collective-permute-done.50.refs_5_), channel_id=1, source_target_pairs={{16,8},{8,0},{17,9},{9,1},{18,10},{10,2},{19,11},{11,3},{20,12},{1... | collective-permute-start | bytes 1327112 | tf_op jit(solution)/shard_map/ppermute | solution.py:48
  338.0 16.4 %collective-permute-start.56 = (bf16[384,1152]{1,0:T(8,128)(2,1)S(1)}, bf16[384,1152]{1,0:T(8,128)(2,1)S(1)}, u32[]{:S(2)}, u32[]{:S(2)}) collective-permute-start(bf16[384,1152]{1,0:T(8,128)(2,1)S(1)} %gate_up.5.refs_4_), channel_id=1, source_target_pairs={{0,8},{8,16},{16,24},{1,9},{9,17},{17,25},{2,10},{10,18},{18,26},{... | collective-permute-start | bytes 2654216 | tf_op jit(solution)/shard_map/ppermute | solution.py:47
  343.9 23.0 %collective-permute-start.57 = (bf16[384,1152]{1,0:T(8,128)(2,1)S(1)}, bf16[384,1152]{1,0:T(8,128)(2,1)}, u32[]{:S(2)}, u32[]{:S(2)}) collective-permute-start(bf16[384,1152]{1,0:T(8,128)(2,1)S(1)} %gate_up.5.refs_4_), channel_id=1, source_target_pairs={{24,16},{16,8},{8,0},{25,17},{17,9},{9,1},{26,18},{18,10},{10,2},{... | collective-permute-start | bytes 2654216 | tf_op jit(solution)/shard_map/ppermute | solution.py:48
  346.9 23.6 %collective-permute-start.65 = (bf16[192,1152]{1,0:T(8,128)(2,1)}, bf16[192,1152]{1,0:T(8,128)(2,1)S(1)}, u32[]{:S(2)}, u32[]{:S(2)}) collective-permute-start(bf16[192,1152]{1,0:T(8,128)(2,1)} %collective-permute-done.47.refs_2_), channel_id=1, source_target_pairs={{16,24},{17,25},{18,26},{19,27},{20,28},{21,29},{22,30},{23,31}} | collective-permute-start | bytes 1327112 | tf_op jit(solution)/shard_map/ppermute | solution.py:47
  347.6 24.7 %collective-permute-start.66 = (bf16[192,1152]{1,0:T(8,128)(2,1)}, bf16[192,1152]{1,0:T(8,128)(2,1)S(1)}, u32[]{:S(2)}, u32[]{:S(2)}) collective-permute-start(bf16[192,1152]{1,0:T(8,128)(2,1)} %collective-permute-done.48.refs_6_), channel_id=1, source_target_pairs={{8,0},{9,1},{10,2},{11,3},{12,4},{13,5},{14,6},{15,7}} | collective-permute-start | bytes 1327112 | tf_op jit(solution)/shard_map/ppermute | solution.py:48
  366.9 25.6 %collective-permute-start.58 = (bf16[384,1152]{1,0:T(8,128)(2,1)S(1)}, bf16[384,1152]{1,0:T(8,128)(2,1)}, u32[]{:S(2)}, u32[]{:S(2)}) collective-permute-start(bf16[384,1152]{1,0:T(8,128)(2,1)S(1)} %collective-permute-done.56.refs_3_), channel_id=1, source_target_pairs={{8,16},{16,24},{9,17},{17,25},{10,18},{18,26},{11,19},{19,27},{12,... | collective-permute-start | bytes 2654216 | tf_op jit(solution)/shard_map/ppermute | solution.py:47
  368.5 25.2 %collective-permute-start.59 = (bf16[384,1152]{1,0:T(8,128)(2,1)}, bf16[384,1152]{1,0:T(8,128)(2,1)}, u32[]{:S(2)}, u32[]{:S(2)}) collective-permute-start(bf16[384,1152]{1,0:T(8,128)(2,1)} %collective-permute-done.57.refs_5_), channel_id=1, source_target_pairs={{16,8},{8,0},{17,9},{9,1},{18,10},{10,2},{19,11},{11,3},{20,12},{1... | collective-permute-start | bytes 2654216 | tf_op jit(solution)/shard_map/ppermute | solution.py:48
  393.7 10.4 %collective-permute-start.71 = (bf16[192,1152]{1,0:T(8,128)(2,1)}, bf16[192,1152]{1,0:T(8,128)(2,1)S(1)}, u32[]{:S(2)}, u32[]{:S(2)}) collective-permute-start(bf16[192,1152]{1,0:T(8,128)(2,1)} %collective-permute-done.55.refs_6_), channel_id=1, source_target_pairs={{8,0},{9,1},{10,2},{11,3},{12,4},{13,5},{14,6},{15,7}} | collective-permute-start | bytes 1327112 | tf_op jit(solution)/shard_map/ppermute | solution.py:48
  395.0 19.9 %collective-permute-start.60 = (bf16[384,1152]{1,0:T(8,128)(2,1)}, bf16[384,1152]{1,0:T(8,128)(2,1)S(1)}, u32[]{:S(2)}, u32[]{:S(2)}) collective-permute-start(bf16[384,1152]{1,0:T(8,128)(2,1)} %collective-permute-done.58.refs_2_), channel_id=1, source_target_pairs={{16,24},{17,25},{18,26},{19,27},{20,28},{21,29},{22,30},{23,31}} | collective-permute-start | bytes 2654216 | tf_op jit(solution)/shard_map/ppermute | solution.py:47
  395.7 19.1 %collective-permute-start.61 = (bf16[384,1152]{1,0:T(8,128)(2,1)}, bf16[384,1152]{1,0:T(8,128)(2,1)S(1)}, u32[]{:S(2)}, u32[]{:S(2)}) collective-permute-start(bf16[384,1152]{1,0:T(8,128)(2,1)} %collective-permute-done.59.refs_6_), channel_id=1, source_target_pairs={{8,0},{9,1},{10,2},{11,3},{12,4},{13,5},{14,6},{15,7}} | collective-permute-start | bytes 2654216 | tf_op jit(solution)/shard_map/ppermute | solution.py:48
  411.3 14.7 %collective-permute-start.74 = (bf16[48,1536]{1,0:T(8,128)(2,1)S(1)}, bf16[48,1536]{1,0:T(8,128)(2,1)S(1)}, u32[]{:S(2)}, u32[]{:S(2)}) collective-permute-start(bf16[48,1536]{1,0:T(8,128)(2,1)S(1)} %get-tuple-element.216), channel_id=1, source_target_pairs={{0,3},{1,2},{2,1},{3,0},{4,7},{5,6},{6,5},{7,4},{8,11},{9,10},{10,... | collective-permute-start | bytes 442376 | tf_op jit(solution)/shard_map/ppermute | solution.py:33
  413.0 14.8 %collective-permute-start.73 = (bf16[48,1536]{1,0:T(8,128)(2,1)S(1)}, bf16[48,1536]{1,0:T(8,128)(2,1)S(1)}, u32[]{:S(2)}, u32[]{:S(2)}) collective-permute-start(bf16[48,1536]{1,0:T(8,128)(2,1)S(1)} %get-tuple-element.215), channel_id=1, source_target_pairs={{0,2},{1,3},{2,0},{3,1},{4,6},{5,7},{6,4},{7,5},{8,10},{9,11},{10,... | collective-permute-start | bytes 442376 | tf_op jit(solution)/shard_map/ppermute | solution.py:33
  413.1 14.6 %collective-permute-start.72 = (bf16[48,1536]{1,0:T(8,128)(2,1)S(1)}, bf16[48,1536]{1,0:T(8,128)(2,1)S(1)}, u32[]{:S(2)}, u32[]{:S(2)}) collective-permute-start(bf16[48,1536]{1,0:T(8,128)(2,1)S(1)} %get-tuple-element.214), channel_id=1, source_target_pairs={{0,1},{1,0},{2,3},{3,2},{4,5},{5,4},{6,7},{7,6},{8,9},{9,8},{10,11... | collective-permute-start | bytes 442376 | tf_op jit(solution)/shard_map/ppermute | solution.py:33
  437.8 10.4 %collective-permute-start.76 = (bf16[64,1536]{1,0:T(8,128)(2,1)S(1)}, bf16[64,1536]{1,0:T(8,128)(2,1)S(1)}, u32[]{:S(2)}, u32[]{:S(2)}) collective-permute-start(bf16[64,1536]{1,0:T(8,128)(2,1)S(1)} %get-tuple-element.229), channel_id=1, source_target_pairs={{0,16},{8,24},{16,0},{24,8},{1,17},{9,25},{17,1},{25,9},{2,18},{10... | collective-permute-start | bytes 589832 | tf_op jit(solution)/shard_map/ppermute | solution.py:28
  437.8 10.4 %collective-permute-start.75 = (bf16[64,1536]{1,0:T(8,128)(2,1)S(1)}, bf16[64,1536]{1,0:T(8,128)(2,1)S(1)}, u32[]{:S(2)}, u32[]{:S(2)}) collective-permute-start(bf16[64,1536]{1,0:T(8,128)(2,1)S(1)} %get-tuple-element.230), channel_id=1, source_target_pairs={{0,8},{8,16},{16,24},{24,0},{1,9},{9,17},{17,25},{25,1},{2,10},{10... | collective-permute-start | bytes 589832 | tf_op jit(solution)/shard_map/ppermute | solution.py:28
  (60 other events, 585.0 us)
Sparse Core Ops, SparseCore 0:
  8.9 19.4 all-gather.9
  29.9 27.9 all-gather.11
  59.5 27.2 all-gather.13
  88.2 27.5 all-gather.7
where the time goes:
time: 465 us; the launch traced here: 456 us
  waiting for transfers between devices  166 us (36%)
  starting transfers between devices  132 us (28%)
  Pallas kernels  93.3 us (20%)
  local copies, waits for them, and re-layouts  27.2 us (6%)
  matrix products  14.7 us (3%)
  between operations  14.7 us (3%)
  other arithmetic  8.1 us (2%)
    ppermute x18, waiting for transfers between devices, line_gather(): lax.ppermute(leftward, 'z', [(n - 1 - i, n - 1 - j) for i, j in onward])  79.4 us
    pallas_call x3, Pallas kernels, gate_up_call(): pl.pallas_call(lambda *refs: gate_up_kernel(len(pieces), tiles, *refs), n...  48.1 us
    ppermute x18, starting transfers between devices, line_gather(): right.append(lax.ppermute(rightward, 'z', onward))  47.5 us
    ppermute x15, starting transfers between devices, shift_z(): return lax.ppermute(x, 'z', perm)  31.9 us
    ppermute x18, waiting for transfers between devices, line_gather(): right.append(lax.ppermute(rightward, 'z', onward))  31.3 us
    ppermute x24, starting transfers between devices, to_expert(): return lax.ppermute(x, 'expert', [(i, i ^ k) for i in range(n)])  28.8 us
    ppermute x24, waiting for transfers between devices, to_expert(): return lax.ppermute(x, 'expert', [(i, i ^ k) for i in range(n)])  27.8 us
    pallas_call x3, Pallas kernels, down_call(): pl.pallas_call(lambda *refs: down_kernel(n, count, *refs), name='down', o...  24.5 us
  transfers between devices with their start and end apart: 82, of which 25 were waited for; matrix products, arithmetic and copies ran while one was open for 7% of the time, Pallas kernels for 20%

commit v1 on v0

--- a/solution.py
+++ b/solution.py
@@ -38,15 +38,25 @@
     return jnp.where(first, own, other), jnp.where(first, other, own)
 
 
-def line_gather(x):
+def line_gather(x, pending=(), work=None):
     n = lax.axis_size("z")
-    right, left = [x], [x]
+    right, left, made = [x], [x], []
     for step in range(n - 1):
         onward = [(i, i + 1) for i in range(step, n - 1)]
-        rightward, leftward = lax.optimization_barrier((right[-1], left[-1]))
-        right.append(lax.ppermute(rightward, "z", onward))
-        left.append(lax.ppermute(leftward, "z", [(n - 1 - i, n - 1 - j) for i, j in onward]))
-    return right[:0:-1] + left
+        held = (right[-1], left[-1])
+        if made and len(made) == step:
+            held, made[-1] = lax.optimization_barrier((held, made[-1]))
+        elif step:
+            held = lax.optimization_barrier(held)
+        now = None
+        if step < len(pending):
+            held, now = lax.optimization_barrier((held, pending[step]))
+        right.append(lax.ppermute(held[0], "z", onward))
+        left.append(lax.ppermute(held[1], "z", [(n - 1 - i, n - 1 - j) for i, j in onward]))
+        if now is not None:
+            made.append(work(now))
+    made += [work(x) for x in pending[n - 1 :]]
+    return right[:0:-1] + left, made
 
 
 def copy_shard(z, n, s, pieces, rows, target, sem, skipped=0):
@@ -303,7 +313,7 @@
     )
 
 
-def attention(queries, keys, values, decay_rate, start_state, first):
+def attention(queries, keys, values, decay_rate, start_state, named):
     core, z, n_z = lax.axis_index("core"), lax.axis_index("z"), lax.axis_size("z")
     heads, head_dim = start_state.shape[:2]
     length = queries.shape[0]
@@ -318,8 +328,13 @@
     local = jnp.einsum(
         "shd,she->hde", scaled_keys, values.astype(F32), precision=lax.Precision.HIGHEST
     )
-    other_total, other_local = swap_core(total), swap_core(local.astype(BF)).astype(F32)
-    total0, total1 = by_core(core, total, other_total)
+    tall = named.shape[1]
+    note = jnp.concatenate([named, total.reshape(-1, tall)], axis=0)
+    notes = jnp.stack([note] + [shift_z(note, k, True) for k in range(1, n_z)])
+    named, totals = notes[:, : named.shape[0]], notes[:, named.shape[0] :].reshape(n_z, heads)
+    other_local = swap_core(local.astype(BF)).astype(F32)
+    totals0, totals1 = by_core(core, totals, swap_core(totals))
+    total0, total1 = totals0[0], totals1[0]
     half = heads // 2
 
     def mine(x):
@@ -327,11 +342,11 @@
 
     own_half, other_half = mine(local), mine(other_local)
     local0, local1 = by_core(core, own_half, other_half)
-    chip_total = total0 + total1
     chip_state = (jnp.exp(-mine(total1))[:, None, None] * local0 + local1).astype(BF)
-    chip_state = after(chip_state, first)
     earlier_states = [shift_z(chip_state, k) for k in range(1, n_z)]
-    earlier_totals = [shift_z(chip_total, k) for k in range(1, n_z)]
+    earlier_totals = [
+        jnp.where(z >= k, totals0[k] + totals1[k], 0.0) for k in range(1, n_z)
+    ]
 
     causal = upto.T[None, :, :]
     diff = cum[:, None, :] - cum[:, :, None]
@@ -358,7 +373,7 @@
     )
     attended = intra + inter * jnp.exp(-cum).T[:, :, None]
     scale = lax.rsqrt(jnp.mean(attended * attended, axis=-1, keepdims=True) + 1e-06)
-    return (attended * scale).astype(BF).reshape(length, heads * head_dim)
+    return (attended * scale).astype(BF).reshape(length, heads * head_dim), list(named)
 
 
 def shards(
@@ -387,14 +402,18 @@
     ]
 
     named = jnp.concatenate([expert_ids.astype(F32), expert_gates], axis=1)
-    named = absolute([named[None]] + [shift_z(named[None], k, True) for k in range(1, n_z)], 0)
-    ids, gates = named[:, :, :2].astype(jnp.int32), named[:, :, 2:]
 
     def columns_of(k):
         return lax.dynamic_slice_in_dim(residual, lax.rem(z + k, n_z) * part, part, axis=1)
 
     kept = [columns_of(0)] + [shift_z(columns_of(k), k, True) for k in range(1, n_z)]
     kept = absolute(kept, 0).reshape(n_z, rows, part)
+
+    head_out, named = attention(
+        attn_queries, attn_keys, attn_values, decay_rate, start_state, named
+    )
+    named = absolute([x[None] for x in named], 0)
+    ids, gates = named[:, :, :2].astype(jnp.int32), named[:, :, 2:]
 
     partner = expert ^ jnp.arange(n_exp)
     names = ids[:, :, :, None] == partner
@@ -408,10 +427,7 @@
     chosen = names[:, :, :, :, None] & (slot[:, :, None, :, None] == places)
     chosen = chosen.astype(BF).reshape(n_z, rows, 2, n_exp * capacity)
 
-    head_out = attention(
-        attn_queries, attn_keys, attn_values, decay_rate, start_state, (named, kept)
-    )
-    acts = line_gather(head_out)
+    acts, _ = line_gather(head_out)
     gain = moe_gain.reshape(1, width)
 
     def of_block(x, block):
@@ -436,8 +452,10 @@
             picks.append(one.reshape(n_exp, len(group) * capacity, len(block) * rows))
         return route_call(n_z, pieces, gain, picks)
 
-    def combine(block, stream, hidden):
-        expert_out = down_call(n_z, n_exp, hidden, w_down)
+    def down(hidden):
+        return down_call(n_z, n_exp, hidden, w_down)
+
+    def combine(block, stream, expert_out):
         returned = [to_expert(expert_out[k], k) if k else expert_out[k] for k in range(n_exp)]
         returned = [x.reshape(len(block), capacity, part) for x in returned]
         returned = jnp.concatenate(returned, axis=1)
@@ -460,7 +478,7 @@
     for i, count in enumerate(GROUPS):
         block = middle_first[i * size : (i + 1) * size]
         stream, summed = project(block, summed)
-        full = line_gather(after(stream, full, sent))
+        full, _ = line_gather(after(stream, full, sent))
         fine = [block[j : j + size // count] for j in range(0, size, size // count)]
         sent = route(block, fine, full)
         for group, rows_for in zip(fine, sent):
@@ -469,16 +487,18 @@
             ]
             started = hidden[near]
             made = gate_up_call([after(x, started) for x in routed], (w_gate, w_up))
-            hidden = line_gather(after(made, hidden[1:-1]))
+            last = i + 1 == len(GROUPS) and group is fine[-1]
+            hidden, downs = line_gather(
+                after(made, hidden[1:-1]), waiting if last else [], down
+            )
             at = [block.index(s) * rows for s in group]
             groups.append(group)
             streams.append(jnp.stack([stream[r : r + rows] for r in at]))
             waiting.append(hidden)
+    downs.append(down(hidden))
     out = [None] * n_z
-    for i, group in enumerate(groups):
-        later = waiting[i + 1][near] if i + 1 < len(groups) else ()
-        pieces = [after(x, later) for x in waiting[i]]
-        for s, piece in zip(group, combine(group, streams[i], pieces)):
+    for group, stream, expert_out in zip(groups, streams, downs):
+        for s, piece in zip(group, combine(group, stream, expert_out)):
             out[s] = piece
     out = jnp.stack(out)
 

time: 465 us -> 458 us (0.985)
  starting transfers between devices: 132 us -> 124 us
    ppermute x15 -> x12, starting transfers between devices: 31.9 us -> 24.8 us  [shift_z(): return lax.ppermute(x, 'z', perm)]
    ppermute x15 -> x12, waiting for transfers between devices: 23.6 us -> 16.5 us  [shift_z(): return lax.ppermute(x, 'z', perm)]
    unnamed x84 -> x110, local copies, waits for them, and re-layouts: 18 us -> 16.2 us
  transfers between devices with their start and end apart: 82 -> 79, of which waited for: 25 -> 28; matrix products, arithmetic and copies ran while one was open for 7% -> 7% of each run, Pallas kernels for 20% -> 21%
where the time goes in v1:
time: 458 us; the launch traced here: 450 us
  waiting for transfers between devices  167 us (36%)
  starting transfers between devices  124 us (27%)
  Pallas kernels  94.8 us (21%)
  local copies, waits for them, and re-layouts  26.6 us (6%)
  between operations  14.8 us (3%)
  matrix products  12.5 us (3%)
  other arithmetic  10 us (2%)
    ppermute x18, waiting for transfers between devices, line_gather(): lax.ppermute(held[1], 'z', [(n - 1 - i, n - 1 - j) for i, j in onward])  95.7 us
    pallas_call x3, Pallas kernels, gate_up_call(): pl.pallas_call(lambda *refs: gate_up_kernel(len(pieces), tiles, *refs), n...  50.3 us
    ppermute x18, starting transfers between devices, line_gather(): right.append(lax.ppermute(held[0], 'z', onward))  45.8 us
    ppermute x24, waiting for transfers between devices, to_expert(): return lax.ppermute(x, 'expert', [(i, i ^ k) for i in range(n)])  31 us
    ppermute x24, starting transfers between devices, to_expert(): return lax.ppermute(x, 'expert', [(i, i ^ k) for i in range(n)])  29.6 us
    ppermute x12, starting transfers between devices, shift_z(): return lax.ppermute(x, 'z', perm)  24.8 us
    pallas_call x3, Pallas kernels, down_call(): pl.pallas_call(lambda *refs: down_kernel(n, count, *refs), name='down', o...  23.8 us
    ppermute x18, starting transfers between devices, line_gather(): lax.ppermute(held[1], 'z', [(n - 1 - i, n - 1 - j) for i, j in onward])  23.8 us
  transfers between devices with their start and end apart: 79, of which 28 were waited for; matrix products, arithmetic and copies ran while one was open for 7% of the time, Pallas kernels for 21%

profile of v1, /device:TPU:0, one launch (start us, length us, event | category | flops | bytes accessed | tf_op | source)
XLA Modules:
  0.0 449.6 jit_solution(16456261135253561668)
XLA Ops:
  10.1 5.1 %collective-permute-start.5 = (f32[68,4]{0,1:T(4,128)S(1)}, f32[68,4]{0,1:T(4,128)S(1)}, u32[]{:S(2)}, u32[]{:S(2)}) collective-permute-start(f32[68,4]{0,1:T(4,128)S(1)} %pad_maximum_fusion.15), channel_id=1, source_target_pairs={{0,24},{8,0},{16,8},{24,16},{1,25},{9,1},{17,9},{25,17},{2,26},{10... | collective-permute-start | bytes 3272 | tf_op jit(solution)/shard_map/ppermute | solution.py:28
  16.8 3.4 fusion.76
  23.8 5.2 %collective-permute-start.8 = (bf16[8,128,128]{2,1,0:T(8,128)(2,1)S(1)}, bf16[8,128,128]{2,1,0:T(8,128)(2,1)}, u32[]{:S(2)}, u32[]{:S(2)}) collective-permute-start(bf16[8,128,128]{2,1,0:T(8,128)(2,1)S(1)} %add_convert_fusion.3), channel_id=1, source_target_pairs={{0,8},{8,16},{16,24},{1,9},{9,17},{17,25},{2,10},{10,18},{18,26},{... | collective-permute-start | bytes 786440 | tf_op jit(solution)/shard_map/ppermute | solution.py:28
  29.0 2.7 collective-permute-start.9
  31.7 2.0 collective-permute-start.10
  33.7 4.3 convolution_bitcast_fusion
  38.2 2.4 collective-permute-done.9
  40.6 4.8 %collective-permute-done.10 = bf16[8,128,128]{2,1,0:T(8,128)(2,1)} collective-permute-done((bf16[8,128,128]{2,1,0:T(8,128)(2,1)S(1)}, bf16[8,128,128]{2,1,0:T(8,128)(2,1)}, u32[]{:S(2)}, u32[]{:S(2)}) %collective-permute-start.10) | collective-permute-done | bytes 262176 | tf_op jit(solution)/shard_map/ppermute | solution.py:28
  45.4 1.6 add_convert_fusion.2
  47.1 1.9 collective-permute-done.11
  49.1 2.7 multiply_reduce_fusion
  52.7 7.8 %collective-permute-start.12 = (bf16[256,2048]{1,0:T(8,128)(2,1)S(1)}, bf16[256,2048]{1,0:T(8,128)(2,1)S(1)}, u32[]{:S(2)}, u32[]{:S(2)}) collective-permute-start(bf16[256,2048]{1,0:T(8,128)(2,1)S(1)} %copy.61.refs_4_.refs_3_), channel_id=1, source_target_pairs={{0,8},{8,16},{16,24},{1,9},{9,17},{17,25},{2,10},{10,18},{18,26},{... | collective-permute-start | bytes 3145736 | tf_op jit(solution)/shard_map/ppermute | solution.py:54
  62.7 6.2 %collective-permute-start.2 = (bf16[64,1536]{1,0:T(8,128)(2,1)}, bf16[64,1536]{1,0:T(8,128)(2,1)S(1)}, u32[]{:S(2)}, u32[]{:S(2)}) collective-permute-start(bf16[64,1536]{1,0:T(8,128)(2,1)} %get-tuple-element.234), channel_id=1, source_target_pairs={{0,24},{8,0},{16,8},{24,16},{1,25},{9,1},{17,9},{25,17},{2,26},{10... | collective-permute-start | bytes 589832 | tf_op jit(solution)/shard_map/ppermute | solution.py:28
  71.0 12.9 %collective-permute-done.12.refs_3_.refs_2_ = bf16[256,2048]{1,0:T(8,128)(2,1)S(1)} collective-permute-done((bf16[256,2048]{1,0:T(8,128)(2,1)S(1)}, bf16[256,2048]{1,0:T(8,128)(2,1)S(1)}, u32[]{:S(2)}, u32[]{:S(2)}) %collective-permute-start.12) | collective-permute-done | bytes 1048608 | tf_op jit(solution)/shard_map/ppermute | solution.py:54
  83.9 4.6 %collective-permute-done.13.refs_5_.refs_4_ = bf16[256,2048]{1,0:T(8,128)(2,1)} collective-permute-done((bf16[256,2048]{1,0:T(8,128)(2,1)S(1)}, bf16[256,2048]{1,0:T(8,128)(2,1)}, u32[]{:S(2)}, u32[]{:S(2)}) %collective-permute-start.13) | collective-permute-done | bytes 1048608 | tf_op jit(solution)/shard_map/ppermute | solution.py:55
  88.5 1.6 collective-permute-start.14
  92.4 34.5 %collective-permute-done.15.refs_6_.refs_5_ = bf16[256,2048]{1,0:T(8,128)(2,1)} collective-permute-done((bf16[256,2048]{1,0:T(8,128)(2,1)}, bf16[256,2048]{1,0:T(8,128)(2,1)}, u32[]{:S(2)}, u32[]{:S(2)}) %collective-permute-start.15) | collective-permute-done | bytes 1048608 | tf_op jit(solution)/shard_map/ppermute | solution.py:55
  126.9 1.6 collective-permute-start.16
  129.8 2.8 copy-done.2
  132.6 6.5 %project.3 = (bf16[128,1536]{1,0:T(8,128)(2,1)S(1)}, bf16[128,1536]{1,0:T(8,128)(2,1)S(1)}, bf16[128,1536]{1,0:T(8,128)(2,1)S(1)}, bf16[128,1536]{1,0:T(8,128)(2,1)S(1)}) custom-call(s32[3]{0:T(128)S(1)} %pad_add_fusion.refs_0_, bf16[256,2048]{1,0:T(8,128)(2,1)} %collective-permute-done.14.refs_2_.refs_1_, ...), custom_call_target="tpu_custom_call" | custom-call | flops 3221225472 | bytes 12582912 | tf_op jit(solution)/shard_map/project/pallas_call | solution.py:117
  139.2 1.5 collective-permute-start.18
  140.7 1.5 collective-permute-start.19
  144.6 6.7 %collective-permute-done.18 = bf16[128,1536]{1,0:T(8,128)(2,1)S(1)} collective-permute-done((bf16[128,1536]{1,0:T(8,128)(2,1)S(1)}, bf16[128,1536]{1,0:T(8,128)(2,1)S(1)}, u32[]{:S(2)}, u32[]{:S(2)}) %collective-permute-start.18) | collective-permute-done | bytes 393248 | tf_op jit(solution)/shard_map/ppermute | solution.py:33
  151.3 7.2 %collective-permute-done.19 = bf16[128,1536]{1,0:T(8,128)(2,1)S(1)} collective-permute-done((bf16[128,1536]{1,0:T(8,128)(2,1)S(1)}, bf16[128,1536]{1,0:T(8,128)(2,1)S(1)}, u32[]{:S(2)}, u32[]{:S(2)}) %collective-permute-start.19) | collective-permute-done | bytes 393248 | tf_op jit(solution)/shard_map/ppermute | solution.py:33
  158.8 5.2 %collective-permute-start.24 = (bf16[128,1536]{1,0:T(8,128)(2,1)S(1)}, bf16[128,1536]{1,0:T(8,128)(2,1)S(1)}, u32[]{:S(2)}, u32[]{:S(2)}) collective-permute-start(bf16[128,1536]{1,0:T(8,128)(2,1)S(1)} %add_convert_fusion.refs_4_), channel_id=1, source_target_pairs={{0,8},{8,16},{16,24},{1,9},{9,17},{17,25},{2,10},{10,18},{18,26},{... | collective-permute-start | bytes 1179656 | tf_op jit(solution)/shard_map/ppermute | solution.py:54
  165.4 6.6 %project.2 = (bf16[128,1536]{1,0:T(8,128)(2,1)S(1)}, bf16[128,1536]{1,0:T(8,128)(2,1)}, bf16[128,1536]{1,0:T(8,128)(2,1)}, bf16[128,1536]{1,0:T(8,128)(2,1)}) custom-call(s32[3]{0:T(128)S(1)} %pad_add_fusion.refs_0_, bf16[256,2048]{1,0:T(8,128)(2,1)} %collective-permute-done.16.refs_1_, bf16[256,2048]{1,0:T(8,128)(2,1)} %collective-permute-done.14.refs_2_.refs_1_, ...), custom_call_target="tpu_custom_call" | custom-call | flops 3221225472 | bytes 12582912 | tf_op jit(solution)/shard_map/project/pallas_call | solution.py:117
  172.7 1.5 collective-permute-start.23
  179.5 9.4 %collective-permute-done.27.refs_6_ = bf16[128,1536]{1,0:T(8,128)(2,1)S(1)} collective-permute-done((bf16[128,1536]{1,0:T(8,128)(2,1)}, bf16[128,1536]{1,0:T(8,128)(2,1)S(1)}, u32[]{:S(2)}, u32[]{:S(2)}) %collective-permute-start.27) | collective-permute-done | bytes 393248 | tf_op jit(solution)/shard_map/ppermute | solution.py:55
  192.3 7.0 %collective-permute-done.29.refs_7_ = bf16[128,1536]{1,0:T(8,128)(2,1)S(1)} collective-permute-done((bf16[128,1536]{1,0:T(8,128)(2,1)S(1)}, bf16[128,1536]{1,0:T(8,128)(2,1)S(1)}, u32[]{:S(2)}, u32[]{:S(2)}) %collective-permute-start.29) | collective-permute-done | bytes 393248 | tf_op jit(solution)/shard_map/ppermute | solution.py:55
  199.3 3.9 route.2
  204.0 2.3 collective-permute-start.30
  209.6 1.4 collective-permute-start.38
  211.1 4.9 %collective-permute-done.31.refs_5_ = bf16[128,1536]{1,0:T(8,128)(2,1)} collective-permute-done((bf16[128,1536]{1,0:T(8,128)(2,1)S(1)}, bf16[128,1536]{1,0:T(8,128)(2,1)}, u32[]{:S(2)}, u32[]{:S(2)}) %collective-permute-start.31) | collective-permute-done | bytes 393248 | tf_op jit(solution)/shard_map/ppermute | solution.py:55
  217.4 1.5 collective-permute-start.33
  220.9 3.2 collective-permute-done.36.refs_1_
  224.9 6.5 %collective-permute-done.37.refs_2_ = bf16[48,6144]{1,0:T(8,128)(2,1)S(1)} collective-permute-done((bf16[48,6144]{1,0:T(8,128)(2,1)}, bf16[48,6144]{1,0:T(8,128)(2,1)S(1)}, u32[]{:S(2)}, u32[]{:S(2)}) %collective-permute-start.37) | collective-permute-done | bytes 589856 | tf_op jit(solution)/shard_map/ppermute | solution.py:33
  232.3 3.1 collective-permute-start.41
  235.7 1.5 collective-permute-start.43
  241.3 15.8 %gate_up.3.refs_4_ = bf16[192,1152]{1,0:T(8,128)(2,1)S(1)} custom-call(bf16[48,6144]{1,0:T(8,128)(2,1)S(1)} %get-tuple-element.132.refs_0_, bf16[48,6144]{1,0:T(8,128)(2,1)S(1)} %copy-done.5, bf16[48,6144]{1,0:T(8,128)(2,1)S(1)} %copy-done.7, bf16[48,6144]{1,0:T(8,128)(2,1)} %collective-permute-done.38.refs_3_, bf16[2,576,6144]{2,1,0:T(8,128)(2,1)} %bitcast.202, ...), custom_call_target="tpu_custom_call" | custom-call | flops 5435817984 | bytes 30670848 | tf_op jit(solution)/shard_map/gate_up/pallas_call | solution.py:225
  257.2 5.4 %collective-permute-start.39 = (bf16[192,1152]{1,0:T(8,128)(2,1)S(1)}, bf16[192,1152]{1,0:T(8,128)(2,1)S(1)}, u32[]{:S(2)}, u32[]{:S(2)}) collective-permute-start(bf16[192,1152]{1,0:T(8,128)(2,1)S(1)} %gate_up.3.refs_4_), channel_id=1, source_target_pairs={{0,8},{8,16},{16,24},{1,9},{9,17},{17,25},{2,10},{10,18},{18,26},{... | collective-permute-start | bytes 1327112 | tf_op jit(solution)/shard_map/ppermute | solution.py:54
  263.9 3.7 route.3
  267.6 1.8 collective-permute-start.48
  271.2 5.8 %collective-permute-done.40.refs_5_ = bf16[192,1152]{1,0:T(8,128)(2,1)S(1)} collective-permute-done((bf16[192,1152]{1,0:T(8,128)(2,1)S(1)}, bf16[192,1152]{1,0:T(8,128)(2,1)S(1)}, u32[]{:S(2)}, u32[]{:S(2)}) %collective-permute-start.40) | collective-permute-done | bytes 442400 | tf_op jit(solution)/shard_map/ppermute | solution.py:55
  278.9 15.9 %gate_up.4.refs_4_ = bf16[192,1152]{1,0:T(8,128)(2,1)S(1)} custom-call(bf16[48,6144]{1,0:T(8,128)(2,1)S(1)} %get-tuple-element.146.refs_0_, bf16[48,6144]{1,0:T(8,128)(2,1)S(1)} %collective-permute-done.41.refs_1_, bf16[48,6144]{1,0:T(8,128)(2,1)} %collective-permute-done.42.refs_2_, bf16[48,6144]{1,0:T(8,128)(2,1)} %collective-permute-done.43.refs_3_, ...), custom_call_target="tpu_custom_call" | custom-call | flops 5435817984 | bytes 30670848 | tf_op jit(solution)/shard_map/gate_up/pallas_call | solution.py:225
  294.9 4.6 %collective-permute-start.46 = (bf16[192,1152]{1,0:T(8,128)(2,1)S(1)}, bf16[192,1152]{1,0:T(8,128)(2,1)S(1)}, u32[]{:S(2)}, u32[]{:S(2)}) collective-permute-start(bf16[192,1152]{1,0:T(8,128)(2,1)S(1)} %gate_up.4.refs_4_), channel_id=1, source_target_pairs={{0,8},{8,16},{16,24},{1,9},{9,17},{17,25},{2,10},{10,18},{18,26},{... | collective-permute-start | bytes 1327112 | tf_op jit(solution)/shard_map/ppermute | solution.py:54
  300.8 4.5 collective-permute-done.46.refs_3_
  306.0 3.7 collective-permute-done.47.refs_5_
  313.0 1.7 collective-permute-start.52
  314.6 18.6 %gate_up.5.refs_4_ = bf16[384,1152]{1,0:T(8,128)(2,1)S(1)} custom-call(bf16[96,6144]{1,0:T(8,128)(2,1)S(1)} %get-tuple-element.156.refs_0_, bf16[96,6144]{1,0:T(8,128)(2,1)S(1)} %collective-permute-done.48.refs_1_, bf16[96,6144]{1,0:T(8,128)(2,1)S(1)} %collective-permute-done.49.refs_2_, bf16[96,6144]{1,0:T(8,128)(2,1)} %collective-permute-done.50.refs_3_, ...), custom_call_target="tpu_custom_call" | custom-call | flops 10871635968 | bytes 33030144 | tf_op jit(solution)/shard_map/gate_up/pallas_call | solution.py:225
  334.8 8.4 %collective-permute-start.55 = (bf16[384,1152]{1,0:T(8,128)(2,1)S(1)}, bf16[384,1152]{1,0:T(8,128)(2,1)S(1)}, u32[]{:S(2)}, u32[]{:S(2)}) collective-permute-start(bf16[384,1152]{1,0:T(8,128)(2,1)S(1)} %gate_up.5.refs_4_), channel_id=1, source_target_pairs={{0,8},{8,16},{16,24},{1,9},{9,17},{17,25},{2,10},{10,18},{18,26},{... | collective-permute-start | bytes 2654216 | tf_op jit(solution)/shard_map/ppermute | solution.py:54
  348.7 1.6 copy.53
  357.2 7.2 %down.3 = (bf16[48,1536]{1,0:T(8,128)(2,1)S(1)}, bf16[48,1536]{1,0:T(8,128)(2,1)S(1)}, bf16[48,1536]{1,0:T(8,128)(2,1)S(1)}, bf16[48,1536]{1,0:T(8,128)(2,1)S(1)}) custom-call(s32[3]{0:T(128)S(1)} %pad_add_fusion.refs_0_, bf16[192,1152]{1,0:T(8,128)(2,1)S(1)} %copy-done.21, bf16[192,1152]{1,0:T(8,128)(2,1)S(1)} %copy-done.17, ...), custom_call_target="tpu_custom_call" | custom-call | flops 2717908992 | bytes 20971520 | tf_op jit(solution)/shard_map/down/pallas_call | solution.py:282
  364.4 2.1 collective-permute-done.58.refs_7_
  368.6 1.7 collective-permute-start.68
  372.2 7.3 %down.4 = (bf16[48,1536]{1,0:T(8,128)(2,1)S(1)}, bf16[48,1536]{1,0:T(8,128)(2,1)S(1)}, bf16[48,1536]{1,0:T(8,128)(2,1)S(1)}, bf16[48,1536]{1,0:T(8,128)(2,1)S(1)}) custom-call(s32[3]{0:T(128)S(1)} %pad_add_fusion.refs_0_, bf16[192,1152]{1,0:T(8,128)(2,1)} %collective-permute-done.57.refs_1_, bf16[192,1152]{1,0:T(8,128)(2,1)} %collective-permute-done.51.refs_2_, ...), custom_call_target="tpu_custom_call" | custom-call | flops 2717908992 | bytes 20971520 | tf_op jit(solution)/shard_map/down/pallas_call | solution.py:282
  379.5 14.2 %collective-permute-done.60.refs_6_ = bf16[384,1152]{1,0:T(8,128)(2,1)S(1)} collective-permute-done((bf16[384,1152]{1,0:T(8,128)(2,1)}, bf16[384,1152]{1,0:T(8,128)(2,1)S(1)}, u32[]{:S(2)}, u32[]{:S(2)}) %collective-permute-start.60) | collective-permute-done | bytes 884768 | tf_op jit(solution)/shard_map/ppermute | solution.py:55
  397.8 2.1 collective-permute-start.69
  399.9 9.4 %collective-permute-done.62.refs_7_ = bf16[384,1152]{1,0:T(8,128)(2,1)S(1)} collective-permute-done((bf16[384,1152]{1,0:T(8,128)(2,1)S(1)}, bf16[384,1152]{1,0:T(8,128)(2,1)S(1)}, u32[]{:S(2)}, u32[]{:S(2)}) %collective-permute-start.62) | collective-permute-done | bytes 884768 | tf_op jit(solution)/shard_map/ppermute | solution.py:55
  409.3 9.3 %down.5 = (bf16[96,1536]{1,0:T(8,128)(2,1)S(1)}, bf16[96,1536]{1,0:T(8,128)(2,1)S(1)}, bf16[96,1536]{1,0:T(8,128)(2,1)S(1)}, bf16[96,1536]{1,0:T(8,128)(2,1)S(1)}) custom-call(s32[3]{0:T(128)S(1)} %pad_add_fusion.refs_0_, bf16[384,1152]{1,0:T(8,128)(2,1)S(1)} %collective-permute-done.61.refs_1_, bf16[384,1152]{1,0:T(8,128)(2,1)S(1)} %collective-permute-done.59.refs_2_, ...), custom_call_target="tpu_custom_call" | custom-call | flops 5435817984 | bytes 20971520 | tf_op jit(solution)/shard_map/down/pallas_call | solution.py:282
  420.2 2.1 collective-permute-start.63
  422.8 3.6 collective-permute-done.65
  426.5 3.1 collective-permute-done.64
  432.5 5.0 %collective-permute-done.74 = bf16[64,1536]{1,0:T(8,128)(2,1)S(1)} collective-permute-done((bf16[64,1536]{1,0:T(8,128)(2,1)S(1)}, bf16[64,1536]{1,0:T(8,128)(2,1)S(1)}, u32[]{:S(2)}, u32[]{:S(2)}) %collective-permute-start.74) | collective-permute-done | bytes 196640 | tf_op jit(solution)/shard_map/ppermute | solution.py:28
  437.5 4.0 collective-permute-done.73
  (304 shorter events, 82.9 us)
Async XLA Ops:
  6.5 123.3 %all-gather.10.cloned.1.call-start = ((), (), s32[]{:S(2)}) async-start(), calls=%async_computation.1 | async-start | bytes 9437184 | tf_op jit(solution)/shard_map/all_gather | solution.py:401
  7.3 231.9 %all-gather.12.cloned.1.call-start = ((), (), s32[]{:S(2)}) async-start(), calls=%async_computation.2 | async-start | bytes 21233664 | tf_op jit(solution)/shard_map/all_gather | solution.py:401
  8.0 231.2 %all-gather.14.cloned.1.call-start = ((), (), s32[]{:S(2)}) async-start(), calls=%async_computation.3 | async-start | bytes 21233664 | tf_op jit(solution)/shard_map/all_gather | solution.py:401
  8.8 342.3 %all-gather.8.cloned.1.call-start = ((), (), s32[]{:S(2)}) async-start(), calls=%async_computation | async-start | bytes 21233664 | tf_op jit(solution)/shard_map/all_gather | solution.py:401
  10.1 10.2 %collective-permute-start.5 = (f32[68,4]{0,1:T(4,128)S(1)}, f32[68,4]{0,1:T(4,128)S(1)}, u32[]{:S(2)}, u32[]{:S(2)}) collective-permute-start(f32[68,4]{0,1:T(4,128)S(1)} %pad_maximum_fusion.15), channel_id=1, source_target_pairs={{0,24},{8,0},{16,8},{24,16},{1,25},{9,1},{17,9},{25,17},{2,26},{10... | collective-permute-start | bytes 3272 | tf_op jit(solution)/shard_map/ppermute | solution.py:28
  23.8 14.4 %collective-permute-start.8 = (bf16[8,128,128]{2,1,0:T(8,128)(2,1)S(1)}, bf16[8,128,128]{2,1,0:T(8,128)(2,1)}, u32[]{:S(2)}, u32[]{:S(2)}) collective-permute-start(bf16[8,128,128]{2,1,0:T(8,128)(2,1)S(1)} %add_convert_fusion.3), channel_id=1, source_target_pairs={{0,8},{8,16},{16,24},{1,9},{9,17},{17,25},{2,10},{10,18},{18,26},{... | collective-permute-start | bytes 786440 | tf_op jit(solution)/shard_map/ppermute | solution.py:28
  29.0 11.6 %collective-permute-start.9 = (bf16[8,128,128]{2,1,0:T(8,128)(2,1)S(1)}, bf16[8,128,128]{2,1,0:T(8,128)(2,1)}, u32[]{:S(2)}, u32[]{:S(2)}) collective-permute-start(bf16[8,128,128]{2,1,0:T(8,128)(2,1)S(1)} %add_convert_fusion.3), channel_id=1, source_target_pairs={{0,16},{8,24},{1,17},{9,25},{2,18},{10,26},{3,19},{11,27},{4,20},{... | collective-permute-start | bytes 786440 | tf_op jit(solution)/shard_map/ppermute | solution.py:28
  31.7 13.7 %collective-permute-start.10 = (bf16[8,128,128]{2,1,0:T(8,128)(2,1)S(1)}, bf16[8,128,128]{2,1,0:T(8,128)(2,1)}, u32[]{:S(2)}, u32[]{:S(2)}) collective-permute-start(bf16[8,128,128]{2,1,0:T(8,128)(2,1)S(1)} %add_convert_fusion.3), channel_id=1, source_target_pairs={{0,24},{1,25},{2,26},{3,27},{4,28},{5,29},{6,30},{7,31}} | collective-permute-start | bytes 786440 | tf_op jit(solution)/shard_map/ppermute | solution.py:28
  52.7 31.2 %collective-permute-start.12 = (bf16[256,2048]{1,0:T(8,128)(2,1)S(1)}, bf16[256,2048]{1,0:T(8,128)(2,1)S(1)}, u32[]{:S(2)}, u32[]{:S(2)}) collective-permute-start(bf16[256,2048]{1,0:T(8,128)(2,1)S(1)} %copy.61.refs_4_.refs_3_), channel_id=1, source_target_pairs={{0,8},{8,16},{16,24},{1,9},{9,17},{17,25},{2,10},{10,18},{18,26},{... | collective-permute-start | bytes 3145736 | tf_op jit(solution)/shard_map/ppermute | solution.py:54
  60.5 28.0 %collective-permute-start.13 = (bf16[256,2048]{1,0:T(8,128)(2,1)S(1)}, bf16[256,2048]{1,0:T(8,128)(2,1)}, u32[]{:S(2)}, u32[]{:S(2)}) collective-permute-start(bf16[256,2048]{1,0:T(8,128)(2,1)S(1)} %copy.61.refs_4_.refs_3_), channel_id=1, source_target_pairs={{24,16},{16,8},{8,0},{25,17},{17,9},{9,1},{26,18},{18,10},{10,2},{... | collective-permute-start | bytes 3145736 | tf_op jit(solution)/shard_map/ppermute | solution.py:55
  62.7 76.5 %collective-permute-start.2 = (bf16[64,1536]{1,0:T(8,128)(2,1)}, bf16[64,1536]{1,0:T(8,128)(2,1)S(1)}, u32[]{:S(2)}, u32[]{:S(2)}) collective-permute-start(bf16[64,1536]{1,0:T(8,128)(2,1)} %get-tuple-element.234), channel_id=1, source_target_pairs={{0,24},{8,0},{16,8},{24,16},{1,25},{9,1},{17,9},{25,17},{2,26},{10... | collective-permute-start | bytes 589832 | tf_op jit(solution)/shard_map/ppermute | solution.py:28
  68.9 71.8 %collective-permute-start.1 = (bf16[64,1536]{1,0:T(8,128)(2,1)}, bf16[64,1536]{1,0:T(8,128)(2,1)}, u32[]{:S(2)}, u32[]{:S(2)}) collective-permute-start(bf16[64,1536]{1,0:T(8,128)(2,1)} %get-tuple-element.235), channel_id=1, source_target_pairs={{0,16},{8,24},{16,0},{24,8},{1,17},{9,25},{17,1},{25,9},{2,18},{10... | collective-permute-start | bytes 589832 | tf_op jit(solution)/shard_map/ppermute | solution.py:28
  68.9 73.3 %collective-permute-start = (bf16[64,1536]{1,0:T(8,128)(2,1)}, bf16[64,1536]{1,0:T(8,128)(2,1)}, u32[]{:S(2)}, u32[]{:S(2)}) collective-permute-start(bf16[64,1536]{1,0:T(8,128)(2,1)} %get-tuple-element.233), channel_id=1, source_target_pairs={{0,8},{8,16},{16,24},{24,0},{1,9},{9,17},{17,25},{25,1},{2,10},{10... | collective-permute-start | bytes 589832 | tf_op jit(solution)/shard_map/ppermute | solution.py:28
  90.2 36.7 %collective-permute-start.15 = (bf16[256,2048]{1,0:T(8,128)(2,1)}, bf16[256,2048]{1,0:T(8,128)(2,1)}, u32[]{:S(2)}, u32[]{:S(2)}) collective-permute-start(bf16[256,2048]{1,0:T(8,128)(2,1)} %collective-permute-done.13.refs_5_.refs_4_), channel_id=1, source_target_pairs={{16,8},{8,0},{17,9},{9,1},{18,10},{10,2},{19,11},{11,3},{20,12},{1... | collective-permute-start | bytes 3145736 | tf_op jit(solution)/shard_map/ppermute | solution.py:55
  126.9 38.5 %collective-permute-start.16 = (bf16[256,2048]{1,0:T(8,128)(2,1)}, bf16[256,2048]{1,0:T(8,128)(2,1)}, u32[]{:S(2)}, u32[]{:S(2)}) collective-permute-start(bf16[256,2048]{1,0:T(8,128)(2,1)} %collective-permute-done.14.refs_2_.refs_1_), channel_id=1, source_target_pairs={{16,24},{17,25},{18,26},{19,27},{20,28},{21,29},{22,30},{23,31}} | collective-permute-start | bytes 3145736 | tf_op jit(solution)/shard_map/ppermute | solution.py:54
  128.5 36.9 %collective-permute-start.17 = (bf16[256,2048]{1,0:T(8,128)(2,1)}, bf16[256,2048]{1,0:T(8,128)(2,1)}, u32[]{:S(2)}, u32[]{:S(2)}) collective-permute-start(bf16[256,2048]{1,0:T(8,128)(2,1)} %collective-permute-done.15.refs_6_.refs_5_), channel_id=1, source_target_pairs={{8,0},{9,1},{10,2},{11,3},{12,4},{13,5},{14,6},{15,7}} | collective-permute-start | bytes 3145736 | tf_op jit(solution)/shard_map/ppermute | solution.py:55
  139.2 12.1 %collective-permute-start.18 = (bf16[128,1536]{1,0:T(8,128)(2,1)S(1)}, bf16[128,1536]{1,0:T(8,128)(2,1)S(1)}, u32[]{:S(2)}, u32[]{:S(2)}) collective-permute-start(bf16[128,1536]{1,0:T(8,128)(2,1)S(1)} %get-tuple-element.120), channel_id=1, source_target_pairs={{0,1},{1,0},{2,3},{3,2},{4,5},{5,4},{6,7},{7,6},{8,9},{9,8},{10,11... | collective-permute-start | bytes 1179656 | tf_op jit(solution)/shard_map/ppermute | solution.py:33
  140.7 17.8 %collective-permute-start.19 = (bf16[128,1536]{1,0:T(8,128)(2,1)S(1)}, bf16[128,1536]{1,0:T(8,128)(2,1)S(1)}, u32[]{:S(2)}, u32[]{:S(2)}) collective-permute-start(bf16[128,1536]{1,0:T(8,128)(2,1)S(1)} %get-tuple-element.121), channel_id=1, source_target_pairs={{0,2},{1,3},{2,0},{3,1},{4,6},{5,7},{6,4},{7,5},{8,10},{9,11},{10,... | collective-permute-start | bytes 1179656 | tf_op jit(solution)/shard_map/ppermute | solution.py:33
  142.3 16.3 %collective-permute-start.20 = (bf16[128,1536]{1,0:T(8,128)(2,1)S(1)}, bf16[128,1536]{1,0:T(8,128)(2,1)S(1)}, u32[]{:S(2)}, u32[]{:S(2)}) collective-permute-start(bf16[128,1536]{1,0:T(8,128)(2,1)S(1)} %get-tuple-element.122), channel_id=1, source_target_pairs={{0,3},{1,2},{2,1},{3,0},{4,7},{5,6},{6,5},{7,4},{8,11},{9,10},{10,... | collective-permute-start | bytes 1179656 | tf_op jit(solution)/shard_map/ppermute | solution.py:33
  158.8 17.4 %collective-permute-start.24 = (bf16[128,1536]{1,0:T(8,128)(2,1)S(1)}, bf16[128,1536]{1,0:T(8,128)(2,1)S(1)}, u32[]{:S(2)}, u32[]{:S(2)}) collective-permute-start(bf16[128,1536]{1,0:T(8,128)(2,1)S(1)} %add_convert_fusion.refs_4_), channel_id=1, source_target_pairs={{0,8},{8,16},{16,24},{1,9},{9,17},{17,25},{2,10},{10,18},{18,26},{... | collective-permute-start | bytes 1179656 | tf_op jit(solution)/shard_map/ppermute | solution.py:54
  164.0 12.2 %collective-permute-start.25 = (bf16[128,1536]{1,0:T(8,128)(2,1)S(1)}, bf16[128,1536]{1,0:T(8,128)(2,1)}, u32[]{:S(2)}, u32[]{:S(2)}) collective-permute-start(bf16[128,1536]{1,0:T(8,128)(2,1)S(1)} %add_convert_fusion.refs_4_), channel_id=1, source_target_pairs={{24,16},{16,8},{8,0},{25,17},{17,9},{9,1},{26,18},{18,10},{10,2},{... | collective-permute-start | bytes 1179656 | tf_op jit(solution)/shard_map/ppermute | solution.py:55
  172.7 18.2 %collective-permute-start.23 = (bf16[128,1536]{1,0:T(8,128)(2,1)}, bf16[128,1536]{1,0:T(8,128)(2,1)S(1)}, u32[]{:S(2)}, u32[]{:S(2)}) collective-permute-start(bf16[128,1536]{1,0:T(8,128)(2,1)} %get-tuple-element.127), channel_id=1, source_target_pairs={{0,3},{1,2},{2,1},{3,0},{4,7},{5,6},{6,5},{7,4},{8,11},{9,10},{10,... | collective-permute-start | bytes 1179656 | tf_op jit(solution)/shard_map/ppermute | solution.py:33
  174.2 16.7 %collective-permute-start.22 = (bf16[128,1536]{1,0:T(8,128)(2,1)}, bf16[128,1536]{1,0:T(8,128)(2,1)S(1)}, u32[]{:S(2)}, u32[]{:S(2)}) collective-permute-start(bf16[128,1536]{1,0:T(8,128)(2,1)} %get-tuple-element.125), channel_id=1, source_target_pairs={{0,2},{1,3},{2,0},{3,1},{4,6},{5,7},{6,4},{7,5},{8,10},{9,11},{10,... | collective-permute-start | bytes 1179656 | tf_op jit(solution)/shard_map/ppermute | solution.py:33
  175.4 15.5 %collective-permute-start.21 = (bf16[128,1536]{1,0:T(8,128)(2,1)}, bf16[128,1536]{1,0:T(8,128)(2,1)S(1)}, u32[]{:S(2)}, u32[]{:S(2)}) collective-permute-start(bf16[128,1536]{1,0:T(8,128)(2,1)} %get-tuple-element.123), channel_id=1, source_target_pairs={{0,1},{1,0},{2,3},{3,2},{4,5},{5,4},{6,7},{7,6},{8,9},{9,8},{10,11... | collective-permute-start | bytes 1179656 | tf_op jit(solution)/shard_map/ppermute | solution.py:33
  176.9 12.0 %collective-permute-start.27 = (bf16[128,1536]{1,0:T(8,128)(2,1)}, bf16[128,1536]{1,0:T(8,128)(2,1)S(1)}, u32[]{:S(2)}, u32[]{:S(2)}) collective-permute-start(bf16[128,1536]{1,0:T(8,128)(2,1)} %collective-permute-done.25.refs_5_), channel_id=1, source_target_pairs={{16,8},{8,0},{17,9},{9,1},{18,10},{10,2},{19,11},{11,3},{20,12},{1... | collective-permute-start | bytes 1179656 | tf_op jit(solution)/shard_map/ppermute | solution.py:55
  206.2 9.8 %collective-permute-start.31 = (bf16[128,1536]{1,0:T(8,128)(2,1)S(1)}, bf16[128,1536]{1,0:T(8,128)(2,1)}, u32[]{:S(2)}, u32[]{:S(2)}) collective-permute-start(bf16[128,1536]{1,0:T(8,128)(2,1)S(1)} %add_convert_fusion.1.refs_4_), channel_id=1, source_target_pairs={{24,16},{16,8},{8,0},{25,17},{17,9},{9,1},{26,18},{18,10},{10,2},{... | collective-permute-start | bytes 1179656 | tf_op jit(solution)/shard_map/ppermute | solution.py:55
  207.5 16.5 %collective-permute-start.36 = (bf16[48,6144]{1,0:T(8,128)(2,1)}, bf16[48,6144]{1,0:T(8,128)(2,1)S(1)}, u32[]{:S(2)}, u32[]{:S(2)}) collective-permute-start(bf16[48,6144]{1,0:T(8,128)(2,1)} %get-tuple-element.133), channel_id=1, source_target_pairs={{0,1},{1,0},{2,3},{3,2},{4,5},{5,4},{6,7},{7,6},{8,9},{9,8},{10,11... | collective-permute-start | bytes 1769480 | tf_op jit(solution)/shard_map/ppermute | solution.py:33
  208.8 22.6 %collective-permute-start.37 = (bf16[48,6144]{1,0:T(8,128)(2,1)}, bf16[48,6144]{1,0:T(8,128)(2,1)S(1)}, u32[]{:S(2)}, u32[]{:S(2)}) collective-permute-start(bf16[48,6144]{1,0:T(8,128)(2,1)} %get-tuple-element.134), channel_id=1, source_target_pairs={{0,2},{1,3},{2,0},{3,1},{4,6},{5,7},{6,4},{7,5},{8,10},{9,11},{10,... | collective-permute-start | bytes 1769480 | tf_op jit(solution)/shard_map/ppermute | solution.py:33
  209.6 22.7 %collective-permute-start.38 = (bf16[48,6144]{1,0:T(8,128)(2,1)}, bf16[48,6144]{1,0:T(8,128)(2,1)}, u32[]{:S(2)}, u32[]{:S(2)}) collective-permute-start(bf16[48,6144]{1,0:T(8,128)(2,1)} %get-tuple-element.135), channel_id=1, source_target_pairs={{0,3},{1,2},{2,1},{3,0},{4,7},{5,6},{6,5},{7,4},{8,11},{9,10},{10,... | collective-permute-start | bytes 1769480 | tf_op jit(solution)/shard_map/ppermute | solution.py:33
  216.0 21.1 %collective-permute-start.32 = (bf16[128,1536]{1,0:T(8,128)(2,1)}, bf16[128,1536]{1,0:T(8,128)(2,1)}, u32[]{:S(2)}, u32[]{:S(2)}) collective-permute-start(bf16[128,1536]{1,0:T(8,128)(2,1)} %collective-permute-done.30.refs_3_), channel_id=1, source_target_pairs={{8,16},{16,24},{9,17},{17,25},{10,18},{18,26},{11,19},{19,27},{12,... | collective-permute-start | bytes 1179656 | tf_op jit(solution)/shard_map/ppermute | solution.py:54
  217.4 19.8 %collective-permute-start.33 = (bf16[128,1536]{1,0:T(8,128)(2,1)}, bf16[128,1536]{1,0:T(8,128)(2,1)}, u32[]{:S(2)}, u32[]{:S(2)}) collective-permute-start(bf16[128,1536]{1,0:T(8,128)(2,1)} %collective-permute-done.31.refs_5_), channel_id=1, source_target_pairs={{16,8},{8,0},{17,9},{9,1},{18,10},{10,2},{19,11},{11,3},{20,12},{1... | collective-permute-start | bytes 1179656 | tf_op jit(solution)/shard_map/ppermute | solution.py:55
  232.3 35.3 %collective-permute-start.41 = (bf16[48,6144]{1,0:T(8,128)(2,1)}, bf16[48,6144]{1,0:T(8,128)(2,1)S(1)}, u32[]{:S(2)}, u32[]{:S(2)}) collective-permute-start(bf16[48,6144]{1,0:T(8,128)(2,1)} %copy-done.28), channel_id=1, source_target_pairs={{0,1},{1,0},{2,3},{3,2},{4,5},{5,4},{6,7},{7,6},{8,9},{9,8},{10,11... | collective-permute-start | bytes 1769480 | tf_op jit(solution)/shard_map/ppermute | solution.py:33
  235.5 32.2 %collective-permute-start.42 = (bf16[48,6144]{1,0:T(8,128)(2,1)}, bf16[48,6144]{1,0:T(8,128)(2,1)}, u32[]{:S(2)}, u32[]{:S(2)}) collective-permute-start(bf16[48,6144]{1,0:T(8,128)(2,1)} %copy-done.27), channel_id=1, source_target_pairs={{0,2},{1,3},{2,0},{3,1},{4,6},{5,7},{6,4},{7,5},{8,10},{9,11},{10,... | collective-permute-start | bytes 1769480 | tf_op jit(solution)/shard_map/ppermute | solution.py:33
  235.7 31.9 %collective-permute-start.43 = (bf16[48,6144]{1,0:T(8,128)(2,1)}, bf16[48,6144]{1,0:T(8,128)(2,1)}, u32[]{:S(2)}, u32[]{:S(2)}) collective-permute-start(bf16[48,6144]{1,0:T(8,128)(2,1)} %copy-done.26), channel_id=1, source_target_pairs={{0,3},{1,2},{2,1},{3,0},{4,7},{5,6},{6,5},{7,4},{8,11},{9,10},{10,... | collective-permute-start | bytes 1769480 | tf_op jit(solution)/shard_map/ppermute | solution.py:33
  237.2 20.0 %collective-permute-start.34 = (bf16[128,1536]{1,0:T(8,128)(2,1)}, bf16[128,1536]{1,0:T(8,128)(2,1)S(1)}, u32[]{:S(2)}, u32[]{:S(2)}) collective-permute-start(bf16[128,1536]{1,0:T(8,128)(2,1)} %collective-permute-done.32.refs_2_), channel_id=1, source_target_pairs={{16,24},{17,25},{18,26},{19,27},{20,28},{21,29},{22,30},{23,31}} | collective-permute-start | bytes 1179656 | tf_op jit(solution)/shard_map/ppermute | solution.py:54
  237.8 24.7 %collective-permute-start.35 = (bf16[128,1536]{1,0:T(8,128)(2,1)}, bf16[128,1536]{1,0:T(8,128)(2,1)}, u32[]{:S(2)}, u32[]{:S(2)}) collective-permute-start(bf16[128,1536]{1,0:T(8,128)(2,1)} %collective-permute-done.33.refs_6_), channel_id=1, source_target_pairs={{8,0},{9,1},{10,2},{11,3},{12,4},{13,5},{14,6},{15,7}} | collective-permute-start | bytes 1179656 | tf_op jit(solution)/shard_map/ppermute | solution.py:55
  257.2 14.0 %collective-permute-start.39 = (bf16[192,1152]{1,0:T(8,128)(2,1)S(1)}, bf16[192,1152]{1,0:T(8,128)(2,1)S(1)}, u32[]{:S(2)}, u32[]{:S(2)}) collective-permute-start(bf16[192,1152]{1,0:T(8,128)(2,1)S(1)} %gate_up.3.refs_4_), channel_id=1, source_target_pairs={{0,8},{8,16},{16,24},{1,9},{9,17},{17,25},{2,10},{10,18},{18,26},{... | collective-permute-start | bytes 1327112 | tf_op jit(solution)/shard_map/ppermute | solution.py:54
  262.6 14.4 %collective-permute-start.40 = (bf16[192,1152]{1,0:T(8,128)(2,1)S(1)}, bf16[192,1152]{1,0:T(8,128)(2,1)S(1)}, u32[]{:S(2)}, u32[]{:S(2)}) collective-permute-start(bf16[192,1152]{1,0:T(8,128)(2,1)S(1)} %gate_up.3.refs_4_), channel_id=1, source_target_pairs={{24,16},{16,8},{8,0},{25,17},{17,9},{9,1},{26,18},{18,10},{10,2},{... | collective-permute-start | bytes 1327112 | tf_op jit(solution)/shard_map/ppermute | solution.py:55
  267.6 43.4 %collective-permute-start.48 = (bf16[96,6144]{1,0:T(8,128)(2,1)S(1)}, bf16[96,6144]{1,0:T(8,128)(2,1)S(1)}, u32[]{:S(2)}, u32[]{:S(2)}) collective-permute-start(bf16[96,6144]{1,0:T(8,128)(2,1)S(1)} %get-tuple-element.158), channel_id=1, source_target_pairs={{0,1},{1,0},{2,3},{3,2},{4,5},{5,4},{6,7},{7,6},{8,9},{9,8},{10,11... | collective-permute-start | bytes 3538952 | tf_op jit(solution)/shard_map/ppermute | solution.py:33
  269.4 42.1 %collective-permute-start.49 = (bf16[96,6144]{1,0:T(8,128)(2,1)S(1)}, bf16[96,6144]{1,0:T(8,128)(2,1)S(1)}, u32[]{:S(2)}, u32[]{:S(2)}) collective-permute-start(bf16[96,6144]{1,0:T(8,128)(2,1)S(1)} %get-tuple-element.161), channel_id=1, source_target_pairs={{0,2},{1,3},{2,0},{3,1},{4,6},{5,7},{6,4},{7,5},{8,10},{9,11},{10,... | collective-permute-start | bytes 3538952 | tf_op jit(solution)/shard_map/ppermute | solution.py:33
  269.8 41.7 %collective-permute-start.50 = (bf16[96,6144]{1,0:T(8,128)(2,1)S(1)}, bf16[96,6144]{1,0:T(8,128)(2,1)}, u32[]{:S(2)}, u32[]{:S(2)}) collective-permute-start(bf16[96,6144]{1,0:T(8,128)(2,1)S(1)} %get-tuple-element.164), channel_id=1, source_target_pairs={{0,3},{1,2},{2,1},{3,0},{4,7},{5,6},{6,5},{7,4},{8,11},{9,10},{10,... | collective-permute-start | bytes 3538952 | tf_op jit(solution)/shard_map/ppermute | solution.py:33
  277.0 17.9 %collective-permute-start.44 = (bf16[192,1152]{1,0:T(8,128)(2,1)S(1)}, bf16[192,1152]{1,0:T(8,128)(2,1)S(1)}, u32[]{:S(2)}, u32[]{:S(2)}) collective-permute-start(bf16[192,1152]{1,0:T(8,128)(2,1)S(1)} %collective-permute-done.39.refs_3_), channel_id=1, source_target_pairs={{8,16},{16,24},{9,17},{17,25},{10,18},{18,26},{11,19},{19,27},{12,... | collective-permute-start | bytes 1327112 | tf_op jit(solution)/shard_map/ppermute | solution.py:54
  277.6 17.3 %collective-permute-start.45 = (bf16[192,1152]{1,0:T(8,128)(2,1)S(1)}, bf16[192,1152]{1,0:T(8,128)(2,1)S(1)}, u32[]{:S(2)}, u32[]{:S(2)}) collective-permute-start(bf16[192,1152]{1,0:T(8,128)(2,1)S(1)} %collective-permute-done.40.refs_5_), channel_id=1, source_target_pairs={{16,8},{8,0},{17,9},{9,1},{18,10},{10,2},{19,11},{11,3},{20,12},{1... | collective-permute-start | bytes 1327112 | tf_op jit(solution)/shard_map/ppermute | solution.py:55
  294.9 10.4 %collective-permute-start.46 = (bf16[192,1152]{1,0:T(8,128)(2,1)S(1)}, bf16[192,1152]{1,0:T(8,128)(2,1)S(1)}, u32[]{:S(2)}, u32[]{:S(2)}) collective-permute-start(bf16[192,1152]{1,0:T(8,128)(2,1)S(1)} %gate_up.4.refs_4_), channel_id=1, source_target_pairs={{0,8},{8,16},{16,24},{1,9},{9,17},{17,25},{2,10},{10,18},{18,26},{... | collective-permute-start | bytes 1327112 | tf_op jit(solution)/shard_map/ppermute | solution.py:54
  299.5 10.2 %collective-permute-start.47 = (bf16[192,1152]{1,0:T(8,128)(2,1)S(1)}, bf16[192,1152]{1,0:T(8,128)(2,1)S(1)}, u32[]{:S(2)}, u32[]{:S(2)}) collective-permute-start(bf16[192,1152]{1,0:T(8,128)(2,1)S(1)} %gate_up.4.refs_4_), channel_id=1, source_target_pairs={{24,16},{16,8},{8,0},{25,17},{17,9},{9,1},{26,18},{18,10},{10,2},{... | collective-permute-start | bytes 1327112 | tf_op jit(solution)/shard_map/ppermute | solution.py:55
  305.3 28.0 %collective-permute-start.53 = (bf16[192,1152]{1,0:T(8,128)(2,1)S(1)}, bf16[192,1152]{1,0:T(8,128)(2,1)S(1)}, u32[]{:S(2)}, u32[]{:S(2)}) collective-permute-start(bf16[192,1152]{1,0:T(8,128)(2,1)S(1)} %collective-permute-done.44.refs_2_), channel_id=1, source_target_pairs={{16,24},{17,25},{18,26},{19,27},{20,28},{21,29},{22,30},{23,31}} | collective-permute-start | bytes 1327112 | tf_op jit(solution)/shard_map/ppermute | solution.py:54
  309.7 24.3 %collective-permute-start.54 = (bf16[192,1152]{1,0:T(8,128)(2,1)S(1)}, bf16[192,1152]{1,0:T(8,128)(2,1)S(1)}, u32[]{:S(2)}, u32[]{:S(2)}) collective-permute-start(bf16[192,1152]{1,0:T(8,128)(2,1)S(1)} %collective-permute-done.45.refs_6_), channel_id=1, source_target_pairs={{8,0},{9,1},{10,2},{11,3},{12,4},{13,5},{14,6},{15,7}} | collective-permute-start | bytes 1327112 | tf_op jit(solution)/shard_map/ppermute | solution.py:55
  311.5 21.7 %collective-permute-start.51 = (bf16[192,1152]{1,0:T(8,128)(2,1)S(1)}, bf16[192,1152]{1,0:T(8,128)(2,1)}, u32[]{:S(2)}, u32[]{:S(2)}) collective-permute-start(bf16[192,1152]{1,0:T(8,128)(2,1)S(1)} %collective-permute-done.46.refs_3_), channel_id=1, source_target_pairs={{8,16},{16,24},{9,17},{17,25},{10,18},{18,26},{11,19},{19,27},{12,... | collective-permute-start | bytes 1327112 | tf_op jit(solution)/shard_map/ppermute | solution.py:54
  313.0 20.3 %collective-permute-start.52 = (bf16[192,1152]{1,0:T(8,128)(2,1)S(1)}, bf16[192,1152]{1,0:T(8,128)(2,1)}, u32[]{:S(2)}, u32[]{:S(2)}) collective-permute-start(bf16[192,1152]{1,0:T(8,128)(2,1)S(1)} %collective-permute-done.47.refs_5_), channel_id=1, source_target_pairs={{16,8},{8,0},{17,9},{9,1},{18,10},{10,2},{19,11},{11,3},{20,12},{1... | collective-permute-start | bytes 1327112 | tf_op jit(solution)/shard_map/ppermute | solution.py:55
  334.8 29.6 %collective-permute-start.55 = (bf16[384,1152]{1,0:T(8,128)(2,1)S(1)}, bf16[384,1152]{1,0:T(8,128)(2,1)S(1)}, u32[]{:S(2)}, u32[]{:S(2)}) collective-permute-start(bf16[384,1152]{1,0:T(8,128)(2,1)S(1)} %gate_up.5.refs_4_), channel_id=1, source_target_pairs={{0,8},{8,16},{16,24},{1,9},{9,17},{17,25},{2,10},{10,18},{18,26},{... | collective-permute-start | bytes 2654216 | tf_op jit(solution)/shard_map/ppermute | solution.py:54
  343.2 21.2 %collective-permute-start.56 = (bf16[384,1152]{1,0:T(8,128)(2,1)S(1)}, bf16[384,1152]{1,0:T(8,128)(2,1)}, u32[]{:S(2)}, u32[]{:S(2)}) collective-permute-start(bf16[384,1152]{1,0:T(8,128)(2,1)S(1)} %gate_up.5.refs_4_), channel_id=1, source_target_pairs={{24,16},{16,8},{8,0},{25,17},{17,9},{9,1},{26,18},{18,10},{10,2},{... | collective-permute-start | bytes 2654216 | tf_op jit(solution)/shard_map/ppermute | solution.py:55
  345.4 19.0 %collective-permute-start.57 = (bf16[192,1152]{1,0:T(8,128)(2,1)}, bf16[192,1152]{1,0:T(8,128)(2,1)}, u32[]{:S(2)}, u32[]{:S(2)}) collective-permute-start(bf16[192,1152]{1,0:T(8,128)(2,1)} %collective-permute-done.51.refs_2_), channel_id=1, source_target_pairs={{16,24},{17,25},{18,26},{19,27},{20,28},{21,29},{22,30},{23,31}} | collective-permute-start | bytes 1327112 | tf_op jit(solution)/shard_map/ppermute | solution.py:54
  346.8 19.8 %collective-permute-start.58 = (bf16[192,1152]{1,0:T(8,128)(2,1)}, bf16[192,1152]{1,0:T(8,128)(2,1)}, u32[]{:S(2)}, u32[]{:S(2)}) collective-permute-start(bf16[192,1152]{1,0:T(8,128)(2,1)} %collective-permute-done.52.refs_6_), channel_id=1, source_target_pairs={{8,0},{9,1},{10,2},{11,3},{12,4},{13,5},{14,6},{15,7}} | collective-permute-start | bytes 1327112 | tf_op jit(solution)/shard_map/ppermute | solution.py:55
  366.5 12.9 %collective-permute-start.59 = (bf16[384,1152]{1,0:T(8,128)(2,1)S(1)}, bf16[384,1152]{1,0:T(8,128)(2,1)S(1)}, u32[]{:S(2)}, u32[]{:S(2)}) collective-permute-start(bf16[384,1152]{1,0:T(8,128)(2,1)S(1)} %collective-permute-done.55.refs_3_), channel_id=1, source_target_pairs={{8,16},{16,24},{9,17},{17,25},{10,18},{18,26},{11,19},{19,27},{12,... | collective-permute-start | bytes 2654216 | tf_op jit(solution)/shard_map/ppermute | solution.py:54
  367.2 26.4 %collective-permute-start.60 = (bf16[384,1152]{1,0:T(8,128)(2,1)}, bf16[384,1152]{1,0:T(8,128)(2,1)S(1)}, u32[]{:S(2)}, u32[]{:S(2)}) collective-permute-start(bf16[384,1152]{1,0:T(8,128)(2,1)} %collective-permute-done.56.refs_5_), channel_id=1, source_target_pairs={{16,8},{8,0},{17,9},{9,1},{18,10},{10,2},{19,11},{11,3},{20,12},{1... | collective-permute-start | bytes 2654216 | tf_op jit(solution)/shard_map/ppermute | solution.py:55
  368.6 27.1 %collective-permute-start.68 = (bf16[48,1536]{1,0:T(8,128)(2,1)S(1)}, bf16[48,1536]{1,0:T(8,128)(2,1)S(1)}, u32[]{:S(2)}, u32[]{:S(2)}) collective-permute-start(bf16[48,1536]{1,0:T(8,128)(2,1)S(1)} %get-tuple-element.210), channel_id=1, source_target_pairs={{0,3},{1,2},{2,1},{3,0},{4,7},{5,6},{6,5},{7,4},{8,11},{9,10},{10,... | collective-permute-start | bytes 442376 | tf_op jit(solution)/shard_map/ppermute | solution.py:33
  370.3 25.4 %collective-permute-start.67 = (bf16[48,1536]{1,0:T(8,128)(2,1)S(1)}, bf16[48,1536]{1,0:T(8,128)(2,1)S(1)}, u32[]{:S(2)}, u32[]{:S(2)}) collective-permute-start(bf16[48,1536]{1,0:T(8,128)(2,1)S(1)} %get-tuple-element.209), channel_id=1, source_target_pairs={{0,2},{1,3},{2,0},{3,1},{4,6},{5,7},{6,4},{7,5},{8,10},{9,11},{10,... | collective-permute-start | bytes 442376 | tf_op jit(solution)/shard_map/ppermute | solution.py:33
  370.9 24.8 %collective-permute-start.66 = (bf16[48,1536]{1,0:T(8,128)(2,1)S(1)}, bf16[48,1536]{1,0:T(8,128)(2,1)S(1)}, u32[]{:S(2)}, u32[]{:S(2)}) collective-permute-start(bf16[48,1536]{1,0:T(8,128)(2,1)S(1)} %get-tuple-element.208), channel_id=1, source_target_pairs={{0,1},{1,0},{2,3},{3,2},{4,5},{5,4},{6,7},{7,6},{8,9},{9,8},{10,11... | collective-permute-start | bytes 442376 | tf_op jit(solution)/shard_map/ppermute | solution.py:33
  394.4 14.9 %collective-permute-start.62 = (bf16[384,1152]{1,0:T(8,128)(2,1)S(1)}, bf16[384,1152]{1,0:T(8,128)(2,1)S(1)}, u32[]{:S(2)}, u32[]{:S(2)}) collective-permute-start(bf16[384,1152]{1,0:T(8,128)(2,1)S(1)} %collective-permute-done.60.refs_6_), channel_id=1, source_target_pairs={{8,0},{9,1},{10,2},{11,3},{12,4},{13,5},{14,6},{15,7}} | collective-permute-start | bytes 2654216 | tf_op jit(solution)/shard_map/ppermute | solution.py:55
  396.3 23.9 %collective-permute-start.71 = (bf16[48,1536]{1,0:T(8,128)(2,1)S(1)}, bf16[48,1536]{1,0:T(8,128)(2,1)S(1)}, u32[]{:S(2)}, u32[]{:S(2)}) collective-permute-start(bf16[48,1536]{1,0:T(8,128)(2,1)S(1)} %get-tuple-element.214), channel_id=1, source_target_pairs={{0,3},{1,2},{2,1},{3,0},{4,7},{5,6},{6,5},{7,4},{8,11},{9,10},{10,... | collective-permute-start | bytes 442376 | tf_op jit(solution)/shard_map/ppermute | solution.py:33
  397.6 24.6 %collective-permute-start.70 = (bf16[48,1536]{1,0:T(8,128)(2,1)S(1)}, bf16[48,1536]{1,0:T(8,128)(2,1)S(1)}, u32[]{:S(2)}, u32[]{:S(2)}) collective-permute-start(bf16[48,1536]{1,0:T(8,128)(2,1)S(1)} %get-tuple-element.213), channel_id=1, source_target_pairs={{0,2},{1,3},{2,0},{3,1},{4,6},{5,7},{6,4},{7,5},{8,10},{9,11},{10,... | collective-permute-start | bytes 442376 | tf_op jit(solution)/shard_map/ppermute | solution.py:33
  397.8 24.4 %collective-permute-start.69 = (bf16[48,1536]{1,0:T(8,128)(2,1)S(1)}, bf16[48,1536]{1,0:T(8,128)(2,1)S(1)}, u32[]{:S(2)}, u32[]{:S(2)}) collective-permute-start(bf16[48,1536]{1,0:T(8,128)(2,1)S(1)} %get-tuple-element.212), channel_id=1, source_target_pairs={{0,1},{1,0},{2,3},{3,2},{4,5},{5,4},{6,7},{7,6},{8,9},{9,8},{10,11... | collective-permute-start | bytes 442376 | tf_op jit(solution)/shard_map/ppermute | solution.py:33
  430.5 11.0 %collective-permute-start.73 = (bf16[64,1536]{1,0:T(8,128)(2,1)S(1)}, bf16[64,1536]{1,0:T(8,128)(2,1)S(1)}, u32[]{:S(2)}, u32[]{:S(2)}) collective-permute-start(bf16[64,1536]{1,0:T(8,128)(2,1)S(1)} %get-tuple-element.226), channel_id=1, source_target_pairs={{0,16},{8,24},{16,0},{24,8},{1,17},{9,25},{17,1},{25,9},{2,18},{10... | collective-permute-start | bytes 589832 | tf_op jit(solution)/shard_map/ppermute | solution.py:28
  431.5 10.0 %collective-permute-start.72 = (bf16[64,1536]{1,0:T(8,128)(2,1)S(1)}, bf16[64,1536]{1,0:T(8,128)(2,1)S(1)}, u32[]{:S(2)}, u32[]{:S(2)}) collective-permute-start(bf16[64,1536]{1,0:T(8,128)(2,1)S(1)} %get-tuple-element.227), channel_id=1, source_target_pairs={{0,8},{8,16},{16,24},{24,0},{1,9},{9,17},{17,25},{25,1},{2,10},{10... | collective-permute-start | bytes 589832 | tf_op jit(solution)/shard_map/ppermute | solution.py:28
  (70 other events, 947.0 us)
Sparse Core Ops, SparseCore 0:
  8.9 19.4 all-gather.9
  30.0 27.9 all-gather.11
  59.5 27.6 all-gather.13
  88.6 27.5 all-gather.7

commit v2 on v1

--- a/solution.py
+++ b/solution.py
@@ -436,7 +436,7 @@
     def project(block, first):
         pieces = project_call(block, n_z, n_exp, rows, acts, w_out)
         arrived = [pieces[0]] + [
-            to_expert(after(pieces[k], first), k) for k in range(1, n_exp)
+            to_expert(pieces[k], k) for k in range(1, n_exp)
         ]
         total = jnp.concatenate([kept[s] for s in block], axis=0).astype(F32)
         for x in arrived:

time: 458 us -> 461 us (level)
  waiting for transfers between devices: 167 us -> 174 us
    ppermute x24, waiting for transfers between devices: 31 us -> 36.2 us  [to_expert(): return lax.ppermute(x, 'expert', [(i, i ^ k) for i in range(n)])]
  transfers between devices with their start and end apart: 79 -> 79, of which waited for: 28 -> 30; matrix products, arithmetic and copies ran while one was open for 7% -> 7% of each run, Pallas kernels for 21% -> 21%
where the time goes in v2:
time: 461 us; the launch traced here: 452 us
  waiting for transfers between devices  174 us (38%)
  starting transfers between devices  121 us (26%)
  Pallas kernels  94.7 us (21%)
  local copies, waits for them, and re-layouts  26.5 us (6%)
  between operations  14.8 us (3%)
  matrix products  12.5 us (3%)
  other arithmetic  9.01 us (2%)
    ppermute x18, waiting for transfers between devices, line_gather(): lax.ppermute(held[1], 'z', [(n - 1 - i, n - 1 - j) for i, j in onward])  97.6 us
    pallas_call x3, Pallas kernels, gate_up_call(): pl.pallas_call(lambda *refs: gate_up_kernel(len(pieces), tiles, *refs), n...  50.2 us
    ppermute x18, starting transfers between devices, line_gather(): right.append(lax.ppermute(held[0], 'z', onward))  43.8 us
    ppermute x24, waiting for transfers between devices, to_expert(): return lax.ppermute(x, 'expert', [(i, i ^ k) for i in range(n)])  36.2 us
    ppermute x24, starting transfers between devices, to_expert(): return lax.ppermute(x, 'expert', [(i, i ^ k) for i in range(n)])  28.3 us
    ppermute x12, starting transfers between devices, shift_z(): return lax.ppermute(x, 'z', perm)  24.8 us
    pallas_call x3, Pallas kernels, down_call(): pl.pallas_call(lambda *refs: down_kernel(n, count, *refs), name='down', o...  23.8 us
    ppermute x18, starting transfers between devices, line_gather(): lax.ppermute(held[1], 'z', [(n - 1 - i, n - 1 - j) for i, j in onward])  23.8 us
  transfers between devices with their start and end apart: 79, of which 30 were waited for; matrix products, arithmetic and copies ran while one was open for 7% of the time, Pallas kernels for 21%

profile of v2, /device:TPU:0, one launch (start us, length us, event | category | flops | bytes accessed | tf_op | source)
XLA Modules:
  0.0 452.3 jit_solution(14314644824563316421)
XLA Ops:
  10.1 5.1 %collective-permute-start.5 = (f32[68,4]{0,1:T(4,128)S(1)}, f32[68,4]{0,1:T(4,128)S(1)}, u32[]{:S(2)}, u32[]{:S(2)}) collective-permute-start(f32[68,4]{0,1:T(4,128)S(1)} %pad_maximum_fusion.15), channel_id=1, source_target_pairs={{0,24},{8,0},{16,8},{24,16},{1,25},{9,1},{17,9},{25,17},{2,26},{10... | collective-permute-start | bytes 3272 | tf_op jit(solution)/shard_map/ppermute | solution.py:28
  16.8 3.4 fusion.76
  23.8 5.2 %collective-permute-start.8 = (bf16[8,128,128]{2,1,0:T(8,128)(2,1)S(1)}, bf16[8,128,128]{2,1,0:T(8,128)(2,1)}, u32[]{:S(2)}, u32[]{:S(2)}) collective-permute-start(bf16[8,128,128]{2,1,0:T(8,128)(2,1)S(1)} %add_convert_fusion.3), channel_id=1, source_target_pairs={{0,8},{8,16},{16,24},{1,9},{9,17},{17,25},{2,10},{10,18},{18,26},{... | collective-permute-start | bytes 786440 | tf_op jit(solution)/shard_map/ppermute | solution.py:28
  29.0 2.7 collective-permute-start.9
  31.7 2.0 collective-permute-start.10
  33.7 4.3 convolution_bitcast_fusion
  38.2 2.4 collective-permute-done.9
  40.6 4.8 %collective-permute-done.10 = bf16[8,128,128]{2,1,0:T(8,128)(2,1)} collective-permute-done((bf16[8,128,128]{2,1,0:T(8,128)(2,1)S(1)}, bf16[8,128,128]{2,1,0:T(8,128)(2,1)}, u32[]{:S(2)}, u32[]{:S(2)}) %collective-permute-start.10) | collective-permute-done | bytes 262176 | tf_op jit(solution)/shard_map/ppermute | solution.py:28
  47.1 1.9 collective-permute-done.11
  49.1 2.7 multiply_reduce_fusion
  52.7 7.8 %collective-permute-start.12 = (bf16[256,2048]{1,0:T(8,128)(2,1)S(1)}, bf16[256,2048]{1,0:T(8,128)(2,1)S(1)}, u32[]{:S(2)}, u32[]{:S(2)}) collective-permute-start(bf16[256,2048]{1,0:T(8,128)(2,1)S(1)} %copy.61.refs_4_.refs_3_), channel_id=1, source_target_pairs={{0,8},{8,16},{16,24},{1,9},{9,17},{17,25},{2,10},{10,18},{18,26},{... | collective-permute-start | bytes 3145736 | tf_op jit(solution)/shard_map/ppermute | solution.py:54
  62.7 6.2 %collective-permute-start.2 = (bf16[64,1536]{1,0:T(8,128)(2,1)}, bf16[64,1536]{1,0:T(8,128)(2,1)S(1)}, u32[]{:S(2)}, u32[]{:S(2)}) collective-permute-start(bf16[64,1536]{1,0:T(8,128)(2,1)} %get-tuple-element.228), channel_id=1, source_target_pairs={{0,24},{8,0},{16,8},{24,16},{1,25},{9,1},{17,9},{25,17},{2,26},{10... | collective-permute-start | bytes 589832 | tf_op jit(solution)/shard_map/ppermute | solution.py:28
  71.0 12.9 %collective-permute-done.12.refs_3_.refs_2_ = bf16[256,2048]{1,0:T(8,128)(2,1)S(1)} collective-permute-done((bf16[256,2048]{1,0:T(8,128)(2,1)S(1)}, bf16[256,2048]{1,0:T(8,128)(2,1)S(1)}, u32[]{:S(2)}, u32[]{:S(2)}) %collective-permute-start.12) | collective-permute-done | bytes 1048608 | tf_op jit(solution)/shard_map/ppermute | solution.py:54
  83.9 4.6 %collective-permute-done.13.refs_5_.refs_4_ = bf16[256,2048]{1,0:T(8,128)(2,1)} collective-permute-done((bf16[256,2048]{1,0:T(8,128)(2,1)S(1)}, bf16[256,2048]{1,0:T(8,128)(2,1)}, u32[]{:S(2)}, u32[]{:S(2)}) %collective-permute-start.13) | collective-permute-done | bytes 1048608 | tf_op jit(solution)/shard_map/ppermute | solution.py:55
  88.5 1.6 collective-permute-start.14
  92.4 34.5 %collective-permute-done.15.refs_6_.refs_5_ = bf16[256,2048]{1,0:T(8,128)(2,1)} collective-permute-done((bf16[256,2048]{1,0:T(8,128)(2,1)}, bf16[256,2048]{1,0:T(8,128)(2,1)}, u32[]{:S(2)}, u32[]{:S(2)}) %collective-permute-start.15) | collective-permute-done | bytes 1048608 | tf_op jit(solution)/shard_map/ppermute | solution.py:55
  126.9 1.6 collective-permute-start.16
  129.8 2.8 copy-done.2
  132.6 6.5 %project.3 = (bf16[128,1536]{1,0:T(8,128)(2,1)S(1)}, bf16[128,1536]{1,0:T(8,128)(2,1)S(1)}, bf16[128,1536]{1,0:T(8,128)(2,1)S(1)}, bf16[128,1536]{1,0:T(8,128)(2,1)S(1)}) custom-call(s32[3]{0:T(128)S(1)} %pad_add_fusion.refs_0_, bf16[256,2048]{1,0:T(8,128)(2,1)} %collective-permute-done.14.refs_2_.refs_1_, ...), custom_call_target="tpu_custom_call" | custom-call | flops 3221225472 | bytes 12582912 | tf_op jit(solution)/shard_map/project/pallas_call | solution.py:117
  139.2 2.5 collective-permute-start.23
  143.6 8.6 %collective-permute-done.23 = bf16[128,1536]{1,0:T(8,128)(2,1)S(1)} collective-permute-done((bf16[128,1536]{1,0:T(8,128)(2,1)S(1)}, bf16[128,1536]{1,0:T(8,128)(2,1)S(1)}, u32[]{:S(2)}, u32[]{:S(2)}) %collective-permute-start.23) | collective-permute-done | bytes 393248 | tf_op jit(solution)/shard_map/ppermute | solution.py:33
  152.2 6.0 %collective-permute-done.22 = bf16[128,1536]{1,0:T(8,128)(2,1)S(1)} collective-permute-done((bf16[128,1536]{1,0:T(8,128)(2,1)S(1)}, bf16[128,1536]{1,0:T(8,128)(2,1)S(1)}, u32[]{:S(2)}, u32[]{:S(2)}) %collective-permute-start.22) | collective-permute-done | bytes 393248 | tf_op jit(solution)/shard_map/ppermute | solution.py:33
  158.6 5.2 %collective-permute-start.24 = (bf16[128,1536]{1,0:T(8,128)(2,1)S(1)}, bf16[128,1536]{1,0:T(8,128)(2,1)S(1)}, u32[]{:S(2)}, u32[]{:S(2)}) collective-permute-start(bf16[128,1536]{1,0:T(8,128)(2,1)S(1)} %add_convert_fusion.refs_4_), channel_id=1, source_target_pairs={{0,8},{8,16},{16,24},{1,9},{9,17},{17,25},{2,10},{10,18},{18,26},{... | collective-permute-start | bytes 1179656 | tf_op jit(solution)/shard_map/ppermute | solution.py:54
  165.2 6.6 %project.2 = (bf16[128,1536]{1,0:T(8,128)(2,1)S(1)}, bf16[128,1536]{1,0:T(8,128)(2,1)}, bf16[128,1536]{1,0:T(8,128)(2,1)}, bf16[128,1536]{1,0:T(8,128)(2,1)}) custom-call(s32[3]{0:T(128)S(1)} %pad_add_fusion.refs_0_, bf16[256,2048]{1,0:T(8,128)(2,1)} %collective-permute-done.16.refs_1_, bf16[256,2048]{1,0:T(8,128)(2,1)} %collective-permute-done.14.refs_2_.refs_1_, ...), custom_call_target="tpu_custom_call" | custom-call | flops 3221225472 | bytes 12582912 | tf_op jit(solution)/shard_map/project/pallas_call | solution.py:117
  172.5 1.7 collective-permute-start.20
  179.7 11.1 %collective-permute-done.27.refs_6_ = bf16[128,1536]{1,0:T(8,128)(2,1)S(1)} collective-permute-done((bf16[128,1536]{1,0:T(8,128)(2,1)}, bf16[128,1536]{1,0:T(8,128)(2,1)S(1)}, u32[]{:S(2)}, u32[]{:S(2)}) %collective-permute-start.27) | collective-permute-done | bytes 393248 | tf_op jit(solution)/shard_map/ppermute | solution.py:55
  194.1 8.1 %collective-permute-done.29.refs_7_ = bf16[128,1536]{1,0:T(8,128)(2,1)S(1)} collective-permute-done((bf16[128,1536]{1,0:T(8,128)(2,1)S(1)}, bf16[128,1536]{1,0:T(8,128)(2,1)S(1)}, u32[]{:S(2)}, u32[]{:S(2)}) %collective-permute-start.29) | collective-permute-done | bytes 393248 | tf_op jit(solution)/shard_map/ppermute | solution.py:55
  202.2 3.9 route.2
  206.9 2.3 collective-permute-start.30
  212.2 1.8 collective-permute-start.38
  214.0 4.9 %collective-permute-done.31.refs_5_ = bf16[128,1536]{1,0:T(8,128)(2,1)} collective-permute-done((bf16[128,1536]{1,0:T(8,128)(2,1)S(1)}, bf16[128,1536]{1,0:T(8,128)(2,1)}, u32[]{:S(2)}, u32[]{:S(2)}) %collective-permute-start.31) | collective-permute-done | bytes 393248 | tf_op jit(solution)/shard_map/ppermute | solution.py:55
  223.8 3.2 collective-permute-done.36.refs_1_
  227.8 7.0 %collective-permute-done.37.refs_2_ = bf16[48,6144]{1,0:T(8,128)(2,1)S(1)} collective-permute-done((bf16[48,6144]{1,0:T(8,128)(2,1)}, bf16[48,6144]{1,0:T(8,128)(2,1)S(1)}, u32[]{:S(2)}, u32[]{:S(2)}) %collective-permute-start.37) | collective-permute-done | bytes 589856 | tf_op jit(solution)/shard_map/ppermute | solution.py:33
  235.7 2.3 collective-permute-done.38.refs_3_
  238.0 1.9 collective-permute-start.42
  239.9 1.6 collective-permute-start.43
  245.7 15.7 %gate_up.3.refs_4_ = bf16[192,1152]{1,0:T(8,128)(2,1)S(1)} custom-call(bf16[48,6144]{1,0:T(8,128)(2,1)S(1)} %get-tuple-element.126.refs_0_, bf16[48,6144]{1,0:T(8,128)(2,1)S(1)} %copy-done.5, bf16[48,6144]{1,0:T(8,128)(2,1)S(1)} %copy-done.7, bf16[48,6144]{1,0:T(8,128)(2,1)} %collective-permute-done.38.refs_3_, bf16[2,576,6144]{2,1,0:T(8,128)(2,1)} %bitcast.202, ...), custom_call_target="tpu_custom_call" | custom-call | flops 5435817984 | bytes 30670848 | tf_op jit(solution)/shard_map/gate_up/pallas_call | solution.py:225
  261.4 5.3 %collective-permute-start.39 = (bf16[192,1152]{1,0:T(8,128)(2,1)S(1)}, bf16[192,1152]{1,0:T(8,128)(2,1)S(1)}, u32[]{:S(2)}, u32[]{:S(2)}) collective-permute-start(bf16[192,1152]{1,0:T(8,128)(2,1)S(1)} %gate_up.3.refs_4_), channel_id=1, source_target_pairs={{0,8},{8,16},{16,24},{1,9},{9,17},{17,25},{2,10},{10,18},{18,26},{... | collective-permute-start | bytes 1327112 | tf_op jit(solution)/shard_map/ppermute | solution.py:54
  268.1 3.7 route.3
  271.9 1.9 collective-permute-start.49
  273.8 1.6 collective-permute-start.50
  275.3 3.7 collective-permute-done.40.refs_5_
  281.0 15.9 %gate_up.4.refs_4_ = bf16[192,1152]{1,0:T(8,128)(2,1)S(1)} custom-call(bf16[48,6144]{1,0:T(8,128)(2,1)S(1)} %get-tuple-element.140.refs_0_, bf16[48,6144]{1,0:T(8,128)(2,1)S(1)} %collective-permute-done.41.refs_1_, bf16[48,6144]{1,0:T(8,128)(2,1)} %collective-permute-done.42.refs_2_, bf16[48,6144]{1,0:T(8,128)(2,1)} %collective-permute-done.43.refs_3_, ...), custom_call_target="tpu_custom_call" | custom-call | flops 5435817984 | bytes 30670848 | tf_op jit(solution)/shard_map/gate_up/pallas_call | solution.py:225
  297.0 4.7 %collective-permute-start.46 = (bf16[192,1152]{1,0:T(8,128)(2,1)S(1)}, bf16[192,1152]{1,0:T(8,128)(2,1)S(1)}, u32[]{:S(2)}, u32[]{:S(2)}) collective-permute-start(bf16[192,1152]{1,0:T(8,128)(2,1)S(1)} %gate_up.4.refs_4_), channel_id=1, source_target_pairs={{0,8},{8,16},{16,24},{1,9},{9,17},{17,25},{2,10},{10,18},{18,26},{... | collective-permute-start | bytes 1327112 | tf_op jit(solution)/shard_map/ppermute | solution.py:54
  303.0 4.5 collective-permute-done.46.refs_3_
  308.2 6.8 %collective-permute-done.47.refs_5_ = bf16[192,1152]{1,0:T(8,128)(2,1)S(1)} collective-permute-done((bf16[192,1152]{1,0:T(8,128)(2,1)S(1)}, bf16[192,1152]{1,0:T(8,128)(2,1)S(1)}, u32[]{:S(2)}, u32[]{:S(2)}) %collective-permute-start.47) | collective-permute-done | bytes 442400 | tf_op jit(solution)/shard_map/ppermute | solution.py:55
  316.3 2.2 collective-permute-done.49.refs_2_
  319.9 1.7 collective-permute-start.52
  321.6 18.6 %gate_up.5.refs_4_ = bf16[384,1152]{1,0:T(8,128)(2,1)S(1)} custom-call(bf16[96,6144]{1,0:T(8,128)(2,1)S(1)} %get-tuple-element.150.refs_0_, bf16[96,6144]{1,0:T(8,128)(2,1)S(1)} %collective-permute-done.48.refs_1_, bf16[96,6144]{1,0:T(8,128)(2,1)S(1)} %collective-permute-done.49.refs_2_, bf16[96,6144]{1,0:T(8,128)(2,1)} %collective-permute-done.50.refs_3_, ...), custom_call_target="tpu_custom_call" | custom-call | flops 10871635968 | bytes 33030144 | tf_op jit(solution)/shard_map/gate_up/pallas_call | solution.py:225
  341.8 6.4 %collective-permute-start.55 = (bf16[384,1152]{1,0:T(8,128)(2,1)S(1)}, bf16[384,1152]{1,0:T(8,128)(2,1)S(1)}, u32[]{:S(2)}, u32[]{:S(2)}) collective-permute-start(bf16[384,1152]{1,0:T(8,128)(2,1)S(1)} %gate_up.5.refs_4_), channel_id=1, source_target_pairs={{0,8},{8,16},{16,24},{1,9},{9,17},{17,25},{2,10},{10,18},{18,26},{... | collective-permute-start | bytes 2654216 | tf_op jit(solution)/shard_map/ppermute | solution.py:54
  353.7 1.6 copy.53
  362.2 7.2 %down.3 = (bf16[48,1536]{1,0:T(8,128)(2,1)S(1)}, bf16[48,1536]{1,0:T(8,128)(2,1)S(1)}, bf16[48,1536]{1,0:T(8,128)(2,1)S(1)}, bf16[48,1536]{1,0:T(8,128)(2,1)S(1)}) custom-call(s32[3]{0:T(128)S(1)} %pad_add_fusion.refs_0_, bf16[192,1152]{1,0:T(8,128)(2,1)S(1)} %copy-done.21, bf16[192,1152]{1,0:T(8,128)(2,1)S(1)} %copy-done.17, ...), custom_call_target="tpu_custom_call" | custom-call | flops 2717908992 | bytes 20971520 | tf_op jit(solution)/shard_map/down/pallas_call | solution.py:282
  369.4 4.4 collective-permute-done.58.refs_7_
  375.9 2.1 collective-permute-start.68
  379.5 7.3 %down.4 = (bf16[48,1536]{1,0:T(8,128)(2,1)S(1)}, bf16[48,1536]{1,0:T(8,128)(2,1)S(1)}, bf16[48,1536]{1,0:T(8,128)(2,1)S(1)}, bf16[48,1536]{1,0:T(8,128)(2,1)S(1)}) custom-call(s32[3]{0:T(128)S(1)} %pad_add_fusion.refs_0_, bf16[192,1152]{1,0:T(8,128)(2,1)} %collective-permute-done.57.refs_1_, bf16[192,1152]{1,0:T(8,128)(2,1)} %collective-permute-done.51.refs_2_, ...), custom_call_target="tpu_custom_call" | custom-call | flops 2717908992 | bytes 20971520 | tf_op jit(solution)/shard_map/down/pallas_call | solution.py:282
  386.8 9.6 %collective-permute-done.60.refs_6_ = bf16[384,1152]{1,0:T(8,128)(2,1)S(1)} collective-permute-done((bf16[384,1152]{1,0:T(8,128)(2,1)}, bf16[384,1152]{1,0:T(8,128)(2,1)S(1)}, u32[]{:S(2)}, u32[]{:S(2)}) %collective-permute-start.60) | collective-permute-done | bytes 884768 | tf_op jit(solution)/shard_map/ppermute | solution.py:55
  400.3 1.8 collective-permute-start.70
  402.6 9.4 %collective-permute-done.62.refs_7_ = bf16[384,1152]{1,0:T(8,128)(2,1)S(1)} collective-permute-done((bf16[384,1152]{1,0:T(8,128)(2,1)S(1)}, bf16[384,1152]{1,0:T(8,128)(2,1)S(1)}, u32[]{:S(2)}, u32[]{:S(2)}) %collective-permute-start.62) | collective-permute-done | bytes 884768 | tf_op jit(solution)/shard_map/ppermute | solution.py:55
  412.0 9.3 %down.5 = (bf16[96,1536]{1,0:T(8,128)(2,1)S(1)}, bf16[96,1536]{1,0:T(8,128)(2,1)S(1)}, bf16[96,1536]{1,0:T(8,128)(2,1)S(1)}, bf16[96,1536]{1,0:T(8,128)(2,1)S(1)}) custom-call(s32[3]{0:T(128)S(1)} %pad_add_fusion.refs_0_, bf16[384,1152]{1,0:T(8,128)(2,1)S(1)} %collective-permute-done.61.refs_1_, bf16[384,1152]{1,0:T(8,128)(2,1)S(1)} %collective-permute-done.59.refs_2_, ...), custom_call_target="tpu_custom_call" | custom-call | flops 5435817984 | bytes 20971520 | tf_op jit(solution)/shard_map/down/pallas_call | solution.py:282
  422.7 1.8 collective-permute-start.64
  425.5 3.6 collective-permute-done.65
  429.1 3.1 collective-permute-done.64
  435.2 5.0 %collective-permute-done.74 = bf16[64,1536]{1,0:T(8,128)(2,1)S(1)} collective-permute-done((bf16[64,1536]{1,0:T(8,128)(2,1)S(1)}, bf16[64,1536]{1,0:T(8,128)(2,1)S(1)}, u32[]{:S(2)}, u32[]{:S(2)}) %collective-permute-start.74) | collective-permute-done | bytes 196640 | tf_op jit(solution)/shard_map/ppermute | solution.py:28
  440.2 4.0 collective-permute-done.73
  (304 shorter events, 83.0 us)
Async XLA Ops:
  6.5 123.3 %all-gather.10.cloned.1.call-start = ((), (), s32[]{:S(2)}) async-start(), calls=%async_computation.1 | async-start | bytes 9437184 | tf_op jit(solution)/shard_map/all_gather | solution.py:401
  7.3 236.2 %all-gather.12.cloned.1.call-start = ((), (), s32[]{:S(2)}) async-start(), calls=%async_computation.2 | async-start | bytes 21233664 | tf_op jit(solution)/shard_map/all_gather | solution.py:401
  8.0 235.5 %all-gather.14.cloned.1.call-start = ((), (), s32[]{:S(2)}) async-start(), calls=%async_computation.3 | async-start | bytes 21233664 | tf_op jit(solution)/shard_map/all_gather | solution.py:401
  8.8 347.3 %all-gather.8.cloned.1.call-start = ((), (), s32[]{:S(2)}) async-start(), calls=%async_computation | async-start | bytes 21233664 | tf_op jit(solution)/shard_map/all_gather | solution.py:401
  10.1 10.2 %collective-permute-start.5 = (f32[68,4]{0,1:T(4,128)S(1)}, f32[68,4]{0,1:T(4,128)S(1)}, u32[]{:S(2)}, u32[]{:S(2)}) collective-permute-start(f32[68,4]{0,1:T(4,128)S(1)} %pad_maximum_fusion.15), channel_id=1, source_target_pairs={{0,24},{8,0},{16,8},{24,16},{1,25},{9,1},{17,9},{25,17},{2,26},{10... | collective-permute-start | bytes 3272 | tf_op jit(solution)/shard_map/ppermute | solution.py:28
  23.8 14.4 %collective-permute-start.8 = (bf16[8,128,128]{2,1,0:T(8,128)(2,1)S(1)}, bf16[8,128,128]{2,1,0:T(8,128)(2,1)}, u32[]{:S(2)}, u32[]{:S(2)}) collective-permute-start(bf16[8,128,128]{2,1,0:T(8,128)(2,1)S(1)} %add_convert_fusion.3), channel_id=1, source_target_pairs={{0,8},{8,16},{16,24},{1,9},{9,17},{17,25},{2,10},{10,18},{18,26},{... | collective-permute-start | bytes 786440 | tf_op jit(solution)/shard_map/ppermute | solution.py:28
  29.0 11.6 %collective-permute-start.9 = (bf16[8,128,128]{2,1,0:T(8,128)(2,1)S(1)}, bf16[8,128,128]{2,1,0:T(8,128)(2,1)}, u32[]{:S(2)}, u32[]{:S(2)}) collective-permute-start(bf16[8,128,128]{2,1,0:T(8,128)(2,1)S(1)} %add_convert_fusion.3), channel_id=1, source_target_pairs={{0,16},{8,24},{1,17},{9,25},{2,18},{10,26},{3,19},{11,27},{4,20},{... | collective-permute-start | bytes 786440 | tf_op jit(solution)/shard_map/ppermute | solution.py:28
  31.7 13.7 %collective-permute-start.10 = (bf16[8,128,128]{2,1,0:T(8,128)(2,1)S(1)}, bf16[8,128,128]{2,1,0:T(8,128)(2,1)}, u32[]{:S(2)}, u32[]{:S(2)}) collective-permute-start(bf16[8,128,128]{2,1,0:T(8,128)(2,1)S(1)} %add_convert_fusion.3), channel_id=1, source_target_pairs={{0,24},{1,25},{2,26},{3,27},{4,28},{5,29},{6,30},{7,31}} | collective-permute-start | bytes 786440 | tf_op jit(solution)/shard_map/ppermute | solution.py:28
  52.7 31.2 %collective-permute-start.12 = (bf16[256,2048]{1,0:T(8,128)(2,1)S(1)}, bf16[256,2048]{1,0:T(8,128)(2,1)S(1)}, u32[]{:S(2)}, u32[]{:S(2)}) collective-permute-start(bf16[256,2048]{1,0:T(8,128)(2,1)S(1)} %copy.61.refs_4_.refs_3_), channel_id=1, source_target_pairs={{0,8},{8,16},{16,24},{1,9},{9,17},{17,25},{2,10},{10,18},{18,26},{... | collective-permute-start | bytes 3145736 | tf_op jit(solution)/shard_map/ppermute | solution.py:54
  60.5 28.0 %collective-permute-start.13 = (bf16[256,2048]{1,0:T(8,128)(2,1)S(1)}, bf16[256,2048]{1,0:T(8,128)(2,1)}, u32[]{:S(2)}, u32[]{:S(2)}) collective-permute-start(bf16[256,2048]{1,0:T(8,128)(2,1)S(1)} %copy.61.refs_4_.refs_3_), channel_id=1, source_target_pairs={{24,16},{16,8},{8,0},{25,17},{17,9},{9,1},{26,18},{18,10},{10,2},{... | collective-permute-start | bytes 3145736 | tf_op jit(solution)/shard_map/ppermute | solution.py:55
  62.7 76.5 %collective-permute-start.2 = (bf16[64,1536]{1,0:T(8,128)(2,1)}, bf16[64,1536]{1,0:T(8,128)(2,1)S(1)}, u32[]{:S(2)}, u32[]{:S(2)}) collective-permute-start(bf16[64,1536]{1,0:T(8,128)(2,1)} %get-tuple-element.228), channel_id=1, source_target_pairs={{0,24},{8,0},{16,8},{24,16},{1,25},{9,1},{17,9},{25,17},{2,26},{10... | collective-permute-start | bytes 589832 | tf_op jit(solution)/shard_map/ppermute | solution.py:28
  68.9 72.8 %collective-permute-start.1 = (bf16[64,1536]{1,0:T(8,128)(2,1)}, bf16[64,1536]{1,0:T(8,128)(2,1)S(1)}, u32[]{:S(2)}, u32[]{:S(2)}) collective-permute-start(bf16[64,1536]{1,0:T(8,128)(2,1)} %get-tuple-element.229), channel_id=1, source_target_pairs={{0,16},{8,24},{16,0},{24,8},{1,17},{9,25},{17,1},{25,9},{2,18},{10... | collective-permute-start | bytes 589832 | tf_op jit(solution)/shard_map/ppermute | solution.py:28
  68.9 73.3 %collective-permute-start = (bf16[64,1536]{1,0:T(8,128)(2,1)}, bf16[64,1536]{1,0:T(8,128)(2,1)S(1)}, u32[]{:S(2)}, u32[]{:S(2)}) collective-permute-start(bf16[64,1536]{1,0:T(8,128)(2,1)} %get-tuple-element.227), channel_id=1, source_target_pairs={{0,8},{8,16},{16,24},{24,0},{1,9},{9,17},{17,25},{25,1},{2,10},{10... | collective-permute-start | bytes 589832 | tf_op jit(solution)/shard_map/ppermute | solution.py:28
  90.2 36.7 %collective-permute-start.15 = (bf16[256,2048]{1,0:T(8,128)(2,1)}, bf16[256,2048]{1,0:T(8,128)(2,1)}, u32[]{:S(2)}, u32[]{:S(2)}) collective-permute-start(bf16[256,2048]{1,0:T(8,128)(2,1)} %collective-permute-done.13.refs_5_.refs_4_), channel_id=1, source_target_pairs={{16,8},{8,0},{17,9},{9,1},{18,10},{10,2},{19,11},{11,3},{20,12},{1... | collective-permute-start | bytes 3145736 | tf_op jit(solution)/shard_map/ppermute | solution.py:55
  126.9 38.3 %collective-permute-start.16 = (bf16[256,2048]{1,0:T(8,128)(2,1)}, bf16[256,2048]{1,0:T(8,128)(2,1)}, u32[]{:S(2)}, u32[]{:S(2)}) collective-permute-start(bf16[256,2048]{1,0:T(8,128)(2,1)} %collective-permute-done.14.refs_2_.refs_1_), channel_id=1, source_target_pairs={{16,24},{17,25},{18,26},{19,27},{20,28},{21,29},{22,30},{23,31}} | collective-permute-start | bytes 3145736 | tf_op jit(solution)/shard_map/ppermute | solution.py:54
  128.5 36.7 %collective-permute-start.17 = (bf16[256,2048]{1,0:T(8,128)(2,1)}, bf16[256,2048]{1,0:T(8,128)(2,1)}, u32[]{:S(2)}, u32[]{:S(2)}) collective-permute-start(bf16[256,2048]{1,0:T(8,128)(2,1)} %collective-permute-done.15.refs_6_.refs_5_), channel_id=1, source_target_pairs={{8,0},{9,1},{10,2},{11,3},{12,4},{13,5},{14,6},{15,7}} | collective-permute-start | bytes 3145736 | tf_op jit(solution)/shard_map/ppermute | solution.py:55
  139.2 13.1 %collective-permute-start.23 = (bf16[128,1536]{1,0:T(8,128)(2,1)S(1)}, bf16[128,1536]{1,0:T(8,128)(2,1)S(1)}, u32[]{:S(2)}, u32[]{:S(2)}) collective-permute-start(bf16[128,1536]{1,0:T(8,128)(2,1)S(1)} %get-tuple-element.121), channel_id=1, source_target_pairs={{0,3},{1,2},{2,1},{3,0},{4,7},{5,6},{6,5},{7,4},{8,11},{9,10},{10,... | collective-permute-start | bytes 1179656 | tf_op jit(solution)/shard_map/ppermute | solution.py:33
  141.7 16.5 %collective-permute-start.22 = (bf16[128,1536]{1,0:T(8,128)(2,1)S(1)}, bf16[128,1536]{1,0:T(8,128)(2,1)S(1)}, u32[]{:S(2)}, u32[]{:S(2)}) collective-permute-start(bf16[128,1536]{1,0:T(8,128)(2,1)S(1)} %get-tuple-element.120), channel_id=1, source_target_pairs={{0,2},{1,3},{2,0},{3,1},{4,6},{5,7},{6,4},{7,5},{8,10},{9,11},{10,... | collective-permute-start | bytes 1179656 | tf_op jit(solution)/shard_map/ppermute | solution.py:33
  142.2 16.1 %collective-permute-start.21 = (bf16[128,1536]{1,0:T(8,128)(2,1)S(1)}, bf16[128,1536]{1,0:T(8,128)(2,1)S(1)}, u32[]{:S(2)}, u32[]{:S(2)}) collective-permute-start(bf16[128,1536]{1,0:T(8,128)(2,1)S(1)} %get-tuple-element.119), channel_id=1, source_target_pairs={{0,1},{1,0},{2,3},{3,2},{4,5},{5,4},{6,7},{7,6},{8,9},{9,8},{10,11... | collective-permute-start | bytes 1179656 | tf_op jit(solution)/shard_map/ppermute | solution.py:33
  158.6 17.4 %collective-permute-start.24 = (bf16[128,1536]{1,0:T(8,128)(2,1)S(1)}, bf16[128,1536]{1,0:T(8,128)(2,1)S(1)}, u32[]{:S(2)}, u32[]{:S(2)}) collective-permute-start(bf16[128,1536]{1,0:T(8,128)(2,1)S(1)} %add_convert_fusion.refs_4_), channel_id=1, source_target_pairs={{0,8},{8,16},{16,24},{1,9},{9,17},{17,25},{2,10},{10,18},{18,26},{... | collective-permute-start | bytes 1179656 | tf_op jit(solution)/shard_map/ppermute | solution.py:54
  163.7 12.7 %collective-permute-start.25 = (bf16[128,1536]{1,0:T(8,128)(2,1)S(1)}, bf16[128,1536]{1,0:T(8,128)(2,1)}, u32[]{:S(2)}, u32[]{:S(2)}) collective-permute-start(bf16[128,1536]{1,0:T(8,128)(2,1)S(1)} %add_convert_fusion.refs_4_), channel_id=1, source_target_pairs={{24,16},{16,8},{8,0},{25,17},{17,9},{9,1},{26,18},{18,10},{10,2},{... | collective-permute-start | bytes 1179656 | tf_op jit(solution)/shard_map/ppermute | solution.py:55
  172.5 20.2 %collective-permute-start.20 = (bf16[128,1536]{1,0:T(8,128)(2,1)}, bf16[128,1536]{1,0:T(8,128)(2,1)S(1)}, u32[]{:S(2)}, u32[]{:S(2)}) collective-permute-start(bf16[128,1536]{1,0:T(8,128)(2,1)} %get-tuple-element.117), channel_id=1, source_target_pairs={{0,3},{1,2},{2,1},{3,0},{4,7},{5,6},{6,5},{7,4},{8,11},{9,10},{10,... | collective-permute-start | bytes 1179656 | tf_op jit(solution)/shard_map/ppermute | solution.py:33
  174.2 18.6 %collective-permute-start.19 = (bf16[128,1536]{1,0:T(8,128)(2,1)}, bf16[128,1536]{1,0:T(8,128)(2,1)S(1)}, u32[]{:S(2)}, u32[]{:S(2)}) collective-permute-start(bf16[128,1536]{1,0:T(8,128)(2,1)} %get-tuple-element.116), channel_id=1, source_target_pairs={{0,2},{1,3},{2,0},{3,1},{4,6},{5,7},{6,4},{7,5},{8,10},{9,11},{10,... | collective-permute-start | bytes 1179656 | tf_op jit(solution)/shard_map/ppermute | solution.py:33
  175.5 17.3 %collective-permute-start.18 = (bf16[128,1536]{1,0:T(8,128)(2,1)}, bf16[128,1536]{1,0:T(8,128)(2,1)S(1)}, u32[]{:S(2)}, u32[]{:S(2)}) collective-permute-start(bf16[128,1536]{1,0:T(8,128)(2,1)} %get-tuple-element.115), channel_id=1, source_target_pairs={{0,1},{1,0},{2,3},{3,2},{4,5},{5,4},{6,7},{7,6},{8,9},{9,8},{10,11... | collective-permute-start | bytes 1179656 | tf_op jit(solution)/shard_map/ppermute | solution.py:33
  177.1 13.6 %collective-permute-start.27 = (bf16[128,1536]{1,0:T(8,128)(2,1)}, bf16[128,1536]{1,0:T(8,128)(2,1)S(1)}, u32[]{:S(2)}, u32[]{:S(2)}) collective-permute-start(bf16[128,1536]{1,0:T(8,128)(2,1)} %collective-permute-done.25.refs_5_), channel_id=1, source_target_pairs={{16,8},{8,0},{17,9},{9,1},{18,10},{10,2},{19,11},{11,3},{20,12},{1... | collective-permute-start | bytes 1179656 | tf_op jit(solution)/shard_map/ppermute | solution.py:55
  191.4 10.8 %collective-permute-start.29 = (bf16[128,1536]{1,0:T(8,128)(2,1)S(1)}, bf16[128,1536]{1,0:T(8,128)(2,1)S(1)}, u32[]{:S(2)}, u32[]{:S(2)}) collective-permute-start(bf16[128,1536]{1,0:T(8,128)(2,1)S(1)} %collective-permute-done.27.refs_6_), channel_id=1, source_target_pairs={{8,0},{9,1},{10,2},{11,3},{12,4},{13,5},{14,6},{15,7}} | collective-permute-start | bytes 1179656 | tf_op jit(solution)/shard_map/ppermute | solution.py:55
  210.5 16.5 %collective-permute-start.36 = (bf16[48,6144]{1,0:T(8,128)(2,1)}, bf16[48,6144]{1,0:T(8,128)(2,1)S(1)}, u32[]{:S(2)}, u32[]{:S(2)}) collective-permute-start(bf16[48,6144]{1,0:T(8,128)(2,1)} %get-tuple-element.127), channel_id=1, source_target_pairs={{0,1},{1,0},{2,3},{3,2},{4,5},{5,4},{6,7},{7,6},{8,9},{9,8},{10,11... | collective-permute-start | bytes 1769480 | tf_op jit(solution)/shard_map/ppermute | solution.py:33
  212.0 22.8 %collective-permute-start.37 = (bf16[48,6144]{1,0:T(8,128)(2,1)}, bf16[48,6144]{1,0:T(8,128)(2,1)S(1)}, u32[]{:S(2)}, u32[]{:S(2)}) collective-permute-start(bf16[48,6144]{1,0:T(8,128)(2,1)} %get-tuple-element.128), channel_id=1, source_target_pairs={{0,2},{1,3},{2,0},{3,1},{4,6},{5,7},{6,4},{7,5},{8,10},{9,11},{10,... | collective-permute-start | bytes 1769480 | tf_op jit(solution)/shard_map/ppermute | solution.py:33
  212.2 25.8 %collective-permute-start.38 = (bf16[48,6144]{1,0:T(8,128)(2,1)}, bf16[48,6144]{1,0:T(8,128)(2,1)}, u32[]{:S(2)}, u32[]{:S(2)}) collective-permute-start(bf16[48,6144]{1,0:T(8,128)(2,1)} %get-tuple-element.129), channel_id=1, source_target_pairs={{0,3},{1,2},{2,1},{3,0},{4,7},{5,6},{6,5},{7,4},{8,11},{9,10},{10,... | collective-permute-start | bytes 1769480 | tf_op jit(solution)/shard_map/ppermute | solution.py:33
  219.0 22.5 %collective-permute-start.32 = (bf16[128,1536]{1,0:T(8,128)(2,1)}, bf16[128,1536]{1,0:T(8,128)(2,1)}, u32[]{:S(2)}, u32[]{:S(2)}) collective-permute-start(bf16[128,1536]{1,0:T(8,128)(2,1)} %collective-permute-done.30.refs_3_), channel_id=1, source_target_pairs={{8,16},{16,24},{9,17},{17,25},{10,18},{18,26},{11,19},{19,27},{12,... | collective-permute-start | bytes 1179656 | tf_op jit(solution)/shard_map/ppermute | solution.py:54
  220.4 21.1 %collective-permute-start.33 = (bf16[128,1536]{1,0:T(8,128)(2,1)}, bf16[128,1536]{1,0:T(8,128)(2,1)}, u32[]{:S(2)}, u32[]{:S(2)}) collective-permute-start(bf16[128,1536]{1,0:T(8,128)(2,1)} %collective-permute-done.31.refs_5_), channel_id=1, source_target_pairs={{16,8},{8,0},{17,9},{9,1},{18,10},{10,2},{19,11},{11,3},{20,12},{1... | collective-permute-start | bytes 1179656 | tf_op jit(solution)/shard_map/ppermute | solution.py:55
  238.0 33.7 %collective-permute-start.41 = (bf16[48,6144]{1,0:T(8,128)(2,1)}, bf16[48,6144]{1,0:T(8,128)(2,1)S(1)}, u32[]{:S(2)}, u32[]{:S(2)}) collective-permute-start(bf16[48,6144]{1,0:T(8,128)(2,1)} %copy-done.28), channel_id=1, source_target_pairs={{0,1},{1,0},{2,3},{3,2},{4,5},{5,4},{6,7},{7,6},{8,9},{9,8},{10,11... | collective-permute-start | bytes 1769480 | tf_op jit(solution)/shard_map/ppermute | solution.py:33
  238.0 33.8 %collective-permute-start.42 = (bf16[48,6144]{1,0:T(8,128)(2,1)}, bf16[48,6144]{1,0:T(8,128)(2,1)}, u32[]{:S(2)}, u32[]{:S(2)}) collective-permute-start(bf16[48,6144]{1,0:T(8,128)(2,1)} %copy-done.27), channel_id=1, source_target_pairs={{0,2},{1,3},{2,0},{3,1},{4,6},{5,7},{6,4},{7,5},{8,10},{9,11},{10,... | collective-permute-start | bytes 1769480 | tf_op jit(solution)/shard_map/ppermute | solution.py:33
  239.9 31.9 %collective-permute-start.43 = (bf16[48,6144]{1,0:T(8,128)(2,1)}, bf16[48,6144]{1,0:T(8,128)(2,1)}, u32[]{:S(2)}, u32[]{:S(2)}) collective-permute-start(bf16[48,6144]{1,0:T(8,128)(2,1)} %copy-done.26), channel_id=1, source_target_pairs={{0,3},{1,2},{2,1},{3,0},{4,7},{5,6},{6,5},{7,4},{8,11},{9,10},{10,... | collective-permute-start | bytes 1769480 | tf_op jit(solution)/shard_map/ppermute | solution.py:33
  241.5 19.9 %collective-permute-start.34 = (bf16[128,1536]{1,0:T(8,128)(2,1)}, bf16[128,1536]{1,0:T(8,128)(2,1)S(1)}, u32[]{:S(2)}, u32[]{:S(2)}) collective-permute-start(bf16[128,1536]{1,0:T(8,128)(2,1)} %collective-permute-done.32.refs_2_), channel_id=1, source_target_pairs={{16,24},{17,25},{18,26},{19,27},{20,28},{21,29},{22,30},{23,31}} | collective-permute-start | bytes 1179656 | tf_op jit(solution)/shard_map/ppermute | solution.py:54
  242.2 24.5 %collective-permute-start.35 = (bf16[128,1536]{1,0:T(8,128)(2,1)}, bf16[128,1536]{1,0:T(8,128)(2,1)}, u32[]{:S(2)}, u32[]{:S(2)}) collective-permute-start(bf16[128,1536]{1,0:T(8,128)(2,1)} %collective-permute-done.33.refs_6_), channel_id=1, source_target_pairs={{8,0},{9,1},{10,2},{11,3},{12,4},{13,5},{14,6},{15,7}} | collective-permute-start | bytes 1179656 | tf_op jit(solution)/shard_map/ppermute | solution.py:55
  261.4 13.9 %collective-permute-start.39 = (bf16[192,1152]{1,0:T(8,128)(2,1)S(1)}, bf16[192,1152]{1,0:T(8,128)(2,1)S(1)}, u32[]{:S(2)}, u32[]{:S(2)}) collective-permute-start(bf16[192,1152]{1,0:T(8,128)(2,1)S(1)} %gate_up.3.refs_4_), channel_id=1, source_target_pairs={{0,8},{8,16},{16,24},{1,9},{9,17},{17,25},{2,10},{10,18},{18,26},{... | collective-permute-start | bytes 1327112 | tf_op jit(solution)/shard_map/ppermute | solution.py:54
  266.7 12.3 %collective-permute-start.40 = (bf16[192,1152]{1,0:T(8,128)(2,1)S(1)}, bf16[192,1152]{1,0:T(8,128)(2,1)S(1)}, u32[]{:S(2)}, u32[]{:S(2)}) collective-permute-start(bf16[192,1152]{1,0:T(8,128)(2,1)S(1)} %gate_up.3.refs_4_), channel_id=1, source_target_pairs={{24,16},{16,8},{8,0},{25,17},{17,9},{9,1},{26,18},{18,10},{10,2},{... | collective-permute-start | bytes 1327112 | tf_op jit(solution)/shard_map/ppermute | solution.py:55
  271.8 44.5 %collective-permute-start.48 = (bf16[96,6144]{1,0:T(8,128)(2,1)S(1)}, bf16[96,6144]{1,0:T(8,128)(2,1)S(1)}, u32[]{:S(2)}, u32[]{:S(2)}) collective-permute-start(bf16[96,6144]{1,0:T(8,128)(2,1)S(1)} %get-tuple-element.152), channel_id=1, source_target_pairs={{0,1},{1,0},{2,3},{3,2},{4,5},{5,4},{6,7},{7,6},{8,9},{9,8},{10,11... | collective-permute-start | bytes 3538952 | tf_op jit(solution)/shard_map/ppermute | solution.py:33
  271.9 46.6 %collective-permute-start.49 = (bf16[96,6144]{1,0:T(8,128)(2,1)S(1)}, bf16[96,6144]{1,0:T(8,128)(2,1)S(1)}, u32[]{:S(2)}, u32[]{:S(2)}) collective-permute-start(bf16[96,6144]{1,0:T(8,128)(2,1)S(1)} %get-tuple-element.155), channel_id=1, source_target_pairs={{0,2},{1,3},{2,0},{3,1},{4,6},{5,7},{6,4},{7,5},{8,10},{9,11},{10,... | collective-permute-start | bytes 3538952 | tf_op jit(solution)/shard_map/ppermute | solution.py:33
  273.8 44.7 %collective-permute-start.50 = (bf16[96,6144]{1,0:T(8,128)(2,1)S(1)}, bf16[96,6144]{1,0:T(8,128)(2,1)}, u32[]{:S(2)}, u32[]{:S(2)}) collective-permute-start(bf16[96,6144]{1,0:T(8,128)(2,1)S(1)} %get-tuple-element.158), channel_id=1, source_target_pairs={{0,3},{1,2},{2,1},{3,0},{4,7},{5,6},{6,5},{7,4},{8,11},{9,10},{10,... | collective-permute-start | bytes 3538952 | tf_op jit(solution)/shard_map/ppermute | solution.py:33
  279.0 17.9 %collective-permute-start.44 = (bf16[192,1152]{1,0:T(8,128)(2,1)S(1)}, bf16[192,1152]{1,0:T(8,128)(2,1)S(1)}, u32[]{:S(2)}, u32[]{:S(2)}) collective-permute-start(bf16[192,1152]{1,0:T(8,128)(2,1)S(1)} %collective-permute-done.39.refs_3_), channel_id=1, source_target_pairs={{8,16},{16,24},{9,17},{17,25},{10,18},{18,26},{11,19},{19,27},{12,... | collective-permute-start | bytes 1327112 | tf_op jit(solution)/shard_map/ppermute | solution.py:54
  279.7 17.3 %collective-permute-start.45 = (bf16[192,1152]{1,0:T(8,128)(2,1)S(1)}, bf16[192,1152]{1,0:T(8,128)(2,1)S(1)}, u32[]{:S(2)}, u32[]{:S(2)}) collective-permute-start(bf16[192,1152]{1,0:T(8,128)(2,1)S(1)} %collective-permute-done.40.refs_5_), channel_id=1, source_target_pairs={{16,8},{8,0},{17,9},{9,1},{18,10},{10,2},{19,11},{11,3},{20,12},{1... | collective-permute-start | bytes 1327112 | tf_op jit(solution)/shard_map/ppermute | solution.py:55
  297.0 10.5 %collective-permute-start.46 = (bf16[192,1152]{1,0:T(8,128)(2,1)S(1)}, bf16[192,1152]{1,0:T(8,128)(2,1)S(1)}, u32[]{:S(2)}, u32[]{:S(2)}) collective-permute-start(bf16[192,1152]{1,0:T(8,128)(2,1)S(1)} %gate_up.4.refs_4_), channel_id=1, source_target_pairs={{0,8},{8,16},{16,24},{1,9},{9,17},{17,25},{2,10},{10,18},{18,26},{... | collective-permute-start | bytes 1327112 | tf_op jit(solution)/shard_map/ppermute | solution.py:54
  301.7 13.2 %collective-permute-start.47 = (bf16[192,1152]{1,0:T(8,128)(2,1)S(1)}, bf16[192,1152]{1,0:T(8,128)(2,1)S(1)}, u32[]{:S(2)}, u32[]{:S(2)}) collective-permute-start(bf16[192,1152]{1,0:T(8,128)(2,1)S(1)} %gate_up.4.refs_4_), channel_id=1, source_target_pairs={{24,16},{16,8},{8,0},{25,17},{17,9},{9,1},{26,18},{18,10},{10,2},{... | collective-permute-start | bytes 1327112 | tf_op jit(solution)/shard_map/ppermute | solution.py:55
  307.5 32.8 %collective-permute-start.53 = (bf16[192,1152]{1,0:T(8,128)(2,1)S(1)}, bf16[192,1152]{1,0:T(8,128)(2,1)S(1)}, u32[]{:S(2)}, u32[]{:S(2)}) collective-permute-start(bf16[192,1152]{1,0:T(8,128)(2,1)S(1)} %collective-permute-done.44.refs_2_), channel_id=1, source_target_pairs={{16,24},{17,25},{18,26},{19,27},{20,28},{21,29},{22,30},{23,31}} | collective-permute-start | bytes 1327112 | tf_op jit(solution)/shard_map/ppermute | solution.py:54
  314.9 26.1 %collective-permute-start.54 = (bf16[192,1152]{1,0:T(8,128)(2,1)S(1)}, bf16[192,1152]{1,0:T(8,128)(2,1)S(1)}, u32[]{:S(2)}, u32[]{:S(2)}) collective-permute-start(bf16[192,1152]{1,0:T(8,128)(2,1)S(1)} %collective-permute-done.45.refs_6_), channel_id=1, source_target_pairs={{8,0},{9,1},{10,2},{11,3},{12,4},{13,5},{14,6},{15,7}} | collective-permute-start | bytes 1327112 | tf_op jit(solution)/shard_map/ppermute | solution.py:55
  318.5 21.7 %collective-permute-start.51 = (bf16[192,1152]{1,0:T(8,128)(2,1)S(1)}, bf16[192,1152]{1,0:T(8,128)(2,1)}, u32[]{:S(2)}, u32[]{:S(2)}) collective-permute-start(bf16[192,1152]{1,0:T(8,128)(2,1)S(1)} %collective-permute-done.46.refs_3_), channel_id=1, source_target_pairs={{8,16},{16,24},{9,17},{17,25},{10,18},{18,26},{11,19},{19,27},{12,... | collective-permute-start | bytes 1327112 | tf_op jit(solution)/shard_map/ppermute | solution.py:54
  319.9 20.3 %collective-permute-start.52 = (bf16[192,1152]{1,0:T(8,128)(2,1)S(1)}, bf16[192,1152]{1,0:T(8,128)(2,1)}, u32[]{:S(2)}, u32[]{:S(2)}) collective-permute-start(bf16[192,1152]{1,0:T(8,128)(2,1)S(1)} %collective-permute-done.47.refs_5_), channel_id=1, source_target_pairs={{16,8},{8,0},{17,9},{9,1},{18,10},{10,2},{19,11},{11,3},{20,12},{1... | collective-permute-start | bytes 1327112 | tf_op jit(solution)/shard_map/ppermute | solution.py:55
  341.8 27.6 %collective-permute-start.55 = (bf16[384,1152]{1,0:T(8,128)(2,1)S(1)}, bf16[384,1152]{1,0:T(8,128)(2,1)S(1)}, u32[]{:S(2)}, u32[]{:S(2)}) collective-permute-start(bf16[384,1152]{1,0:T(8,128)(2,1)S(1)} %gate_up.5.refs_4_), channel_id=1, source_target_pairs={{0,8},{8,16},{16,24},{1,9},{9,17},{17,25},{2,10},{10,18},{18,26},{... | collective-permute-start | bytes 2654216 | tf_op jit(solution)/shard_map/ppermute | solution.py:54
  348.2 21.2 %collective-permute-start.56 = (bf16[384,1152]{1,0:T(8,128)(2,1)S(1)}, bf16[384,1152]{1,0:T(8,128)(2,1)}, u32[]{:S(2)}, u32[]{:S(2)}) collective-permute-start(bf16[384,1152]{1,0:T(8,128)(2,1)S(1)} %gate_up.5.refs_4_), channel_id=1, source_target_pairs={{24,16},{16,8},{8,0},{25,17},{17,9},{9,1},{26,18},{18,10},{10,2},{... | collective-permute-start | bytes 2654216 | tf_op jit(solution)/shard_map/ppermute | solution.py:55
  350.4 19.0 %collective-permute-start.57 = (bf16[192,1152]{1,0:T(8,128)(2,1)}, bf16[192,1152]{1,0:T(8,128)(2,1)}, u32[]{:S(2)}, u32[]{:S(2)}) collective-permute-start(bf16[192,1152]{1,0:T(8,128)(2,1)} %collective-permute-done.51.refs_2_), channel_id=1, source_target_pairs={{16,24},{17,25},{18,26},{19,27},{20,28},{21,29},{22,30},{23,31}} | collective-permute-start | bytes 1327112 | tf_op jit(solution)/shard_map/ppermute | solution.py:54
  351.8 22.1 %collective-permute-start.58 = (bf16[192,1152]{1,0:T(8,128)(2,1)}, bf16[192,1152]{1,0:T(8,128)(2,1)}, u32[]{:S(2)}, u32[]{:S(2)}) collective-permute-start(bf16[192,1152]{1,0:T(8,128)(2,1)} %collective-permute-done.52.refs_6_), channel_id=1, source_target_pairs={{8,0},{9,1},{10,2},{11,3},{12,4},{13,5},{14,6},{15,7}} | collective-permute-start | bytes 1327112 | tf_op jit(solution)/shard_map/ppermute | solution.py:55
  373.9 12.9 %collective-permute-start.59 = (bf16[384,1152]{1,0:T(8,128)(2,1)S(1)}, bf16[384,1152]{1,0:T(8,128)(2,1)S(1)}, u32[]{:S(2)}, u32[]{:S(2)}) collective-permute-start(bf16[384,1152]{1,0:T(8,128)(2,1)S(1)} %collective-permute-done.55.refs_3_), channel_id=1, source_target_pairs={{8,16},{16,24},{9,17},{17,25},{10,18},{18,26},{11,19},{19,27},{12,... | collective-permute-start | bytes 2654216 | tf_op jit(solution)/shard_map/ppermute | solution.py:54
  374.6 21.8 %collective-permute-start.60 = (bf16[384,1152]{1,0:T(8,128)(2,1)}, bf16[384,1152]{1,0:T(8,128)(2,1)S(1)}, u32[]{:S(2)}, u32[]{:S(2)}) collective-permute-start(bf16[384,1152]{1,0:T(8,128)(2,1)} %collective-permute-done.56.refs_5_), channel_id=1, source_target_pairs={{16,8},{8,0},{17,9},{9,1},{18,10},{10,2},{19,11},{11,3},{20,12},{1... | collective-permute-start | bytes 2654216 | tf_op jit(solution)/shard_map/ppermute | solution.py:55
  375.9 22.5 %collective-permute-start.68 = (bf16[48,1536]{1,0:T(8,128)(2,1)S(1)}, bf16[48,1536]{1,0:T(8,128)(2,1)S(1)}, u32[]{:S(2)}, u32[]{:S(2)}) collective-permute-start(bf16[48,1536]{1,0:T(8,128)(2,1)S(1)} %get-tuple-element.204), channel_id=1, source_target_pairs={{0,3},{1,2},{2,1},{3,0},{4,7},{5,6},{6,5},{7,4},{8,11},{9,10},{10,... | collective-permute-start | bytes 442376 | tf_op jit(solution)/shard_map/ppermute | solution.py:33
  378.0 20.4 %collective-permute-start.67 = (bf16[48,1536]{1,0:T(8,128)(2,1)S(1)}, bf16[48,1536]{1,0:T(8,128)(2,1)S(1)}, u32[]{:S(2)}, u32[]{:S(2)}) collective-permute-start(bf16[48,1536]{1,0:T(8,128)(2,1)S(1)} %get-tuple-element.203), channel_id=1, source_target_pairs={{0,2},{1,3},{2,0},{3,1},{4,6},{5,7},{6,4},{7,5},{8,10},{9,11},{10,... | collective-permute-start | bytes 442376 | tf_op jit(solution)/shard_map/ppermute | solution.py:33
  378.7 19.7 %collective-permute-start.66 = (bf16[48,1536]{1,0:T(8,128)(2,1)S(1)}, bf16[48,1536]{1,0:T(8,128)(2,1)S(1)}, u32[]{:S(2)}, u32[]{:S(2)}) collective-permute-start(bf16[48,1536]{1,0:T(8,128)(2,1)S(1)} %get-tuple-element.202), channel_id=1, source_target_pairs={{0,1},{1,0},{2,3},{3,2},{4,5},{5,4},{6,7},{7,6},{8,9},{9,8},{10,11... | collective-permute-start | bytes 442376 | tf_op jit(solution)/shard_map/ppermute | solution.py:33
  397.1 14.9 %collective-permute-start.62 = (bf16[384,1152]{1,0:T(8,128)(2,1)S(1)}, bf16[384,1152]{1,0:T(8,128)(2,1)S(1)}, u32[]{:S(2)}, u32[]{:S(2)}) collective-permute-start(bf16[384,1152]{1,0:T(8,128)(2,1)S(1)} %collective-permute-done.60.refs_6_), channel_id=1, source_target_pairs={{8,0},{9,1},{10,2},{11,3},{12,4},{13,5},{14,6},{15,7}} | collective-permute-start | bytes 2654216 | tf_op jit(solution)/shard_map/ppermute | solution.py:55
  399.0 25.5 %collective-permute-start.71 = (bf16[48,1536]{1,0:T(8,128)(2,1)S(1)}, bf16[48,1536]{1,0:T(8,128)(2,1)S(1)}, u32[]{:S(2)}, u32[]{:S(2)}) collective-permute-start(bf16[48,1536]{1,0:T(8,128)(2,1)S(1)} %get-tuple-element.208), channel_id=1, source_target_pairs={{0,3},{1,2},{2,1},{3,0},{4,7},{5,6},{6,5},{7,4},{8,11},{9,10},{10,... | collective-permute-start | bytes 442376 | tf_op jit(solution)/shard_map/ppermute | solution.py:33
  400.3 24.6 %collective-permute-start.70 = (bf16[48,1536]{1,0:T(8,128)(2,1)S(1)}, bf16[48,1536]{1,0:T(8,128)(2,1)S(1)}, u32[]{:S(2)}, u32[]{:S(2)}) collective-permute-start(bf16[48,1536]{1,0:T(8,128)(2,1)S(1)} %get-tuple-element.207), channel_id=1, source_target_pairs={{0,2},{1,3},{2,0},{3,1},{4,6},{5,7},{6,4},{7,5},{8,10},{9,11},{10,... | collective-permute-start | bytes 442376 | tf_op jit(solution)/shard_map/ppermute | solution.py:33
  402.1 22.8 %collective-permute-start.69 = (bf16[48,1536]{1,0:T(8,128)(2,1)S(1)}, bf16[48,1536]{1,0:T(8,128)(2,1)S(1)}, u32[]{:S(2)}, u32[]{:S(2)}) collective-permute-start(bf16[48,1536]{1,0:T(8,128)(2,1)S(1)} %get-tuple-element.206), channel_id=1, source_target_pairs={{0,1},{1,0},{2,3},{3,2},{4,5},{5,4},{6,7},{7,6},{8,9},{9,8},{10,11... | collective-permute-start | bytes 442376 | tf_op jit(solution)/shard_map/ppermute | solution.py:33
  433.2 11.0 %collective-permute-start.73 = (bf16[64,1536]{1,0:T(8,128)(2,1)S(1)}, bf16[64,1536]{1,0:T(8,128)(2,1)S(1)}, u32[]{:S(2)}, u32[]{:S(2)}) collective-permute-start(bf16[64,1536]{1,0:T(8,128)(2,1)S(1)} %get-tuple-element.220), channel_id=1, source_target_pairs={{0,16},{8,24},{16,0},{24,8},{1,17},{9,25},{17,1},{25,9},{2,18},{10... | collective-permute-start | bytes 589832 | tf_op jit(solution)/shard_map/ppermute | solution.py:28
  434.2 10.0 %collective-permute-start.72 = (bf16[64,1536]{1,0:T(8,128)(2,1)S(1)}, bf16[64,1536]{1,0:T(8,128)(2,1)S(1)}, u32[]{:S(2)}, u32[]{:S(2)}) collective-permute-start(bf16[64,1536]{1,0:T(8,128)(2,1)S(1)} %get-tuple-element.221), channel_id=1, source_target_pairs={{0,8},{8,16},{16,24},{24,0},{1,9},{9,17},{17,25},{25,1},{2,10},{10... | collective-permute-start | bytes 589832 | tf_op jit(solution)/shard_map/ppermute | solution.py:28
  (70 other events, 976.1 us)
Sparse Core Ops, SparseCore 0:
  8.9 19.4 all-gather.9
  30.0 27.9 all-gather.11
  59.5 27.6 all-gather.13
  88.6 27.5 all-gather.7
